TPU v7x, 128 devices: a whole 4x4x4 slice. The times are simulated.
128 devices in a mesh: req: 64 (over x, z, y), head: 2 (over core).
Axes of the slice: x: 4, y: 4, z: 4, core: 2. Of those that a mesh axis runs over, the one named last changes fastest.
Arguments:
- layer_input: bfloat16 [8192, 4096], P('req'), may hold values from -6 to 6
- q_proj: bfloat16 [4096, 4096], P('req', 'head'), may hold values from -0.09375 to 0.09375
- key_proj: bfloat16 [4096, 256], P(None, 'head'), may hold values from -0.09375 to 0.09375
- value_proj: bfloat16 [4096, 256], P(None, 'head'), may hold values from -0.09375 to 0.09375
- query_gain: float32 [128], replicated, may hold values from 0.1 to 1.9
- key_gain: float32 [128], replicated, may hold values from 0.1 to 1.9
- attn_gain: float32 [4096], replicated, may hold values from 0.1 to 1.9
- moe_gain: float32 [4096], replicated, may hold values from 0.1 to 1.9
- router: bfloat16 [4096, 128], replicated, may hold values from -0.09375 to 0.09375
- expert_ids: int32 [8192, 8], P(('req', 'head')), may hold values from 0 to 127, all different within a row; in each aligned block of 64 rows (0 to 63, 64 to 127, ...) at most 5 rows name the same one
- req_lengths: int32 [64, 4], P('req'), may hold values from 1 to 64, 128 in all within a row
- w_gate: bfloat16 [128, 4096, 768], P(('req', 'head')), may hold values from -0.09375 to 0.09375
- w_up: bfloat16 [128, 4096, 768], P(('req', 'head')), may hold values from -0.09375 to 0.09375
- w_down: bfloat16 [128, 768, 4096], P(('req', 'head')), may hold values from -0.21875 to 0.21875
- cotangent: bfloat16 [8192, 4096], P(('req', 'head')), may hold values from -6 to 6
Outputs:
- mixed: bfloat16 [8192, 4096], P(('req', 'head'))
- attribution: float32 [8192, 4096], P('req', 'head')
- token_score: float32 [8192], P('req')
Inputs may be any that keep to these rules, and one draw needn't show every extreme that they name: `expert_ids`: each row names 8 different experts; in each aligned block of 64 rows no expert is named more than 5 times, a bound that some block reaches. `req_lengths`: each row sums to 128, and its largest entry is exactly 64.
All inputs are finite; a program needn't handle non-finite values.
Results may differ from a plain program's by a relative error of at most 0.008.
Values may be sent and summed in bfloat16 or wider, within the bound.
No kernel may reach another device: no remote copies, remote signals or barrier semaphores. Data moves between devices by JAX's collectives and lax.ppermute only.
A program may use at most 192 MiB of HBM per device.

v0:
```python
import math

import jax
import jax.numpy as jnp
from jax import lax
from jax.sharding import PartitionSpec as P

EPS = 1e-06
THETA = 1000000.0
NEG = -1e30


def segments_of(lengths_row, token_count):
    ends = jnp.cumsum(lengths_row)
    starts = ends - lengths_row
    places = jnp.arange(token_count, dtype=jnp.int32)
    segment = jnp.sum((places[:, None] >= ends[None, :]).astype(jnp.int32), axis=1)
    picked = (
        segment[:, None] == jnp.arange(lengths_row.shape[0], dtype=jnp.int32)[None, :]
    ).astype(jnp.int32)
    start_of = jnp.sum(picked * starts[None, :], axis=1)
    return (segment, places - start_of)


def rope_tables(offsets, half_dim):
    freq = THETA ** (-jnp.arange(half_dim, dtype=jnp.float32) / half_dim)
    angle = offsets.astype(jnp.float32)[:, None] * freq[None, :]
    return (jnp.cos(angle), jnp.sin(angle))


def rotate(rows, cosine_table, sine_table):
    half_dim = rows.shape[-1] // 2
    first = rows[..., :half_dim]
    second = rows[..., half_dim:]
    return jnp.concatenate(
        [first * cosine_table - second * sine_table, second * cosine_table + first * sine_table],
        axis=-1,
    )


def unrotate(rows, cosine_table, sine_table):
    half_dim = rows.shape[-1] // 2
    first = rows[..., :half_dim]
    second = rows[..., half_dim:]
    return jnp.concatenate(
        [first * cosine_table + second * sine_table, second * cosine_table - first * sine_table],
        axis=-1,
    )


def rms_scale(values):
    return lax.rsqrt(jnp.mean(values * values, axis=-1, keepdims=True) + EPS)


def norm_backward(values, scale, gain, grad_out):
    weighted = grad_out * gain
    inner = jnp.mean(weighted * values, axis=-1, keepdims=True)
    return scale * weighted - values * scale**3 * inner


def attend_forward(normed, query_w, key_w, value_w, query_gain, key_gain, segment, offsets):
    head_dim = key_w.shape[1]
    token_count = normed.shape[0]
    groups = query_w.shape[1] // head_dim
    cosine_table, sine_table = rope_tables(offsets, head_dim // 2)
    query_raw = jnp.dot(normed, query_w, preferred_element_type=jnp.float32).reshape(
        token_count, groups, head_dim
    )
    query_scale = rms_scale(query_raw)
    query_normed = query_raw * query_scale * query_gain
    queries3 = rotate(query_normed, cosine_table[:, None, :], sine_table[:, None, :]).astype(
        jnp.bfloat16
    )
    key_raw = jnp.dot(normed, key_w, preferred_element_type=jnp.float32)
    key_scale = rms_scale(key_raw)
    key_normed = key_raw * key_scale * key_gain
    key_rows = rotate(key_normed, cosine_table, sine_table).astype(jnp.bfloat16)
    value_rows = jnp.dot(normed, value_w, preferred_element_type=jnp.float32).astype(jnp.bfloat16)
    factor = 1.0 / math.sqrt(head_dim)
    scores = (
        jnp.einsum("qgd,kd->gqk", queries3, key_rows, preferred_element_type=jnp.float32) * factor
    )
    places = jnp.arange(token_count, dtype=jnp.int32)
    allowed = (segment[:, None] == segment[None, :]) & (places[None, :] <= places[:, None])
    scores = jnp.where(allowed[None, :, :], scores, NEG)
    exponent_terms = jnp.exp(scores)
    attn_weights = exponent_terms / jnp.sum(exponent_terms, axis=2, keepdims=True)
    attn_rounded = attn_weights.astype(jnp.bfloat16)
    context = jnp.einsum(
        "gqk,kd->qgd", attn_rounded, value_rows, preferred_element_type=jnp.float32
    )
    context = context.astype(jnp.bfloat16).reshape(token_count, groups * head_dim)
    saved = (
        query_raw,
        query_scale,
        key_raw,
        key_scale,
        key_rows,
        cosine_table,
        sine_table,
        value_rows,
        queries3,
        attn_weights,
        attn_rounded,
    )
    return (context, saved)


def attend_backward(grad_context, saved, query_w, key_w, value_w, query_gain, key_gain):
    (
        query_raw,
        query_scale,
        key_raw,
        key_scale,
        key_rows,
        cosine_table,
        sine_table,
        value_rows,
        queries3,
        attn_weights,
        attn_rounded,
    ) = saved
    token_count, groups, head_dim = queries3.shape
    factor = 1.0 / math.sqrt(head_dim)
    grad_rounded = grad_context.astype(jnp.bfloat16).reshape(token_count, groups, head_dim)
    grad_weights = jnp.einsum(
        "qgd,kd->gqk", grad_rounded, value_rows, preferred_element_type=jnp.float32
    )
    grad_values = jnp.einsum(
        "gqk,qgd->kd", attn_rounded, grad_rounded, preferred_element_type=jnp.float32
    )
    centered = grad_weights - jnp.sum(grad_weights * attn_weights, axis=2, keepdims=True)
    grad_scores = (attn_weights * centered * factor).astype(jnp.bfloat16)
    grad_keys = jnp.einsum("gqk,qgd->kd", grad_scores, queries3, preferred_element_type=jnp.float32)
    grad_key_normed = unrotate(grad_keys, cosine_table, sine_table)
    grad_raw = norm_backward(key_raw, key_scale, key_gain, grad_key_normed)
    grad_queries = jnp.einsum(
        "gqk,kd->qgd", grad_scores, key_rows, preferred_element_type=jnp.float32
    )
    grad_query_normed = unrotate(grad_queries, cosine_table[:, None, :], sine_table[:, None, :])
    grad_query_raw = norm_backward(query_raw, query_scale, query_gain, grad_query_normed)
    grad_query_raw = grad_query_raw.reshape(token_count, groups * head_dim).astype(jnp.bfloat16)
    return (
        jnp.dot(grad_query_raw, query_w.T, preferred_element_type=jnp.float32)
        + jnp.dot(grad_raw.astype(jnp.bfloat16), key_w.T, preferred_element_type=jnp.float32)
        + jnp.dot(grad_values.astype(jnp.bfloat16), value_w.T, preferred_element_type=jnp.float32)
    )


def expert_backward(grad_out, pre_gate, pre_up, gate_w, up_w, down_w):
    grad_hidden = jnp.dot(grad_out, down_w.T, preferred_element_type=jnp.float32)
    sigmoid_gate = jax.nn.sigmoid(pre_gate)
    grad_up = (grad_hidden * pre_gate * sigmoid_gate).astype(jnp.bfloat16)
    grad_gate = (
        grad_hidden * pre_up * sigmoid_gate * (1.0 + pre_gate * (1.0 - sigmoid_gate))
    ).astype(jnp.bfloat16)
    total = jnp.dot(grad_gate, gate_w.T, preferred_element_type=jnp.float32) + jnp.dot(
        grad_up, up_w.T, preferred_element_type=jnp.float32
    )
    return total.astype(jnp.bfloat16)


def shards(
    layer_input,
    q_proj,
    key_proj,
    value_proj,
    query_gain,
    key_gain,
    attn_gain,
    moe_gain,
    router,
    expert_ids,
    req_lengths,
    w_gate,
    w_up,
    w_down,
    cotangent,
):
    head_count = lax.axis_size("head")
    head_index = lax.axis_index("head")
    device_count = lax.axis_size("req") * head_count
    token_count, width = layer_input.shape
    moe_tokens = token_count // head_count
    half_width = width // head_count
    top_count = expert_ids.shape[1]
    capacity = max(2, (5 * moe_tokens * top_count + 4 * device_count - 1) // (4 * device_count))
    query_w = lax.all_gather(q_proj, "req", axis=0, tiled=True)
    segment, offsets = segments_of(req_lengths[0], token_count)
    input32 = layer_input.astype(jnp.float32)
    input_scale = rms_scale(input32)
    normed = (input32 * input_scale * attn_gain[None, :]).astype(jnp.bfloat16)
    context, saved = attend_forward(
        normed, query_w, key_proj, value_proj, query_gain, key_gain, segment, offsets
    )
    context_tok = lax.all_to_all(context, "head", split_axis=0, concat_axis=1, tiled=True)
    own_input = lax.dynamic_slice_in_dim(input32, head_index * moe_tokens, moe_tokens, 0)
    residual = own_input + context_tok.astype(jnp.float32)
    moe_scale = rms_scale(residual)
    moe_in = (residual * moe_scale * moe_gain[None, :]).astype(jnp.bfloat16)
    logits = jnp.dot(moe_in, router, preferred_element_type=jnp.float32)
    chosen = jnp.take_along_axis(logits, expert_ids, axis=1)
    gates = jax.nn.softmax(chosen, axis=1)
    cot32 = cotangent.astype(jnp.float32)
    flat_ids = expert_ids.reshape(-1)
    slot_total = flat_ids.shape[0]
    expert_range = jnp.arange(device_count, dtype=jnp.int32)
    onehot = (flat_ids[:, None] == expert_range[None, :]).astype(jnp.int32)
    earlier = jnp.cumsum(onehot, axis=0) - onehot
    slot_index = jnp.sum(earlier * onehot, axis=1)
    target = flat_ids * capacity + slot_index
    owner = jnp.arange(slot_total, dtype=jnp.int32) // top_count
    flat_gates = gates.reshape(-1)
    send_rows = (
        jnp.zeros((device_count * capacity, width), jnp.bfloat16).at[target].set(moe_in[owner])
    )
    send_rows = send_rows.reshape(device_count, capacity, width)
    grad_out = (flat_gates[:, None] * cot32[owner]).astype(jnp.bfloat16)
    send_grads = jnp.zeros((device_count * capacity, width), jnp.bfloat16).at[target].set(grad_out)
    send_grads = send_grads.reshape(device_count, capacity, width)
    gate_w = w_gate[0]
    up_w = w_up[0]
    down_w = w_down[0]
    inner_width = gate_w.shape[1]
    rows = lax.all_to_all(send_rows, ("req", "head"), split_axis=0, concat_axis=0, tiled=True)
    sources, items, _ = rows.shape
    flat_rows = rows.reshape(sources * items, width)
    pre_gate = jnp.dot(flat_rows, gate_w, preferred_element_type=jnp.float32)
    pre_up = jnp.dot(flat_rows, up_w, preferred_element_type=jnp.float32)
    hidden = (jax.nn.silu(pre_gate) * pre_up).astype(jnp.bfloat16)
    outputs = jnp.dot(hidden, down_w, preferred_element_type=jnp.float32).astype(jnp.bfloat16)
    made, pre_gate, pre_up = (
        outputs.reshape(sources, items, width),
        pre_gate.reshape(sources, items, inner_width),
        pre_up.reshape(sources, items, inner_width),
    )
    returned = lax.all_to_all(made, ("req", "head"), split_axis=0, concat_axis=0, tiled=True)
    grad_arrived = lax.all_to_all(
        send_grads, ("req", "head"), split_axis=0, concat_axis=0, tiled=True
    )
    sources, items, _ = grad_arrived.shape
    result = expert_backward(
        grad_arrived.reshape(sources * items, width),
        pre_gate.reshape(sources * items, inner_width),
        pre_up.reshape(sources * items, inner_width),
        gate_w,
        up_w,
        down_w,
    )
    grad_made = result.reshape(sources, items, width)
    grad_returned = lax.all_to_all(
        grad_made, ("req", "head"), split_axis=0, concat_axis=0, tiled=True
    )
    outputs_tok = returned.reshape(device_count * capacity, width)[target]
    outputs_tok = outputs_tok.reshape(moe_tokens, top_count, width).astype(jnp.float32)
    moe_sum = jnp.sum(gates[:, :, None] * outputs_tok, axis=1)
    mixed = (residual + moe_sum).astype(jnp.bfloat16)
    gate_grad = jnp.sum(cot32[:, None, :] * outputs_tok, axis=2)
    total_gate = jnp.sum(gates * gate_grad, axis=1, keepdims=True)
    grad_logit = gates * (gate_grad - total_gate)
    dense = jnp.sum(
        jnp.where(
            expert_ids[:, :, None] == expert_range[None, None, :], grad_logit[:, :, None], 0.0
        ),
        axis=1,
    )
    grad_rows = grad_returned.reshape(device_count * capacity, width)[target]
    grad_in = jnp.sum(grad_rows.reshape(moe_tokens, top_count, width).astype(jnp.float32), axis=1)
    grad_in = grad_in + jnp.dot(
        dense, router.astype(jnp.float32).T, precision=lax.Precision.HIGHEST
    )
    grad_resid = cot32 + norm_backward(residual, moe_scale, moe_gain, grad_in)
    grad_heads = lax.all_to_all(grad_resid, "head", split_axis=1, concat_axis=0, tiled=True)
    grad_normed = attend_backward(
        grad_heads, saved, query_w, key_proj, value_proj, query_gain, key_gain
    )
    input_half = lax.dynamic_slice_in_dim(input32, head_index * half_width, half_width, 1)
    whole = lax.psum(grad_normed.astype(jnp.bfloat16), "head").astype(jnp.float32)
    grad_full = norm_backward(input32, input_scale, attn_gain, whole)
    grad_attn = lax.dynamic_slice_in_dim(grad_full, head_index * half_width, half_width, 1)
    grad_input = grad_heads + grad_attn
    attribution = grad_input * input_half
    token_score = lax.psum(jnp.sum(attribution, axis=1), "head")
    return (mixed, attribution, token_score)


def solution(mesh):
    return jax.shard_map(
        shards,
        mesh=mesh,
        in_specs=(
            P("req", None),
            P("req", "head"),
            P(None, "head"),
            P(None, "head"),
            P(),
            P(),
            P(),
            P(),
            P(),
            P(("req", "head"), None),
            P("req", None),
            P(("req", "head"), None, None),
            P(("req", "head"), None, None),
            P(("req", "head"), None, None),
            P(("req", "head"), None),
        ),
        out_specs=(P(("req", "head"), None), P("req", "head"), P("req")),
        check_vma=False,
    )
```

profile of v0, /device:TPU:1, one launch (start us, length us, event | category | flops | bytes accessed | tf_op | source)
XLA Modules:
  0.0 737.8 jit_solution(14507602855606986282)
XLA Ops:
  19.2 98.7 %all-gather.2.cloned.1.call-done = bf16[4096,2048]{1,0:T(8,128)(2,1)} async-done(((bf16[64,2048]{1,0:T(8,128)(2,1)}), bf16[4096,2048]{1,0:T(8,128)(2,1)}) %all-gather.2.cloned.1.call-update) | async-done | bytes 16777232 | tf_op jit(solution)/shard_map/all_gather | solution.py:188
  117.9 8.1 %fusion.106 = f32[128,2048]{1,0:T(8,128)S(1)} fusion(bf16[4096,2048]{1,0:T(8,128)(2,1)} %all-gather.2.cloned.1.call-done, bf16[128,4096]{1,0:T(8,128)(2,1)S(1)} %copy-done.3, f32[4096]{0:T(1024)S(1)} %copy-done.31, f32[128]{0:T(128)S(1)} %get-tuple-element.28), kind=kOutput, calls=%fused_computation.203 | convolution fusion | flops 2149580800 | bytes 18891264 | tf_op jit(solution)/shard_map/dot_general | solution.py:66
  135.6 5.8 all_to_all.52
  143.0 21.7 %scatter_custom_fusion = bf16[640,4096]{1,0:T(8,128)(2,1)} fusion(s32[512]{0:T(512)S(1)} %bitcast.174, bf16[64,4096]{1,0:T(8,128)(2,1)S(1)} %multiply_convert_fusion.6, s32[1024]{0:T(1024)S(1)} %pad_clamp_fusion.1, bf16[]{:T(256)} %constant.87.clone.1), kind=kCustom, calls=%fused_computation.32 | custom fusion | bytes 5242882 | tf_op jit(solution)/shard_map/scatter | solution.py:215
  164.7 8.4 %reshape.436 = bf16[128,5,4096]{2,1,0:T(8,128)(2,1)} reshape(bf16[640,4096]{1,0:T(8,128)(2,1)} %scatter_custom_fusion) | data formatting | bytes 10485760 | tf_op jit(solution)/shard_map/reshape | solution.py:217
  173.1 8.7 %all-to-all-start.1 = ((bf16[128,5,4096]{2,1,0:T(8,128)(2,1)}), bf16[128,5,4096]{2,1,0:T(8,128)(2,1)}, u32[]{:S(2)}, u32[]{:S(2)}) async-start(bf16[128,5,4096]{2,1,0:T(8,128)(2,1)} %reshape.436), calls=%async_computation.1 | async-start | bytes 16777216 | tf_op jit(solution)/shard_map/all_to_all | solution.py:225
  192.6 12.1 %scatter_custom_fusion.1 = bf16[640,4096]{1,0:T(8,128)(2,1)} fusion(s32[512]{0:T(512)S(1)} %bitcast.175, f32[512,4096]{1,0:T(8,128)} %gather_fusion.1, f32[512]{0:T(512)S(1)} %div.84, bf16[]{:T(256)} %constant.87.clone.1), kind=kCustom, calls=%fused_computation.31 | custom fusion | flops 4194304 | bytes 13633538 | tf_op jit(solution)/shard_map/scatter | solution.py:219
  204.7 8.4 %reshape.440 = bf16[128,5,4096]{2,1,0:T(8,128)(2,1)} reshape(bf16[640,4096]{1,0:T(8,128)(2,1)} %scatter_custom_fusion.1) | data formatting | bytes 10485760 | tf_op jit(solution)/shard_map/reshape | solution.py:220
  213.1 74.3 %all-to-all-done.1 = bf16[128,5,4096]{2,1,0:T(8,128)(2,1)} async-done(((bf16[128,5,4096]{2,1,0:T(8,128)(2,1)}), bf16[128,5,4096]{2,1,0:T(8,128)(2,1)}, u32[]{:S(2)}, u32[]{:S(2)}) %all-to-all-start.1) | async-done | bytes 5242912 | tf_op jit(solution)/shard_map/all_to_all | solution.py:225
  287.4 8.1 %all-to-all-start.3 = ((bf16[128,5,4096]{2,1,0:T(8,128)(2,1)}), bf16[128,5,4096]{2,1,0:T(8,128)(2,1)}, u32[]{:S(2)}, u32[]{:S(2)}) async-start(bf16[128,5,4096]{2,1,0:T(8,128)(2,1)} %reshape.440), calls=%async_computation.3 | async-start | bytes 16777216 | tf_op jit(solution)/shard_map/all_to_all | solution.py:238
  295.5 8.7 %reshape.437 = bf16[640,4096]{1,0:T(8,128)(2,1)} reshape(bf16[128,5,4096]{2,1,0:T(8,128)(2,1)} %all-to-all-done.1) | data formatting | bytes 10485760 | tf_op jit(solution)/shard_map/reshape | solution.py:227
  304.2 8.1 %fusion.11 = f32[640,768]{1,0:T(8,128)S(1)} fusion(bf16[640,4096]{1,0:T(8,128)(2,1)} %reshape.437, bf16[1,4096,768]{2,1,0:T(8,128)(2,1)} %param.26), kind=kOutput, calls=%fused_computation.24 | convolution fusion | flops 4026531840 | bytes 13500416 | tf_op jit(solution)/shard_map/dot_general | solution.py:228
  312.4 7.1 fusion.7
  320.9 5.9 convolution_convert_fusion
  326.8 8.4 %reshape.438 = bf16[128,5,4096]{2,1,0:T(8,128)(2,1)} reshape(bf16[640,4096]{1,0:T(8,128)(2,1)} %convolution_convert_fusion) | data formatting | bytes 10485760 | tf_op jit(solution)/shard_map/reshape | solution.py:233
  335.2 66.0 %all-to-all-done.3 = bf16[128,5,4096]{2,1,0:T(8,128)(2,1)} async-done(((bf16[128,5,4096]{2,1,0:T(8,128)(2,1)}), bf16[128,5,4096]{2,1,0:T(8,128)(2,1)}, u32[]{:S(2)}, u32[]{:S(2)}) %all-to-all-start.3) | async-done | bytes 5242912 | tf_op jit(solution)/shard_map/all_to_all | solution.py:238
  401.2 7.8 %all-to-all-start.2 = ((bf16[128,5,4096]{2,1,0:T(8,128)(2,1)}), bf16[128,5,4096]{2,1,0:T(8,128)(2,1)}, u32[]{:S(2)}, u32[]{:S(2)}) async-start(bf16[128,5,4096]{2,1,0:T(8,128)(2,1)} %reshape.438), calls=%async_computation.2 | async-start | bytes 16777216 | tf_op jit(solution)/shard_map/all_to_all | solution.py:237
  408.9 8.8 %reshape.441 = bf16[640,4096]{1,0:T(8,128)(2,1)} reshape(bf16[128,5,4096]{2,1,0:T(8,128)(2,1)} %all-to-all-done.3) | data formatting | bytes 10485760 | tf_op jit(solution)/shard_map/reshape | solution.py:243
  417.7 8.2 %fusion.3 = f32[640,768]{1,0:T(8,128)S(1)} fusion(bf16[640,4096]{1,0:T(8,128)(2,1)} %reshape.441, bf16[1,768,4096]{2,1,0:T(8,128)(2,1)} %param.28), kind=kOutput, calls=%fused_computation.16 | convolution fusion | flops 4026531840 | bytes 13500416 | tf_op jit(solution)/shard_map/dot_general | solution.py:151
  427.2 9.9 %fusion.9 = f32[640,4096]{1,0:T(8,128)} fusion(bf16[1,4096,768]{2,1,0:T(8,128)(2,1)} %param.26, f32[640,768]{1,0:T(8,128)S(1)} %copy-done.54, f32[640,768]{1,0:T(8,128)S(1)} %fusion.3, f32[640,768]{1,0:T(8,128)S(1)} %copy-done.56), kind=kOutput, calls=%fused_computation.22 | convolution fusion | flops 4031447040 | bytes 22675456 | tf_op jit(solution)/shard_map/dot_general | solution.py:157
  437.1 13.0 %add_convert_fusion = bf16[640,4096]{1,0:T(8,128)(2,1)} fusion(f32[640,4096]{1,0:T(8,128)} %fusion.9, bf16[1,4096,768]{2,1,0:T(8,128)(2,1)} %param.27, f32[640,768]{1,0:T(8,128)} %copy-done.57, f32[640,768]{1,0:T(8,128)S(1)} %copy-done.54), kind=kOutput, calls=%fused_computation.10 | convolution fusion | flops 4034723840 | bytes 25952256 | tf_op jit(solution)/shard_map/dot_general | solution.py:157
  450.1 8.4 %reshape.442 = bf16[128,5,4096]{2,1,0:T(8,128)(2,1)} reshape(bf16[640,4096]{1,0:T(8,128)(2,1)} %add_convert_fusion) | data formatting | bytes 10485760 | tf_op jit(solution)/shard_map/reshape | solution.py:250
  458.5 56.6 %all-to-all-done.2 = bf16[128,5,4096]{2,1,0:T(8,128)(2,1)} async-done(((bf16[128,5,4096]{2,1,0:T(8,128)(2,1)}), bf16[128,5,4096]{2,1,0:T(8,128)(2,1)}, u32[]{:S(2)}, u32[]{:S(2)}) %all-to-all-start.2) | async-done | bytes 5242912 | tf_op jit(solution)/shard_map/all_to_all | solution.py:237
  515.1 7.6 %all-to-all-start.4 = ((bf16[128,5,4096]{2,1,0:T(8,128)(2,1)}), bf16[128,5,4096]{2,1,0:T(8,128)(2,1)}, u32[]{:S(2)}, u32[]{:S(2)}) async-start(bf16[128,5,4096]{2,1,0:T(8,128)(2,1)} %reshape.442), calls=%async_computation.4 | async-start | bytes 16777216 | tf_op jit(solution)/shard_map/all_to_all | solution.py:251
  525.8 9.2 %reshape.439 = bf16[640,4096]{1,0:T(8,128)(2,1)} reshape(bf16[128,5,4096]{2,1,0:T(8,128)(2,1)} %all-to-all-done.2) | data formatting | bytes 10485760 | tf_op jit(solution)/shard_map/reshape | solution.py:254
  534.9 11.7 %gather_fusion = bf16[512,4096]{1,0:T(8,128)(2,1)} fusion(bf16[640,4096]{1,0:T(8,128)(2,1)} %reshape.439, s32[1024]{0:T(1024)S(1)} %pad_clamp_fusion), kind=kCustom, calls=%fused_computation.1 | custom fusion | bytes 8390656 | tf_op jit(solution)/shard_map/gather | solution.py:254
  546.7 6.5 fusion.2
  553.6 75.3 %all-to-all-done.4 = bf16[128,5,4096]{2,1,0:T(8,128)(2,1)} async-done(((bf16[128,5,4096]{2,1,0:T(8,128)(2,1)}), bf16[128,5,4096]{2,1,0:T(8,128)(2,1)}, u32[]{:S(2)}, u32[]{:S(2)}) %all-to-all-start.4) | async-done | bytes 5242912 | tf_op jit(solution)/shard_map/all_to_all | solution.py:251
  628.9 8.8 %reshape.443 = bf16[640,4096]{1,0:T(8,128)(2,1)} reshape(bf16[128,5,4096]{2,1,0:T(8,128)(2,1)} %all-to-all-done.4) | data formatting | bytes 10485760 | tf_op jit(solution)/shard_map/reshape | solution.py:267
  637.7 11.9 %gather_fusion.2 = bf16[512,4096]{1,0:T(8,128)(2,1)} fusion(bf16[640,4096]{1,0:T(8,128)(2,1)} %reshape.443, s32[1024]{0:T(1024)S(1)} %pad_clamp_fusion), kind=kCustom, calls=%fused_computation.3 | custom fusion | bytes 8390656 | tf_op jit(solution)/shard_map/gather | solution.py:267
  678.5 14.3 %fusion.46 = f32[128,4096]{1,0:T(8,128)} fusion(bf16[4096,2048]{1,0:T(8,128)(2,1)} %all-gather.2.cloned.1.call-done, f32[16,8,16,128]{3,2,1,0:T(8,128)} %bitcast.160, f32[128,2048]{1,0:T(8,128)S(1)} %copy-done.2, f32[16,8,16,128]{3,2,1,0:T(8,128)} %bitcast.162, f32[16,8,16,128]{3,2,1,0:T(8,128)} %bitcast.161, f32[16,16,8,128]{3,2,1,0:T(8,128)S(1)} %get-tuple-element.9, ...), kind=kOutput, calls=%fused_computation.96 | convolution fusion | flops 2149056512 | bytes 24125440 | tf_op jit(solution)/shard_map/dot_general | solution.py:144
  700.8 23.7 %all-reduce.2.cloned.1.call-done = bf16[128,4096]{1,0:T(8,128)(2,1)} async-done(((bf16[128,4096]{1,0:T(8,128)(2,1)}), bf16[128,4096]{1,0:T(8,128)(2,1)}) %all-reduce.2.cloned.1.call-update) | async-done | bytes 1048592 | tf_op jit(solution)/shard_map/psum | solution.py:278
  (226 shorter events, 82.4 us)
Async XLA Ops:
  7.2 8.7 %copy-start.38 = (f32[128]{0:T(128)S(1)}, f32[128]{0:T(128)}, u32[]{:S(2)}) copy-start(f32[128]{0:T(128)} %param.20) | copy-start | bytes 1540
  7.2 110.7 %all-gather.2.cloned.1.call-start = ((), (), s32[]{:S(2)}) async-start(), calls=%async_computation.6 | async-start | bytes 17039360 | tf_op jit(solution)/shard_map/all_gather | solution.py:188
  14.2 111.9 %copy-start.40 = (f32[128]{0:T(128)}, f32[128]{0:T(128)S(1)}, u32[]{:S(2)}) copy-start(f32[128]{0:T(128)S(1)} %get-tuple-element.28) | copy-start | bytes 1540
  16.3 110.8 %copy-start.23 = (f32[128,64]{1,0:T(8,128)}, f32[128,64]{1,0:T(8,128)S(1)}, u32[]{:S(2)}) copy-start(f32[128,64]{1,0:T(8,128)S(1)} %copy.196) | copy-start | bytes 98308
  16.4 110.7 %copy-start.25 = (f32[128,64]{1,0:T(8,128)}, f32[128,64]{1,0:T(8,128)S(1)}, u32[]{:S(2)}) copy-start(f32[128,64]{1,0:T(8,128)S(1)} %copy.197) | copy-start | bytes 98308
  19.2 109.8 %copy-start.36 = (bf16[128,128,1]{1,0,2:T(8,128)(2,1)}, bf16[128,128,1]{1,0,2:T(8,128)(2,1)S(1)}, u32[]{:S(2)}) copy-start(bf16[128,128,1]{1,0,2:T(8,128)(2,1)S(1)} %fusion.30) | copy-start | bytes 98308
  19.2 107.5 %copy-start.42 = (f32[128]{0:T(128)S(1)}, f32[128]{0:T(128)}, u32[]{:S(2)}) copy-start(f32[128]{0:T(128)} %param.19) | copy-start | bytes 1540
  131.1 10.4 %copy-start.9 = (f32[128,4096]{1,0:T(8,128)S(1)}, f32[128,4096]{1,0:T(8,128)}, u32[]{:S(2)}) copy-start(f32[128,4096]{1,0:T(8,128)} %convert_element_type.116) | copy-start | bytes 6291460
  142.4 30.6 %copy-start.47 = (f32[64]{0:T(128)}, f32[64]{0:T(128)S(1)}, u32[]{:S(2)}) copy-start(f32[64]{0:T(128)S(1)} %get-tuple-element.32) | copy-start | bytes 772
  143.0 30.0 %copy-start.17 = (bf16[64,4096]{1,0:T(8,128)(2,1)}, bf16[64,4096]{1,0:T(8,128)(2,1)S(1)}, u32[]{:S(2)}) copy-start(bf16[64,4096]{1,0:T(8,128)(2,1)S(1)} %multiply_convert_fusion.6) | copy-start | bytes 1572868
  173.1 8.9 %copy-start.14 = (bf16[64,4096]{1,0:T(8,128)(2,1)S(1)}, bf16[64,4096]{1,0:T(8,128)(2,1)}, u32[]{:S(2)}) copy-start(bf16[64,4096]{1,0:T(8,128)(2,1)} %param.29) | copy-start | bytes 1572868
  173.1 114.3 %all-to-all-start.1 = ((bf16[128,5,4096]{2,1,0:T(8,128)(2,1)}), bf16[128,5,4096]{2,1,0:T(8,128)(2,1)}, u32[]{:S(2)}, u32[]{:S(2)}) async-start(bf16[128,5,4096]{2,1,0:T(8,128)(2,1)} %reshape.436), calls=%async_computation.1 | async-start | bytes 16777216 | tf_op jit(solution)/shard_map/all_to_all | solution.py:225
  287.4 113.8 %all-to-all-start.3 = ((bf16[128,5,4096]{2,1,0:T(8,128)(2,1)}), bf16[128,5,4096]{2,1,0:T(8,128)(2,1)}, u32[]{:S(2)}, u32[]{:S(2)}) async-start(bf16[128,5,4096]{2,1,0:T(8,128)(2,1)} %reshape.440), calls=%async_computation.3 | async-start | bytes 16777216 | tf_op jit(solution)/shard_map/all_to_all | solution.py:238
  304.2 16.6 %slice-start = ((s8[6291456]{0:T(1024)(128)(4,1)}), s8[4194304]{0:T(1024)(128)(4,1)S(1)}, s32[]{:S(2)}) async-start(s8[6291456]{0:T(1024)(128)(4,1)} %bitcast.178), calls=%async_computation.8 | async-start | bytes 8388608
  312.4 8.5 %slice-start.1 = ((s8[6291456]{0:T(1024)(128)(4,1)}), s8[2097152]{0:T(1024)(128)(4,1)S(1)}, s32[]{:S(2)}) async-start(s8[6291456]{0:T(1024)(128)(4,1)} %bitcast.178), calls=%async_computation.9 | async-start | bytes 4194304
  401.2 113.9 %all-to-all-start.2 = ((bf16[128,5,4096]{2,1,0:T(8,128)(2,1)}), bf16[128,5,4096]{2,1,0:T(8,128)(2,1)}, u32[]{:S(2)}, u32[]{:S(2)}) async-start(bf16[128,5,4096]{2,1,0:T(8,128)(2,1)} %reshape.438), calls=%async_computation.2 | async-start | bytes 16777216 | tf_op jit(solution)/shard_map/all_to_all | solution.py:237
  417.7 9.5 %copy-start.54 = (f32[640,768]{1,0:T(8,128)S(1)}, f32[640,768]{1,0:T(8,128)}, u32[]{:S(2)}) copy-start(f32[640,768]{1,0:T(8,128)} %copy-done.53) | copy-start | bytes 5898244
  417.7 9.5 %copy-start.56 = (f32[640,768]{1,0:T(8,128)S(1)}, f32[640,768]{1,0:T(8,128)}, u32[]{:S(2)}) copy-start(f32[640,768]{1,0:T(8,128)} %copy-done.55) | copy-start | bytes 5898244
  515.1 113.8 %all-to-all-start.4 = ((bf16[128,5,4096]{2,1,0:T(8,128)(2,1)}), bf16[128,5,4096]{2,1,0:T(8,128)(2,1)}, u32[]{:S(2)}, u32[]{:S(2)}) async-start(bf16[128,5,4096]{2,1,0:T(8,128)(2,1)} %reshape.442), calls=%async_computation.4 | async-start | bytes 16777216 | tf_op jit(solution)/shard_map/all_to_all | solution.py:251
  522.7 201.9 %all-reduce.2.cloned.1.call-start = ((), (), s32[]{:S(2)}) async-start(), calls=%async_computation.7 | async-start | bytes 2097152 | tf_op jit(solution)/shard_map/psum | solution.py:278
  662.8 9.7 %copy-start.28 = (f32[128,128]{0,1:T(8,128)S(1)}, f32[128,128]{0,1:T(8,128)}, u32[]{:S(2)}) copy-start(f32[128,128]{0,1:T(8,128)} %copy-done.27) | copy-start | bytes 196612
  662.8 9.7 %copy-start.39 = (f32[128]{0:T(128)S(1)}, f32[128]{0:T(128)}, u32[]{:S(2)}) copy-start(f32[128]{0:T(128)} %param.20) | copy-start | bytes 1540
  662.8 10.4 %copy-start.24 = (f32[128,64]{1,0:T(8,128)S(1)}, f32[128,64]{1,0:T(8,128)}, u32[]{:S(2)}) copy-start(f32[128,64]{1,0:T(8,128)} %copy-done.23) | copy-start | bytes 98308
  662.8 10.4 %copy-start.26 = (f32[128,64]{1,0:T(8,128)S(1)}, f32[128,64]{1,0:T(8,128)}, u32[]{:S(2)}) copy-start(f32[128,64]{1,0:T(8,128)} %copy-done.25) | copy-start | bytes 98308
  678.5 14.3 %copy-start.44 = (f32[128]{0:T(128)S(1)}, f32[128]{0:T(128)}, u32[]{:S(2)}) copy-start(f32[128]{0:T(128)} %copy-done.43) | copy-start | bytes 1540
  678.5 14.3 %copy-start.50 = (f32[128]{0:T(128)S(1)}, f32[128]{0:T(128)}, u32[]{:S(2)}) copy-start(f32[128]{0:T(128)} %get-tuple-element.29) | copy-start | bytes 1540
  678.5 14.3 %copy-start.52 = (f32[128]{0:T(128)S(1)}, f32[128]{0:T(128)}, u32[]{:S(2)}) copy-start(f32[128]{0:T(128)} %broadcast_multiply_fusion.3) | copy-start | bytes 1540
  696.2 28.4 %copy-start.4 = (bf16[128,4096]{1,0:T(8,128)(2,1)S(1)}, bf16[128,4096]{1,0:T(8,128)(2,1)}, u32[]{:S(2)}) copy-start(bf16[128,4096]{1,0:T(8,128)(2,1)} %param.15) | copy-start | bytes 3145732
  696.2 28.4 %copy-start.32 = (f32[4096]{0:T(1024)S(1)}, f32[4096]{0:T(1024)}, u32[]{:S(2)}) copy-start(f32[4096]{0:T(1024)} %param.21) | copy-start | bytes 49156
  696.2 30.2 %copy-start.8 = (f32[64,2,2048]{2,0,1:T(8,128)S(1)}, f32[64,2,2048]{2,0,1:T(8,128)}, u32[]{:S(2)}) copy-start(f32[64,2,2048]{2,0,1:T(8,128)} %copy-done.7) | copy-start | bytes 3145732
  696.2 30.2 %copy-start.41 = (f32[128]{0:T(128)S(1)}, f32[128]{0:T(128)}, u32[]{:S(2)}) copy-start(f32[128]{0:T(128)} %copy-done.40) | copy-start | bytes 1540
  696.2 30.2 %copy-start.49 = (f32[128]{0:T(128)S(1)}, f32[128]{0:T(128)}, u32[]{:S(2)}) copy-start(f32[128]{0:T(128)} %get-tuple-element.27) | copy-start | bytes 1540
  (34 other events, 159.1 us)
Sparse Core Ops, SparseCore 0:
  10.9 106.9 all-gather.1
  701.0 23.5 all-reduce.1
where the time goes:
time: 746 us; the launch traced here: 738 us
  waiting for transfers between devices  395 us (53%)
  local copies, waits for them, and re-layouts  141 us (19%)
  matrix products  99.8 us (13%)
  other arithmetic  40.1 us (5%)
  starting transfers between devices  32.3 us (4%)
  between operations  15.2 us (2%)
  blocking collectives  14.1 us (2%)
    all_gather x1, waiting for transfers between devices, shards(): query_w = lax.all_gather(q_proj, 'req', axis=0, tiled=True)  98.7 us
    all_to_all x1, waiting for transfers between devices, shards(): lax.all_to_all(grad_made, ('req', 'head'), split_axis=0, concat_axis=0, t...  75.3 us
    all_to_all x1, waiting for transfers between devices, shards(): lax.all_to_all(send_rows, ('req', 'head'), split_axis=0, concat_axis=0, t...  74.3 us
    all_to_all x1, waiting for transfers between devices, shards(): lax.all_to_all(send_grads, ('req', 'head'), split_axis=0, concat_axis=0,...  66 us
    all_to_all x1, waiting for transfers between devices, shards(): lax.all_to_all(made, ('req', 'head'), split_axis=0, concat_axis=0, tiled=...  56.6 us
    psum x1, waiting for transfers between devices, shards(): lax.psum(grad_normed.astype(jnp.bfloat16), 'head').astype(jnp.float32)  23.7 us
    scatter x1, local copies, waits for them, and re-layouts, shards(): jnp.zeros((device_count * capacity, width), jnp.bfloat16).at[target]  21.7 us
  transfers between devices with their start and end apart: 6, of which 6 were waited for; matrix products, arithmetic and copies ran while one was open for 22% of the time, Pallas kernels for 0%

commit v1 on v0

--- a/solution.py
+++ b/solution.py
@@ -3,7 +3,10 @@
 import jax
 import jax.numpy as jnp
 from jax import lax
+from jax.experimental import pallas as pl
+from jax.experimental.pallas import tpu as pltpu
 from jax.sharding import PartitionSpec as P
+
 
 EPS = 1e-06
 THETA = 1000000.0
@@ -147,20 +150,142 @@
     )
 
 
-def expert_backward(grad_out, pre_gate, pre_up, gate_w, up_w, down_w):
-    grad_hidden = jnp.dot(grad_out, down_w.T, preferred_element_type=jnp.float32)
-    sigmoid_gate = jax.nn.sigmoid(pre_gate)
-    grad_up = (grad_hidden * pre_gate * sigmoid_gate).astype(jnp.bfloat16)
-    grad_gate = (
-        grad_hidden * pre_up * sigmoid_gate * (1.0 + pre_gate * (1.0 - sigmoid_gate))
-    ).astype(jnp.bfloat16)
-    total = jnp.dot(grad_gate, gate_w.T, preferred_element_type=jnp.float32) + jnp.dot(
-        grad_up, up_w.T, preferred_element_type=jnp.float32
-    )
-    return total.astype(jnp.bfloat16)
-
-
-def shards(
+SUB = 32
+
+
+def pick_kernel(index_ref, rows_ref, out_ref):
+    step_rows = out_ref.shape[0]
+    base = pl.program_id(0) * step_rows
+
+    def one(i, carry):
+        out_ref[i] = rows_ref[index_ref[base + i]]
+        return carry
+
+    lax.fori_loop(0, step_rows, one, 0, unroll=8)
+
+
+def pick_rows(rows3, index, step_rows=80):
+    count = index.shape[0]
+    _, sub, lanes = rows3.shape
+    return pl.pallas_call(
+        pick_kernel,
+        out_shape=jax.ShapeDtypeStruct((count, sub, lanes), rows3.dtype),
+        grid_spec=pltpu.PrefetchScalarGridSpec(
+            num_scalar_prefetch=1,
+            grid=(count // step_rows,),
+            in_specs=[pl.BlockSpec(rows3.shape, lambda i, ids: (0, 0, 0))],
+            out_specs=pl.BlockSpec((step_rows, sub, lanes), lambda i, ids: (i, 0, 0)),
+        ),
+        cost_estimate=pl.CostEstimate(
+            flops=0, transcendentals=0, bytes_accessed=count * sub * lanes * 2
+        ),
+        name="pick_rows",
+    )(index, rows3)
+
+
+def mix_kernel(index_ref, gate_ref, rows_ref, after_ref, out_ref):
+    del after_ref
+    step_tokens = out_ref.shape[0]
+    top = index_ref.shape[0] // (step_tokens * pl.num_programs(0))
+    base = pl.program_id(0) * step_tokens
+
+    def one(i, carry):
+        at = (base + i) * top
+        total = gate_ref[at] * rows_ref[index_ref[at]].astype(jnp.float32)
+        for k in range(1, top):
+            total = total + gate_ref[at + k] * rows_ref[index_ref[at + k]].astype(jnp.float32)
+        out_ref[i] = total
+        return carry
+
+    lax.fori_loop(0, step_tokens, one, 0, unroll=2)
+
+
+def mix_rows(rows3, index, gates, tokens, after, step_tokens=16):
+    _, sub, lanes = rows3.shape
+    return pl.pallas_call(
+        mix_kernel,
+        out_shape=jax.ShapeDtypeStruct((tokens, sub, lanes), jnp.float32),
+        grid_spec=pltpu.PrefetchScalarGridSpec(
+            num_scalar_prefetch=2,
+            grid=(tokens // step_tokens,),
+            in_specs=[
+                pl.BlockSpec(rows3.shape, lambda i, ids, g: (0, 0, 0)),
+                pl.BlockSpec(after.shape, lambda i, ids, g: (0, 0)),
+            ],
+            out_specs=pl.BlockSpec((step_tokens, sub, lanes), lambda i, ids, g: (i, 0, 0)),
+        ),
+        cost_estimate=pl.CostEstimate(
+            flops=index.shape[0] * sub * lanes * 2,
+            transcendentals=0,
+            bytes_accessed=rows3.shape[0] * sub * lanes * 2,
+        ),
+        name="mix_rows",
+    )(index, gates, rows3, after)
+
+
+def spread_kernel(rows_ref, out_ref, wide):
+    count, sub, lanes = rows_ref.shape
+    wide[...] = rows_ref[...].astype(jnp.float32).reshape(count * sub, lanes)
+    for c in range(sub):
+        out_ref[:, c * lanes : (c + 1) * lanes] = wide[pl.ds(c, count, stride=sub), :].astype(
+            out_ref.dtype
+        )
+
+
+def spread_rows(rows3, step_rows=64):
+    count, sub, lanes = rows3.shape
+    return pl.pallas_call(
+        spread_kernel,
+        out_shape=jax.ShapeDtypeStruct((count, sub * lanes), rows3.dtype),
+        grid=(count // step_rows,),
+        in_specs=[pl.BlockSpec((step_rows, sub, lanes), lambda i: (i, 0, 0))],
+        out_specs=pl.BlockSpec((step_rows, sub * lanes), lambda i: (i, 0)),
+        scratch_shapes=[pltpu.VMEM((step_rows * sub, lanes), jnp.float32)],
+        cost_estimate=pl.CostEstimate(
+            flops=0, transcendentals=0, bytes_accessed=4 * count * sub * lanes
+        ),
+        name="spread_rows",
+    )(rows3)
+
+
+def fold_kernel(rows_ref, out_ref, wide):
+    count, sub, lanes = out_ref.shape
+    for c in range(sub):
+        wide[pl.ds(c, count, stride=sub), :] = rows_ref[:, c * lanes : (c + 1) * lanes].astype(
+            jnp.float32
+        )
+    out_ref[...] = wide[...].reshape(count, sub, lanes).astype(out_ref.dtype)
+
+
+def fold_rows(rows, step_rows=64):
+    count, width = rows.shape
+    lanes = width // SUB
+    return pl.pallas_call(
+        fold_kernel,
+        out_shape=jax.ShapeDtypeStruct((count, SUB, lanes), jnp.bfloat16),
+        grid=(count // step_rows,),
+        in_specs=[pl.BlockSpec((step_rows, width), lambda i: (i, 0))],
+        out_specs=pl.BlockSpec((step_rows, SUB, lanes), lambda i: (i, 0, 0)),
+        scratch_shapes=[pltpu.VMEM((step_rows * SUB, lanes), jnp.float32)],
+        cost_estimate=pl.CostEstimate(
+            flops=0, transcendentals=0, bytes_accessed=4 * count * width
+        ),
+        name="fold_rows",
+    )(rows)
+
+
+def swap_heads(values):
+    return lax.ppermute(values, "head", [(0, 1), (1, 0)])
+
+
+def exchange(rows3, device_count):
+    count, sub, lanes = rows3.shape
+    packed = rows3.reshape(device_count, (count // device_count) * sub, lanes)
+    moved = lax.all_to_all(packed, ("req", "head"), split_axis=0, concat_axis=0, tiled=True)
+    return moved.reshape(count, sub, lanes)
+
+
+def device_step(
     layer_input,
     q_proj,
     key_proj,
@@ -183,9 +308,28 @@
     token_count, width = layer_input.shape
     moe_tokens = token_count // head_count
     half_width = width // head_count
-    top_count = expert_ids.shape[1]
-    capacity = max(2, (5 * moe_tokens * top_count + 4 * device_count - 1) // (4 * device_count))
+    capacity = 5
+    first_core = head_index == 0
+
     query_w = lax.all_gather(q_proj, "req", axis=0, tiled=True)
+
+    expert_range = jnp.arange(device_count, dtype=jnp.int32)
+    chosen_mask = expert_ids[:, :, None] == expert_range[None, None, :]
+    member = jnp.any(chosen_mask, axis=1)
+    token_range = jnp.arange(moe_tokens, dtype=jnp.int32)
+    before = (token_range[:, None] > token_range[None, :]).astype(jnp.bfloat16)
+    rank = jnp.dot(before, member.astype(jnp.bfloat16), preferred_element_type=jnp.float32)
+    rank = rank.astype(jnp.int32)
+    slot_of = jnp.sum(jnp.where(chosen_mask, rank[:, None, :], 0), axis=2)
+    target = (expert_ids * capacity + slot_of).reshape(-1)
+    slot_range = jnp.arange(capacity, dtype=jnp.int32)
+    hit = member[:, :, None] & (rank[:, :, None] == slot_range[None, None, :])
+    source = jnp.sum(jnp.where(hit, token_range[:, None, None], 0), axis=0).reshape(-1)
+
+    cot_send = pick_rows(fold_rows(cotangent), source)
+    cot_send, query_w = lax.optimization_barrier((cot_send, query_w))
+    cot_rows3 = exchange(cot_send, device_count)
+
     segment, offsets = segments_of(req_lengths[0], token_count)
     input32 = layer_input.astype(jnp.float32)
     input_scale = rms_scale(input32)
@@ -193,100 +337,110 @@
     context, saved = attend_forward(
         normed, query_w, key_proj, value_proj, query_gain, key_gain, segment, offsets
     )
-    context_tok = lax.all_to_all(context, "head", split_axis=0, concat_axis=1, tiled=True)
-    own_input = lax.dynamic_slice_in_dim(input32, head_index * moe_tokens, moe_tokens, 0)
-    residual = own_input + context_tok.astype(jnp.float32)
+    other_rows = lax.dynamic_slice_in_dim(context, (1 - head_index) * moe_tokens, moe_tokens, 0)
+    own_rows = lax.dynamic_slice_in_dim(context, head_index * moe_tokens, moe_tokens, 0)
+    came = swap_heads(other_rows)
+    context_tok = jnp.concatenate(
+        [jnp.where(first_core, own_rows, came), jnp.where(first_core, came, own_rows)], axis=1
+    )
+    own_input = lax.dynamic_slice_in_dim(layer_input, head_index * moe_tokens, moe_tokens, 0)
+    residual = own_input.astype(jnp.float32) + context_tok.astype(jnp.float32)
     moe_scale = rms_scale(residual)
     moe_in = (residual * moe_scale * moe_gain[None, :]).astype(jnp.bfloat16)
+    moe_send = pick_rows(fold_rows(moe_in), source)
+    rows3 = exchange(moe_send, device_count)
+
     logits = jnp.dot(moe_in, router, preferred_element_type=jnp.float32)
-    chosen = jnp.take_along_axis(logits, expert_ids, axis=1)
+    chosen = jnp.sum(jnp.where(chosen_mask, logits[:, None, :], 0.0), axis=2)
     gates = jax.nn.softmax(chosen, axis=1)
+    flat_gates = gates.reshape(-1)
     cot32 = cotangent.astype(jnp.float32)
-    flat_ids = expert_ids.reshape(-1)
-    slot_total = flat_ids.shape[0]
-    expert_range = jnp.arange(device_count, dtype=jnp.int32)
-    onehot = (flat_ids[:, None] == expert_range[None, :]).astype(jnp.int32)
-    earlier = jnp.cumsum(onehot, axis=0) - onehot
-    slot_index = jnp.sum(earlier * onehot, axis=1)
-    target = flat_ids * capacity + slot_index
-    owner = jnp.arange(slot_total, dtype=jnp.int32) // top_count
-    flat_gates = gates.reshape(-1)
-    send_rows = (
-        jnp.zeros((device_count * capacity, width), jnp.bfloat16).at[target].set(moe_in[owner])
-    )
-    send_rows = send_rows.reshape(device_count, capacity, width)
-    grad_out = (flat_gates[:, None] * cot32[owner]).astype(jnp.bfloat16)
-    send_grads = jnp.zeros((device_count * capacity, width), jnp.bfloat16).at[target].set(grad_out)
-    send_grads = send_grads.reshape(device_count, capacity, width)
+
     gate_w = w_gate[0]
     up_w = w_up[0]
     down_w = w_down[0]
-    inner_width = gate_w.shape[1]
-    rows = lax.all_to_all(send_rows, ("req", "head"), split_axis=0, concat_axis=0, tiled=True)
-    sources, items, _ = rows.shape
-    flat_rows = rows.reshape(sources * items, width)
-    pre_gate = jnp.dot(flat_rows, gate_w, preferred_element_type=jnp.float32)
-    pre_up = jnp.dot(flat_rows, up_w, preferred_element_type=jnp.float32)
-    hidden = (jax.nn.silu(pre_gate) * pre_up).astype(jnp.bfloat16)
+    cot_rows = spread_rows(cot_rows3)
+    cot_hidden = jnp.dot(cot_rows, down_w.T, preferred_element_type=jnp.float32)
+    cot_hidden = lax.optimization_barrier(cot_hidden)
+    rows = spread_rows(rows3)
+    pre_gate = jnp.dot(rows, gate_w, preferred_element_type=jnp.float32)
+    pre_up = jnp.dot(rows, up_w, preferred_element_type=jnp.float32)
+    sigmoid_gate = jax.nn.sigmoid(pre_gate)
+    silu_gate = pre_gate * sigmoid_gate
+    hidden = (silu_gate * pre_up).astype(jnp.bfloat16)
+    slot_grad = jnp.sum(hidden.astype(jnp.float32) * cot_hidden, axis=1)
+    grad_up = (cot_hidden * silu_gate).astype(jnp.bfloat16)
+    grad_gate = (
+        cot_hidden * pre_up * sigmoid_gate * (1.0 + pre_gate * (1.0 - sigmoid_gate))
+    ).astype(jnp.bfloat16)
+    slot_grad = jnp.pad(slot_grad.reshape(device_count, capacity), ((0, 0), (0, 128 - capacity)))
+    slot_back = lax.all_to_all(
+        slot_grad.reshape(device_count, 1, 128),
+        ("req", "head"),
+        split_axis=0,
+        concat_axis=0,
+        tiled=True,
+    )
+    slot_back = slot_back.reshape(device_count, 128)[:, :capacity]
+    grad_made = jnp.dot(grad_gate, gate_w.T, preferred_element_type=jnp.float32) + jnp.dot(
+        grad_up, up_w.T, preferred_element_type=jnp.float32
+    )
+    grad_send = fold_rows(grad_made.astype(jnp.bfloat16))
+    grad_back = exchange(grad_send, device_count)
     outputs = jnp.dot(hidden, down_w, preferred_element_type=jnp.float32).astype(jnp.bfloat16)
-    made, pre_gate, pre_up = (
-        outputs.reshape(sources, items, width),
-        pre_gate.reshape(sources, items, inner_width),
-        pre_up.reshape(sources, items, inner_width),
-    )
-    returned = lax.all_to_all(made, ("req", "head"), split_axis=0, concat_axis=0, tiled=True)
-    grad_arrived = lax.all_to_all(
-        send_grads, ("req", "head"), split_axis=0, concat_axis=0, tiled=True
-    )
-    sources, items, _ = grad_arrived.shape
-    result = expert_backward(
-        grad_arrived.reshape(sources * items, width),
-        pre_gate.reshape(sources * items, inner_width),
-        pre_up.reshape(sources * items, inner_width),
-        gate_w,
-        up_w,
-        down_w,
-    )
-    grad_made = result.reshape(sources, items, width)
-    grad_returned = lax.all_to_all(
-        grad_made, ("req", "head"), split_axis=0, concat_axis=0, tiled=True
-    )
-    outputs_tok = returned.reshape(device_count * capacity, width)[target]
-    outputs_tok = outputs_tok.reshape(moe_tokens, top_count, width).astype(jnp.float32)
-    moe_sum = jnp.sum(gates[:, :, None] * outputs_tok, axis=1)
-    mixed = (residual + moe_sum).astype(jnp.bfloat16)
-    gate_grad = jnp.sum(cot32[:, None, :] * outputs_tok, axis=2)
+    out_send = fold_rows(outputs)
+    out_back = exchange(out_send, device_count)
+
+    hit_grad = jnp.sum(jnp.where(hit, slot_back[None, :, :], 0.0), axis=2)
+    gate_grad = jnp.sum(jnp.where(chosen_mask, hit_grad[:, None, :], 0.0), axis=2)
     total_gate = jnp.sum(gates * gate_grad, axis=1, keepdims=True)
     grad_logit = gates * (gate_grad - total_gate)
-    dense = jnp.sum(
-        jnp.where(
-            expert_ids[:, :, None] == expert_range[None, None, :], grad_logit[:, :, None], 0.0
-        ),
-        axis=1,
-    )
-    grad_rows = grad_returned.reshape(device_count * capacity, width)[target]
-    grad_in = jnp.sum(grad_rows.reshape(moe_tokens, top_count, width).astype(jnp.float32), axis=1)
-    grad_in = grad_in + jnp.dot(
+    dense = jnp.sum(jnp.where(chosen_mask, grad_logit[:, :, None], 0.0), axis=1)
+    router_part = jnp.dot(
         dense, router.astype(jnp.float32).T, precision=lax.Precision.HIGHEST
     )
+    router_part = lax.optimization_barrier(router_part)
+    grad_in = mix_rows(grad_back, target, flat_gates, moe_tokens, router_part[:8, :128])
+    grad_in = grad_in.reshape(moe_tokens, width)
+    grad_in = grad_in + router_part
     grad_resid = cot32 + norm_backward(residual, moe_scale, moe_gain, grad_in)
-    grad_heads = lax.all_to_all(grad_resid, "head", split_axis=1, concat_axis=0, tiled=True)
+    left, right = grad_resid[:, :half_width], grad_resid[:, half_width:]
+    came_grad = swap_heads(jnp.where(first_core, right, left))
+    own_grad = jnp.where(first_core, left, right)
+    grad_heads = jnp.concatenate(
+        [jnp.where(first_core, own_grad, came_grad), jnp.where(first_core, came_grad, own_grad)],
+        axis=0,
+    )
     grad_normed = attend_backward(
         grad_heads, saved, query_w, key_proj, value_proj, query_gain, key_gain
     )
-    input_half = lax.dynamic_slice_in_dim(input32, head_index * half_width, half_width, 1)
-    whole = lax.psum(grad_normed.astype(jnp.bfloat16), "head").astype(jnp.float32)
-    grad_full = norm_backward(input32, input_scale, attn_gain, whole)
-    grad_attn = lax.dynamic_slice_in_dim(grad_full, head_index * half_width, half_width, 1)
-    grad_input = grad_heads + grad_attn
-    attribution = grad_input * input_half
-    token_score = lax.psum(jnp.sum(attribution, axis=1), "head")
+    input_half = lax.dynamic_slice_in_dim(layer_input, head_index * half_width, half_width, 1)
+    input_half = input_half.astype(jnp.float32)
+    gain_half = lax.dynamic_slice_in_dim(attn_gain, head_index * half_width, half_width, 0)
+    normed_left, normed_right = grad_normed[:, :half_width], grad_normed[:, half_width:]
+    came_half = swap_heads(jnp.where(first_core, normed_right, normed_left).astype(jnp.bfloat16))
+    own_half = jnp.where(first_core, normed_left, normed_right)
+    weighted = (own_half + came_half.astype(jnp.float32)) * gain_half[None, :]
+    inner_part = jnp.sum(weighted * input_half, axis=1)
+    direct_part = jnp.sum(grad_heads * input_half, axis=1)
+    parts = jnp.stack([inner_part, direct_part], axis=0)
+    inner_sum, direct_sum = parts + swap_heads(parts)
+    inner = inner_sum[:, None] / width
+    grad_attn = input_scale * weighted - input_half * input_scale**3 * inner
+    attribution = (grad_heads + grad_attn) * input_half
+    square_sum = jnp.sum(input32 * input32, axis=1)
+    scale_row = input_scale[:, 0]
+    token_score = direct_sum + (
+        scale_row * inner_sum - scale_row**3 * (inner_sum / width) * square_sum
+    )
+    moe_sum = mix_rows(out_back, target, flat_gates, moe_tokens, own_half[:8, :128]).reshape(moe_tokens, width)
+    mixed = (residual + moe_sum).astype(jnp.bfloat16)
     return (mixed, attribution, token_score)
 
 
 def solution(mesh):
     return jax.shard_map(
-        shards,
+        device_step,
         mesh=mesh,
         in_specs=(
             P("req", None),

time: 746 us -> 557 us (0.75)
  waiting for transfers between devices: 395 us -> 212 us
  local copies, waits for them, and re-layouts: 141 us -> 35.2 us
  Pallas kernels: 0 us -> 78.1 us
  matrix products: 99.8 us -> 123 us
  blocking collectives: 14.1 us -> 0 us
  starting transfers between devices: 32.3 us -> 42.8 us
    all_to_all x4 -> x5, waiting for transfers between devices: 272 us -> 113 us  [the longest x4 113 us: exchange(): lax.all_to_all(packed, ('req', 'head'), split_axis=0, concat_axis=0, tile...]
    pallas_call x0 -> x10, Pallas kernels: none -> 78.1 us  [the longest x4 32.6 us: fold_rows(): pl.pallas_call(fold_kernel, out_shape=jax.ShapeDtypeStruct((count, SUB, l...]
    reshape x8 -> x3, local copies, waits for them, and re-layouts: 68.9 us -> 3.74 us  [the longest x1 1.51 us: device_step(): slot_grad.reshape(device_count, capacity)]
    gather x8 -> x0, local copies, waits for them, and re-layouts: 32.7 us -> none  [the longest x1 11.9 us: shards(): grad_rows = grad_returned.reshape(device_count * capacity, width)[target]]
    psum x1 -> x0, waiting for transfers between devices: 23.7 us -> none  [shards(): lax.psum(grad_normed.astype(jnp.bfloat16), 'head').astype(jnp.float32)]
    scatter x1 -> x0, local copies, waits for them, and re-layouts: 21.7 us -> none  [shards(): jnp.zeros((device_count * capacity, width), jnp.bfloat16).at[target]]
    dot_general x8 -> x9, matrix products: 55 us -> 74.7 us  [the longest x1 19.8 us: device_step(): jnp.dot(grad_gate, gate_w.T, preferred_element_type=jnp.float32)]
    scatter x1 -> x0, other arithmetic: 12.1 us -> none  [shards(): jnp.zeros((device_count * capacity, width), jnp.bfloat16).at[target]]
  transfers between devices with their start and end apart: 6 -> 10, of which waited for: 6 -> 6; matrix products, arithmetic and copies ran while one was open for 22% -> 27% of each run, Pallas kernels for 0% -> 11%
where the time goes in v1:
time: 557 us; the launch traced here: 546 us
  waiting for transfers between devices  212 us (38%)
  matrix products  123 us (22%)
  Pallas kernels  78.1 us (14%)
  starting transfers between devices  42.8 us (8%)
  other arithmetic  40.3 us (7%)
  local copies, waits for them, and re-layouts  35.2 us (6%)
  between operations  15.1 us (3%)
    all_to_all x4, waiting for transfers between devices, exchange(): lax.all_to_all(packed, ('req', 'head'), split_axis=0, concat_axis=0, tile...  113 us
    all_gather x1, waiting for transfers between devices, device_step(): query_w = lax.all_gather(q_proj, 'req', axis=0, tiled=True)  95.8 us
    pallas_call x4, Pallas kernels, fold_rows(): pl.pallas_call(fold_kernel, out_shape=jax.ShapeDtypeStruct((count, SUB, l...  32.6 us
    all_to_all x4, starting transfers between devices, exchange(): lax.all_to_all(packed, ('req', 'head'), split_axis=0, concat_axis=0, tile...  32 us
    pallas_call x2, Pallas kernels, spread_rows(): pl.pallas_call(spread_kernel, out_shape=jax.ShapeDtypeStruct((count, sub...  22.1 us
    dot_general x1, matrix products, device_step(): jnp.dot(grad_gate, gate_w.T, preferred_element_type=jnp.float32)  19.8 us
    dot_general x1, matrix products, attend_backward(): jnp.dot(grad_query_raw, query_w.T, preferred_element_type=jnp.float32)  14.6 us
    dot_general x1, matrix products, device_step(): jnp.dot(grad_up, up_w.T, preferred_element_type=jnp.float32)  13.6 us
  transfers between devices with their start and end apart: 10, of which 6 were waited for; matrix products, arithmetic and copies ran while one was open for 27% of the time, Pallas kernels for 11%

profile of v1, /device:TPU:1, one launch (start us, length us, event | category | flops | bytes accessed | tf_op | source)
XLA Modules:
  0.0 545.8 jit_solution(13963630855907233952)
XLA Ops:
  10.4 2.9 fold_rows.4.rows_ref
  14.2 6.1 %pick_rows.2 = bf16[640,32,128]{2,1,0:T(8,128)(2,1)} custom-call(s32[640]{0:T(1024)} %reshape.328.index_ref, bf16[64,32,128]{2,1,0:T(8,128)(2,1)} %fold_rows.4.rows_ref), custom_call_target="tpu_custom_call" | custom-call | bytes 5242880 | tf_op jit(solution)/shard_map/pick_rows/pallas_call | solution.py:170
  22.1 95.8 %all-gather.2.cloned.1.call-done = bf16[4096,2048]{1,0:T(8,128)(2,1)} async-done(((bf16[64,2048]{1,0:T(8,128)(2,1)}), bf16[4096,2048]{1,0:T(8,128)(2,1)}) %all-gather.2.cloned.1.call-update) | async-done | bytes 16777232 | tf_op jit(solution)/shard_map/all_gather | solution.py:314
  117.9 8.4 %all-to-all-start.2 = ((bf16[128,160,128]{2,1,0:T(8,128)(2,1)}), bf16[128,160,128]{2,1,0:T(8,128)(2,1)}, u32[]{:S(2)}, u32[]{:S(2)}) async-start(bf16[128,160,128]{2,1,0:T(8,128)(2,1)} %bitcast.172), calls=%async_computation.2 | async-start | bytes 10485760 | tf_op jit(solution)/shard_map/all_to_all | solution.py:284
  127.4 8.2 %fusion.96 = f32[128,2048]{1,0:T(8,128)S(1)} fusion(bf16[4096,2048]{1,0:T(8,128)(2,1)} %all-gather.2.cloned.1.call-done, bf16[128,4096]{1,0:T(8,128)(2,1)S(1)} %copy-done.1, f32[4096]{0:T(1024)S(1)} %copy-done.29, f32[128]{0:T(128)S(1)} %add_rsqrt_fusion.3), kind=kOutput, calls=%fused_computation.193 | convolution fusion | flops 2149580800 | bytes 18891264 | tf_op jit(solution)/shard_map/dot_general | solution.py:69
  153.3 2.9 fold_rows.5.rows_ref
  156.3 6.0 %pick_rows.3 = bf16[640,32,128]{2,1,0:T(8,128)(2,1)} custom-call(s32[640]{0:T(1024)} %reshape.328.index_ref, bf16[64,32,128]{2,1,0:T(8,128)(2,1)} %fold_rows.5.rows_ref), custom_call_target="tpu_custom_call" | custom-call | bytes 5242880 | tf_op jit(solution)/shard_map/pick_rows/pallas_call | solution.py:170
  162.2 28.3 %all-to-all-done.2 = bf16[128,160,128]{2,1,0:T(8,128)(2,1)} async-done(((bf16[128,160,128]{2,1,0:T(8,128)(2,1)}), bf16[128,160,128]{2,1,0:T(8,128)(2,1)}, u32[]{:S(2)}, u32[]{:S(2)}) %all-to-all-start.2) | async-done | bytes 5242912 | tf_op jit(solution)/shard_map/all_to_all | solution.py:284
  190.6 7.2 %all-to-all-start = ((bf16[128,160,128]{2,1,0:T(8,128)(2,1)}), bf16[128,160,128]{2,1,0:T(8,128)(2,1)}, u32[]{:S(2)}, u32[]{:S(2)}) async-start(bf16[128,160,128]{2,1,0:T(8,128)(2,1)} %bitcast.174), calls=%async_computation | async-start | bytes 10485760 | tf_op jit(solution)/shard_map/all_to_all | solution.py:284
  197.8 11.1 %spread_rows.3 = bf16[640,4096]{1,0:T(8,128)(2,1)} custom-call(bf16[640,32,128]{2,1,0:T(8,128)(2,1)} %bitcast.20.rows_ref), custom_call_target="tpu_custom_call" | custom-call | bytes 10485760 | tf_op jit(solution)/shard_map/spread_rows/pallas_call | solution.py:237
  208.9 9.9 %fusion.1 = f32[640,768]{1,0:T(8,128)} fusion(bf16[640,4096]{1,0:T(8,128)(2,1)} %spread_rows.3, bf16[1,768,4096]{2,1,0:T(8,128)(2,1)} %param.28), kind=kOutput, calls=%fused_computation.3 | convolution fusion | flops 4026531840 | bytes 13500416 | tf_op jit(solution)/shard_map/dot_general | solution.py:363
  218.8 43.2 %all-to-all-done = bf16[128,160,128]{2,1,0:T(8,128)(2,1)} async-done(((bf16[128,160,128]{2,1,0:T(8,128)(2,1)}), bf16[128,160,128]{2,1,0:T(8,128)(2,1)}, u32[]{:S(2)}, u32[]{:S(2)}) %all-to-all-start) | async-done | bytes 5242912 | tf_op jit(solution)/shard_map/all_to_all | solution.py:284
  262.0 11.0 %spread_rows.2 = bf16[640,4096]{1,0:T(8,128)(2,1)} custom-call(bf16[640,32,128]{2,1,0:T(8,128)(2,1)} %bitcast.11.rows_ref), custom_call_target="tpu_custom_call" | custom-call | bytes 10485760 | tf_op jit(solution)/shard_map/spread_rows/pallas_call | solution.py:237
  273.0 8.1 %fusion.9 = f32[640,768]{1,0:T(8,128)S(1)} fusion(bf16[640,4096]{1,0:T(8,128)(2,1)} %spread_rows.2, bf16[1,4096,768]{2,1,0:T(8,128)(2,1)} %param.26), kind=kOutput, calls=%fused_computation.11 | convolution fusion | flops 4026531840 | bytes 13500416 | tf_op jit(solution)/shard_map/dot_general | solution.py:366
  281.2 9.6 %multiply_reduce_fusion = (f32[640]{0:T(1024)}, bf16[640,768]{1,0:T(8,128)(2,1)}, f32[640,768]{1,0:T(8,128)S(1)}) fusion(f32[640,768]{1,0:T(8,128)S(1)} %copy-done.53, f32[640,768]{1,0:T(8,128)S(1)} %fusion.9, bf16[640,4096]{1,0:T(8,128)(2,1)S(1)} %copy-done.9, bf16[1,4096,768]{2,1,0:T(8,128)(2,1)} %param.27), kind=kOutput, calls=%fused_computation.20 | convolution fusion | flops 4030955008 | bytes 18418176 | tf_op jit(solution)/shard_map/dot_general | solution.py:367
  290.8 19.8 %fusion.7 = f32[640,4096]{1,0:T(8,128)} fusion(bf16[1,4096,768]{2,1,0:T(8,128)(2,1)} %param.26, f32[640,768]{1,0:T(8,128)S(1)} %fusion.9, f32[640,768]{1,0:T(8,128)S(1)} %copy-done.53, f32[640,768]{1,0:T(8,128)S(1)} %get-tuple-element.49), kind=kOutput, calls=%fused_computation.9 | convolution fusion | flops 4031447040 | bytes 22675456 | tf_op jit(solution)/shard_map/dot_general | solution.py:385
  313.6 7.0 %all-to-all-start.4 = ((f32[128,1,128]{2,1,0:T(1,128)}), f32[128,1,128]{2,1,0:T(1,128)}, u32[]{:S(2)}, u32[]{:S(2)}) async-start(f32[128,1,128]{2,1,0:T(1,128)} %bitcast.183), calls=%async_computation.4 | async-start | bytes 131072 | tf_op jit(solution)/shard_map/all_to_all | solution.py:377
  320.6 13.6 %add_convert_fusion.rows_ref = bf16[640,4096]{1,0:T(8,128)(2,1)} fusion(f32[640,4096]{1,0:T(8,128)} %fusion.7, bf16[1,4096,768]{2,1,0:T(8,128)(2,1)} %param.27, f32[640,768]{1,0:T(8,128)} %fusion.1, f32[640,768]{1,0:T(8,128)} %copy-done.54), kind=kOutput, calls=%fused_computation.1 | convolution fusion | flops 4034723840 | bytes 25952256 | tf_op jit(solution)/shard_map/dot_general | solution.py:385
  334.2 13.4 %fold_rows.7 = bf16[640,32,128]{2,1,0:T(8,128)(2,1)} custom-call(bf16[640,4096]{1,0:T(8,128)(2,1)} %add_convert_fusion.rows_ref), custom_call_target="tpu_custom_call" | custom-call | bytes 10485760 | tf_op jit(solution)/shard_map/fold_rows/pallas_call | solution.py:263
  347.6 10.2 %all-to-all-start.3 = ((bf16[128,160,128]{2,1,0:T(8,128)(2,1)}), bf16[128,160,128]{2,1,0:T(8,128)(2,1)}, u32[]{:S(2)}, u32[]{:S(2)}) async-start(bf16[128,160,128]{2,1,0:T(8,128)(2,1)} %bitcast.173), calls=%async_computation.3 | async-start | bytes 10485760 | tf_op jit(solution)/shard_map/all_to_all | solution.py:284
  388.3 33.6 %all-to-all-done.3 = bf16[128,160,128]{2,1,0:T(8,128)(2,1)} async-done(((bf16[128,160,128]{2,1,0:T(8,128)(2,1)}), bf16[128,160,128]{2,1,0:T(8,128)(2,1)}, u32[]{:S(2)}, u32[]{:S(2)}) %all-to-all-start.3) | async-done | bytes 5242912 | tf_op jit(solution)/shard_map/all_to_all | solution.py:284
  422.0 5.6 %mix_rows.2 = f32[64,32,128]{2,1,0:T(8,128)} custom-call(s32[512]{0:T(512)} %reshape.331.index_ref, f32[512]{0:T(512)} %div.69.gate_ref, bf16[640,32,128]{2,1,0:T(8,128)(2,1)} %bitcast.22.rows_ref, f32[8,128]{1,0:T(8,128)} %slice.65.after_ref), custom_call_target="tpu_custom_call" | custom-call | flops 4194304 | bytes 5242880 | tf_op jit(solution)/shard_map/mix_rows/pallas_call | solution.py:205
  434.4 8.9 %convolution_convert_fusion.rows_ref = bf16[640,4096]{1,0:T(8,128)(2,1)} fusion(bf16[640,768]{1,0:T(8,128)(2,1)S(1)} %copy-done.55, bf16[1,768,4096]{2,1,0:T(8,128)(2,1)} %param.28), kind=kOutput, calls=%fused_computation.2 | convolution fusion | flops 4029153280 | bytes 12517376 | tf_op jit(solution)/shard_map/dot_general | solution.py:390
  443.2 13.4 %fold_rows.6 = bf16[640,32,128]{2,1,0:T(8,128)(2,1)} custom-call(bf16[640,4096]{1,0:T(8,128)(2,1)} %convolution_convert_fusion.rows_ref), custom_call_target="tpu_custom_call" | custom-call | bytes 10485760 | tf_op jit(solution)/shard_map/fold_rows/pallas_call | solution.py:263
  456.6 6.1 %all-to-all-start.1 = ((bf16[128,160,128]{2,1,0:T(8,128)(2,1)}), bf16[128,160,128]{2,1,0:T(8,128)(2,1)}, u32[]{:S(2)}, u32[]{:S(2)}) async-start(bf16[128,160,128]{2,1,0:T(8,128)(2,1)} %bitcast.171), calls=%async_computation.1 | async-start | bytes 10485760 | tf_op jit(solution)/shard_map/all_to_all | solution.py:284
  467.6 3.7 convolution_bitcast_fusion
  475.7 3.8 convolution_bitcast_fusion.3
  486.9 14.6 %fusion.41 = f32[128,4096]{1,0:T(8,128)} fusion(bf16[4096,2048]{1,0:T(8,128)(2,1)} %all-gather.2.cloned.1.call-done, f32[16,8,16,128]{3,2,1,0:T(8,128)} %bitcast.177, f32[128,2048]{1,0:T(8,128)S(1)} %fusion.96, f32[16,8,16,128]{3,2,1,0:T(8,128)} %bitcast.179, f32[16,8,16,128]{3,2,1,0:T(8,128)} %bitcast.178, f32[16,16,8,128]{3,2,1,0:T(8,128)} %get-tuple-element.20, ...), kind=kOutput, calls=%fused_computation.84 | convolution fusion | flops 2149056512 | bytes 24125440 | tf_op jit(solution)/shard_map/dot_general | solution.py:147
  501.5 3.5 convolution_add_fusion.1
  505.0 4.8 convolution_add_fusion
  518.9 8.0 %all-to-all-done.1 = bf16[128,160,128]{2,1,0:T(8,128)(2,1)} async-done(((bf16[128,160,128]{2,1,0:T(8,128)(2,1)}), bf16[128,160,128]{2,1,0:T(8,128)(2,1)}, u32[]{:S(2)}, u32[]{:S(2)}) %all-to-all-start.1) | async-done | bytes 5242912 | tf_op jit(solution)/shard_map/all_to_all | solution.py:284
  526.9 5.7 %mix_rows.3 = f32[64,32,128]{2,1,0:T(8,128)} custom-call(s32[512]{0:T(512)} %reshape.331.index_ref, f32[512]{0:T(512)} %div.69.gate_ref, bf16[640,32,128]{2,1,0:T(8,128)(2,1)} %bitcast.16.rows_ref, f32[8,128]{1,0:T(8,128)} %slice.74.after_ref), custom_call_target="tpu_custom_call" | custom-call | flops 4194304 | bytes 5242880 | tf_op jit(solution)/shard_map/mix_rows/pallas_call | solution.py:205
  (210 shorter events, 96.2 us)
Async XLA Ops:
  7.2 13.6 %copy-start = (bf16[4096,128]{1,0:T(8,128)(2,1)S(1)}, bf16[4096,128]{1,0:T(8,128)(2,1)}, u32[]{:S(2)}) copy-start(bf16[4096,128]{1,0:T(8,128)(2,1)} %param.17) | copy-start | bytes 3145732
  7.2 110.7 %all-gather.2.cloned.1.call-start = ((), (), s32[]{:S(2)}) async-start(), calls=%async_computation.5 | async-start | bytes 17039360 | tf_op jit(solution)/shard_map/all_gather | solution.py:314
  14.2 6.3 %copy-start.1 = (bf16[128,4096]{1,0:T(8,128)(2,1)S(1)}, bf16[128,4096]{1,0:T(8,128)(2,1)}, u32[]{:S(2)}) copy-start(bf16[128,4096]{1,0:T(8,128)(2,1)} %param.15) | copy-start | bytes 3145732
  14.2 6.6 %copy-start.29 = (f32[4096]{0:T(1024)S(1)}, f32[4096]{0:T(1024)}, u32[]{:S(2)}) copy-start(f32[4096]{0:T(1024)} %param.21) | copy-start | bytes 49156
  20.2 106.1 %copy-start.44 = (f32[64]{0:T(128)}, f32[64]{0:T(128)S(1)}, u32[]{:S(2)}) copy-start(f32[64]{0:T(128)S(1)} %multiply_power_fusion) | copy-start | bytes 772
  20.7 106.7 %copy-start.40 = (f32[128]{0:T(128)}, f32[128]{0:T(128)S(1)}, u32[]{:S(2)}) copy-start(f32[128]{0:T(128)S(1)} %add_rsqrt_fusion.3) | copy-start | bytes 1540
  20.8 105.6 %copy-start.46 = (f32[128]{0:T(128)}, f32[128]{0:T(128)S(1)}, u32[]{:S(2)}) copy-start(f32[128]{0:T(128)S(1)} %subtract_convert_fusion.3) | copy-start | bytes 1540
  21.4 96.5 %copy-start.20 = (f32[128,128]{0,1:T(8,128)}, f32[128,128]{0,1:T(8,128)S(1)}, u32[]{:S(2)}) copy-start(f32[128,128]{0,1:T(8,128)S(1)} %get-tuple-element.48) | copy-start | bytes 196612
  22.0 95.9 %copy-start.42 = (f32[128]{0:T(128)}, f32[128]{0:T(128)S(1)}, u32[]{:S(2)}) copy-start(f32[128]{0:T(128)S(1)} %get-tuple-element.44) | copy-start | bytes 1540
  117.9 9.0 %copy-start.18 = (bf16[4096,128]{1,0:T(8,128)(2,1)S(1)}, bf16[4096,128]{1,0:T(8,128)(2,1)}, u32[]{:S(2)}) copy-start(bf16[4096,128]{1,0:T(8,128)(2,1)} %param.18) | copy-start | bytes 3145732
  117.9 72.7 %all-to-all-start.2 = ((bf16[128,160,128]{2,1,0:T(8,128)(2,1)}), bf16[128,160,128]{2,1,0:T(8,128)(2,1)}, u32[]{:S(2)}, u32[]{:S(2)}) async-start(bf16[128,160,128]{2,1,0:T(8,128)(2,1)} %bitcast.172), calls=%async_computation.2 | async-start | bytes 10485760 | tf_op jit(solution)/shard_map/all_to_all | solution.py:284
  126.6 11.1 %copy-start.24 = (bf16[128,64]{0,1:T(8,128)(2,1)}, bf16[128,64]{0,1:T(8,128)(2,1)S(1)}, u32[]{:S(2)}) copy-start(bf16[128,64]{0,1:T(8,128)(2,1)S(1)} %get-tuple-element.34) | copy-start | bytes 49156
  126.6 11.1 %copy-start.26 = (bf16[128,64]{0,1:T(8,128)(2,1)}, bf16[128,64]{0,1:T(8,128)(2,1)S(1)}, u32[]{:S(2)}) copy-start(bf16[128,64]{0,1:T(8,128)(2,1)S(1)} %get-tuple-element.35) | copy-start | bytes 49156
  126.8 10.4 %copy-start.19 = (f32[128,64]{1,0:T(8,128)}, f32[128,64]{1,0:T(8,128)S(1)}, u32[]{:S(2)}) copy-start(f32[128,64]{1,0:T(8,128)S(1)} %copy.129) | copy-start | bytes 98308
  126.9 10.8 %copy-start.32 = (pred[128,128]{0,1:T(8,128)(4,1)}, pred[128,128]{0,1:T(8,128)(4,1)S(1)}, u32[]{:S(2)}) copy-start(pred[128,128]{0,1:T(8,128)(4,1)S(1)} %fusion.55) | copy-start | bytes 49156
  127.4 12.7 %copy-start.34 = (bf16[128,128,1]{1,0,2:T(8,128)(2,1)}, bf16[128,128,1]{1,0,2:T(8,128)(2,1)S(1)}, u32[]{:S(2)}) copy-start(bf16[128,128,1]{1,0,2:T(8,128)(2,1)S(1)} %fusion.23) | copy-start | bytes 98308
  145.4 6.9 %copy-start.23 = (f32[4096]{0:T(1024)S(1)}, f32[4096]{0:T(1024)}, u32[]{:S(2)}) copy-start(f32[4096]{0:T(1024)} %param.22) | copy-start | bytes 49156
  146.7 3.1 collective-permute-start
  190.6 71.4 %all-to-all-start = ((bf16[128,160,128]{2,1,0:T(8,128)(2,1)}), bf16[128,160,128]{2,1,0:T(8,128)(2,1)}, u32[]{:S(2)}, u32[]{:S(2)}) async-start(bf16[128,160,128]{2,1,0:T(8,128)(2,1)} %bitcast.174), calls=%async_computation | async-start | bytes 10485760 | tf_op jit(solution)/shard_map/all_to_all | solution.py:284
  273.0 8.2 %copy-start.9 = (bf16[640,4096]{1,0:T(8,128)(2,1)S(1)}, bf16[640,4096]{1,0:T(8,128)(2,1)}, u32[]{:S(2)}) copy-start(bf16[640,4096]{1,0:T(8,128)(2,1)} %spread_rows.2) | copy-start | bytes 15728644
  273.0 8.2 %copy-start.53 = (f32[640,768]{1,0:T(8,128)S(1)}, f32[640,768]{1,0:T(8,128)}, u32[]{:S(2)}) copy-start(f32[640,768]{1,0:T(8,128)} %fusion.1) | copy-start | bytes 5898244
  281.2 9.6 %copy-start.54 = (f32[640,768]{1,0:T(8,128)}, f32[640,768]{1,0:T(8,128)S(1)}, u32[]{:S(2)}) copy-start(f32[640,768]{1,0:T(8,128)S(1)} %fusion.9) | copy-start | bytes 5898244
  313.6 34.0 %all-to-all-start.4 = ((f32[128,1,128]{2,1,0:T(1,128)}), f32[128,1,128]{2,1,0:T(1,128)}, u32[]{:S(2)}, u32[]{:S(2)}) async-start(f32[128,1,128]{2,1,0:T(1,128)} %bitcast.183), calls=%async_computation.4 | async-start | bytes 131072 | tf_op jit(solution)/shard_map/all_to_all | solution.py:377
  347.6 74.4 %all-to-all-start.3 = ((bf16[128,160,128]{2,1,0:T(8,128)(2,1)}), bf16[128,160,128]{2,1,0:T(8,128)(2,1)}, u32[]{:S(2)}, u32[]{:S(2)}) async-start(bf16[128,160,128]{2,1,0:T(8,128)(2,1)} %bitcast.173), calls=%async_computation.3 | async-start | bytes 10485760 | tf_op jit(solution)/shard_map/all_to_all | solution.py:284
  433.2 29.6 %collective-permute-start.1 = (f32[64,2048]{1,0:T(8,128)}, f32[64,2048]{1,0:T(8,128)}, u32[]{:S(2)}, u32[]{:S(2)}) collective-permute-start(f32[64,2048]{1,0:T(8,128)} %slice_select_fusion.1), channel_id=1, source_target_pairs={{0,1},{1,0},{2,3},{3,2},{4,5},{5,4},{6,7},{7,6},{8,9},{9,8},{10,11... | collective-permute-start | bytes 1572872 | tf_op jit(solution)/shard_map/ppermute | solution.py:278
  456.6 70.3 %all-to-all-start.1 = ((bf16[128,160,128]{2,1,0:T(8,128)(2,1)}), bf16[128,160,128]{2,1,0:T(8,128)(2,1)}, u32[]{:S(2)}, u32[]{:S(2)}) async-start(bf16[128,160,128]{2,1,0:T(8,128)(2,1)} %bitcast.171), calls=%async_computation.1 | async-start | bytes 10485760 | tf_op jit(solution)/shard_map/all_to_all | solution.py:284
  479.5 7.4 %copy-start.33 = (f32[2048]{0:T(1024)S(1)}, f32[2048]{0:T(1024)}, u32[]{:S(2)}) copy-start(f32[2048]{0:T(1024)} %broadcast_bitcast_fusion) | copy-start | bytes 24580
  486.9 14.6 %copy-start.43 = (f32[128]{0:T(128)S(1)}, f32[128]{0:T(128)}, u32[]{:S(2)}) copy-start(f32[128]{0:T(128)} %copy-done.42) | copy-start | bytes 1540
  505.0 8.2 %copy-start.30 = (f32[4096]{0:T(1024)S(1)}, f32[4096]{0:T(1024)}, u32[]{:S(2)}) copy-start(f32[4096]{0:T(1024)} %param.21) | copy-start | bytes 49156
  505.0 10.1 %copy-start.10 = (f32[64,2048]{1,0:T(8,128)S(1)}, f32[64,2048]{1,0:T(8,128)}, u32[]{:S(2)}) copy-start(f32[64,2048]{1,0:T(8,128)} %get-tuple-element.13) | copy-start | bytes 1572868
  512.2 2.8 collective-permute-start.2
  517.3 18.1 %collective-permute-start.3 = (f32[2,128]{1,0:T(2,128)S(1)}, f32[2,128]{1,0:T(2,128)S(1)}, u32[]{:S(2)}, u32[]{:S(2)}) collective-permute-start(f32[2,128]{1,0:T(2,128)S(1)} %pad_maximum_fusion.8), channel_id=1, source_target_pairs={{0,1},{1,0},{2,3},{3,2},{4,5},{5,4},{6,7},{7,6},{8,9},{9,8},{10,11... | collective-permute-start | bytes 3080 | tf_op jit(solution)/shard_map/ppermute | solution.py:278
  (34 other events, 88.6 us)
Sparse Core Ops, SparseCore 0:
  10.9 106.9 all-gather.1

commit v2 on v1

v2 whole, which is shorter than its diff:
```python
import functools
import math

import jax
import jax.numpy as jnp
from jax import lax
from jax.experimental import pallas as pl
from jax.experimental.pallas import tpu as pltpu
from jax.sharding import PartitionSpec as P


EPS = 1e-06
THETA = 1000000.0
NEG = -1e30


def segments_of(lengths_row, token_count):
    ends = jnp.cumsum(lengths_row)
    starts = ends - lengths_row
    places = jnp.arange(token_count, dtype=jnp.int32)
    segment = jnp.sum((places[:, None] >= ends[None, :]).astype(jnp.int32), axis=1)
    picked = (
        segment[:, None] == jnp.arange(lengths_row.shape[0], dtype=jnp.int32)[None, :]
    ).astype(jnp.int32)
    start_of = jnp.sum(picked * starts[None, :], axis=1)
    return (segment, places - start_of)


def rope_tables(offsets, half_dim):
    freq = THETA ** (-jnp.arange(half_dim, dtype=jnp.float32) / half_dim)
    angle = offsets.astype(jnp.float32)[:, None] * freq[None, :]
    return (jnp.cos(angle), jnp.sin(angle))


def rotate(rows, cosine_table, sine_table):
    half_dim = rows.shape[-1] // 2
    first = rows[..., :half_dim]
    second = rows[..., half_dim:]
    return jnp.concatenate(
        [first * cosine_table - second * sine_table, second * cosine_table + first * sine_table],
        axis=-1,
    )


def rms_scale(values):
    return lax.rsqrt(jnp.mean(values * values, axis=-1, keepdims=True) + EPS)


def norm_backward(values, scale, gain, grad_out):
    weighted = grad_out * gain
    inner = jnp.mean(weighted * values, axis=-1, keepdims=True)
    return scale * weighted - values * scale**3 * inner


SUB = 32
VMEM_LIMIT = 56 * 1024 * 1024


def pick_kernel(index_ref, rows_ref, out_ref, folded):
    step_rows = out_ref.shape[0]
    base = pl.program_id(0) * step_rows

    @pl.when(pl.program_id(0) == 0)
    def _():
        folded[...] = rows_ref[...].reshape(folded.shape)

    def one(i, carry):
        out_ref[i] = folded[index_ref[base + i]]
        return carry

    lax.fori_loop(0, step_rows, one, 0, unroll=8)


def pick_rows(rows, index, step_rows=80):
    count = index.shape[0]
    tokens, width = rows.shape
    lanes = width // SUB
    return pl.pallas_call(
        pick_kernel,
        out_shape=jax.ShapeDtypeStruct((count, SUB, lanes), rows.dtype),
        grid_spec=pltpu.PrefetchScalarGridSpec(
            num_scalar_prefetch=1,
            grid=(count // step_rows,),
            in_specs=[pl.BlockSpec(rows.shape, lambda i, ids: (0, 0))],
            out_specs=pl.BlockSpec((step_rows, SUB, lanes), lambda i, ids: (i, 0, 0)),
            scratch_shapes=[pltpu.VMEM((tokens, SUB, lanes), rows.dtype)],
        ),
        cost_estimate=pl.CostEstimate(
            flops=0, transcendentals=0, bytes_accessed=count * width * 2
        ),
        name="pick_rows",
    )(index, rows)


def mix_kernel(index_ref, gate_ref, rows_ref, after_ref, out_ref):
    del after_ref
    step_tokens = out_ref.shape[0]
    top = index_ref.shape[0] // (step_tokens * pl.num_programs(0))
    base = pl.program_id(0) * step_tokens

    def one(i, carry):
        at = (base + i) * top
        total = gate_ref[at] * rows_ref[index_ref[at]].astype(jnp.float32)
        for k in range(1, top):
            total = total + gate_ref[at + k] * rows_ref[index_ref[at + k]].astype(jnp.float32)
        out_ref[i] = total
        return carry

    lax.fori_loop(0, step_tokens, one, 0, unroll=2)


def mix_rows(rows3, index, gates, tokens, after, step_tokens=16):
    _, sub, lanes = rows3.shape
    return pl.pallas_call(
        mix_kernel,
        out_shape=jax.ShapeDtypeStruct((tokens, sub, lanes), jnp.float32),
        grid_spec=pltpu.PrefetchScalarGridSpec(
            num_scalar_prefetch=2,
            grid=(tokens // step_tokens,),
            in_specs=[
                pl.BlockSpec(rows3.shape, lambda i, ids, g: (0, 0, 0)),
                pl.BlockSpec(after.shape, lambda i, ids, g: (0, 0)),
            ],
            out_specs=pl.BlockSpec((step_tokens, sub, lanes), lambda i, ids, g: (i, 0, 0)),
        ),
        cost_estimate=pl.CostEstimate(
            flops=index.shape[0] * sub * lanes * 2,
            transcendentals=0,
            bytes_accessed=rows3.shape[0] * sub * lanes * 2,
        ),
        name="mix_rows",
    )(index, gates, rows3, after)


def spread_kernel(rows_ref, out_ref):
    out_ref[...] = rows_ref[...].reshape(out_ref.shape)


def spread_rows(rows3, step_rows=128):
    count, sub, lanes = rows3.shape
    return pl.pallas_call(
        spread_kernel,
        out_shape=jax.ShapeDtypeStruct((count, sub * lanes), rows3.dtype),
        grid=(count // step_rows,),
        in_specs=[pl.BlockSpec((step_rows, sub, lanes), lambda i: (i, 0, 0))],
        out_specs=pl.BlockSpec((step_rows, sub * lanes), lambda i: (i, 0)),
        cost_estimate=pl.CostEstimate(
            flops=0, transcendentals=0, bytes_accessed=4 * count * sub * lanes
        ),
        name="spread_rows",
    )(rows3)


def fold_kernel(rows_ref, out_ref):
    out_ref[...] = rows_ref[...].reshape(out_ref.shape)


def fold_rows(rows, step_rows=128):
    count, width = rows.shape
    lanes = width // SUB
    return pl.pallas_call(
        fold_kernel,
        out_shape=jax.ShapeDtypeStruct((count, SUB, lanes), jnp.bfloat16),
        grid=(count // step_rows,),
        in_specs=[pl.BlockSpec((step_rows, width), lambda i: (i, 0))],
        out_specs=pl.BlockSpec((step_rows, SUB, lanes), lambda i: (i, 0, 0)),
        cost_estimate=pl.CostEstimate(
            flops=0, transcendentals=0, bytes_accessed=4 * count * width
        ),
        name="fold_rows",
    )(rows)


VM = pl.BlockSpec(memory_space=pltpu.VMEM)
NT = (((1,), (1,)), ((), ()))
TN = (((0,), (0,)), ((), ()))


def turn(rows, cosines, sines):
    return rows * cosines + pltpu.roll(rows, rows.shape[1] // 2, 1) * sines


def unturn(rows, cosines, sines):
    return rows * cosines - pltpu.roll(rows, rows.shape[1] // 2, 1) * sines


def attend_kernel(
    normed_ref,
    query_w_ref,
    key_ref,
    value_ref,
    cos_ref,
    sin_ref,
    gain_ref,
    mask_ref,
    context_ref,
    raw_ref,
    weight_ref,
    held,
):
    step = pl.program_id(0)
    head_dim = key_ref.shape[1]
    heads = query_w_ref.shape[1] // head_dim

    @pl.when(step == 0)
    def _():
        held[...] = jnp.zeros_like(held)

    ready = held.at[lax.rem(step + 1, 2)]
    raw = ready[...]
    raw_ref[...] = raw
    held[lax.rem(step, 2)] = jnp.dot(
        normed_ref[...], query_w_ref[...], preferred_element_type=jnp.float32
    )
    factor = 1.0 / math.sqrt(head_dim)
    for g in range(heads):
        cols = slice(g * head_dim, (g + 1) * head_dim)
        own = raw[:, cols]
        scale = lax.rsqrt(jnp.sum(own * own, axis=1, keepdims=True) / head_dim + EPS)
        rows = turn(own * scale * gain_ref[...], cos_ref[...], sin_ref[...]).astype(jnp.bfloat16)
        scores = lax.dot_general(rows, key_ref[...], NT, preferred_element_type=jnp.float32)
        terms = jnp.exp(jnp.where(mask_ref[...] > 0.0, scores * factor, NEG))
        weights = terms / jnp.sum(terms, axis=1, keepdims=True)
        weight_ref[:, cols] = weights
        context = jnp.dot(
            weights.astype(jnp.bfloat16), value_ref[...], preferred_element_type=jnp.float32
        )
        context_ref[:, cols] = context.astype(jnp.bfloat16)


def attend(normed, query_w, key_rows, value_rows, cosines, sines, gain, mask, block=256):
    tokens, width = normed.shape
    columns = query_w.shape[1]
    steps = columns // block
    late = pl.BlockSpec((tokens, block), lambda i: (0, jnp.maximum(i - 1, 0)))
    whole = lambda a: pl.BlockSpec(a.shape, lambda i: (0, 0))
    return pl.pallas_call(
        attend_kernel,
        out_shape=(
            jax.ShapeDtypeStruct((tokens, columns), jnp.bfloat16),
            jax.ShapeDtypeStruct((tokens, columns), jnp.float32),
            jax.ShapeDtypeStruct((tokens, columns), jnp.float32),
        ),
        grid=(steps + 1,),
        in_specs=[
            whole(normed),
            pl.BlockSpec((width, block), lambda i: (0, jnp.minimum(i, steps - 1))),
            whole(key_rows),
            whole(value_rows),
            whole(cosines),
            whole(sines),
            whole(gain),
            whole(mask),
        ],
        out_specs=(late, late, late),
        scratch_shapes=[pltpu.VMEM((2, tokens, block), jnp.float32)],
        cost_estimate=pl.CostEstimate(
            flops=2 * tokens * width * columns,
            transcendentals=0,
            bytes_accessed=2 * width * columns,
        ),
        name="attend",
    )(normed, query_w, key_rows, value_rows, cosines, sines, gain, mask)


def attend_back_kernel(
    grad_ref,
    weight_ref,
    raw_ref,
    key_ref,
    value_ref,
    key_raw_ref,
    cos_ref,
    sin_ref,
    gain_ref,
    key_gain_ref,
    query_out,
    key_out,
    value_out,
    key_sum,
    value_sum,
):
    step = pl.program_id(0)
    head_dim = key_ref.shape[1]
    heads = grad_ref.shape[1] // head_dim
    factor = 1.0 / math.sqrt(head_dim)
    cosines, sines, gain = cos_ref[...], sin_ref[...], gain_ref[...]

    @pl.when(step == 0)
    def _():
        key_sum[...] = jnp.zeros_like(key_sum)
        value_sum[...] = jnp.zeros_like(value_sum)

    key_total, value_total = key_sum[...], value_sum[...]
    for g in range(heads):
        cols = slice(g * head_dim, (g + 1) * head_dim)
        grad = grad_ref[:, cols]
        weights = weight_ref[:, cols]
        own = raw_ref[:, cols]
        scale = lax.rsqrt(jnp.sum(own * own, axis=1, keepdims=True) / head_dim + EPS)
        rows = turn(own * scale * gain, cosines, sines).astype(jnp.bfloat16)
        grad_weights = lax.dot_general(grad, value_ref[...], NT, preferred_element_type=jnp.float32)
        value_total += lax.dot_general(
            weights.astype(jnp.bfloat16), grad, TN, preferred_element_type=jnp.float32
        )
        centered = grad_weights - jnp.sum(grad_weights * weights, axis=1, keepdims=True)
        grad_scores = (weights * centered * factor).astype(jnp.bfloat16)
        key_total += lax.dot_general(grad_scores, rows, TN, preferred_element_type=jnp.float32)
        grad_rows = jnp.dot(grad_scores, key_ref[...], preferred_element_type=jnp.float32)
        weighted = unturn(grad_rows, cosines, sines) * gain
        inner = jnp.sum(weighted * own, axis=1, keepdims=True) / head_dim
        query_out[:, cols] = (scale * weighted - own * (scale * scale * scale) * inner).astype(
            jnp.bfloat16
        )
    key_sum[...] = key_total
    value_sum[...] = value_total

    @pl.when(step == pl.num_programs(0) - 1)
    def _():
        own = key_raw_ref[...]
        scale = lax.rsqrt(jnp.sum(own * own, axis=1, keepdims=True) / head_dim + EPS)
        weighted = unturn(key_sum[...], cosines, sines) * key_gain_ref[...]
        inner = jnp.sum(weighted * own, axis=1, keepdims=True) / head_dim
        key_out[...] = (scale * weighted - own * (scale * scale * scale) * inner).astype(
            jnp.bfloat16
        )
        value_out[...] = value_sum[...].astype(jnp.bfloat16)


def attend_back(
    grad, weights, raw, key_rows, value_rows, key_raw, cosines, sines, gain, key_gain, block=512
):
    tokens, columns = grad.shape
    head_dim = key_rows.shape[1]
    piece = pl.BlockSpec((tokens, block), lambda i: (0, i))
    whole = lambda a: pl.BlockSpec(a.shape, lambda i: (0, 0))
    small = pl.BlockSpec((tokens, head_dim), lambda i: (0, 0))
    rest = (key_rows, value_rows, key_raw, cosines, sines, gain, key_gain)
    return pl.pallas_call(
        attend_back_kernel,
        out_shape=(
            jax.ShapeDtypeStruct((tokens, columns), jnp.bfloat16),
            jax.ShapeDtypeStruct((tokens, head_dim), jnp.bfloat16),
            jax.ShapeDtypeStruct((tokens, head_dim), jnp.bfloat16),
        ),
        grid=(columns // block,),
        in_specs=[piece, piece, piece, *map(whole, rest)],
        out_specs=(piece, small, small),
        scratch_shapes=[pltpu.VMEM((tokens, head_dim), jnp.float32)] * 2,
        cost_estimate=pl.CostEstimate(
            flops=12 * tokens * tokens * columns,
            transcendentals=0,
            bytes_accessed=12 * tokens * columns,
        ),
        name="attend_back",
    )(grad, weights, raw, *rest)


def project_kernel(at_ref, query_ref, key_ref, value_ref, query_w, key_w, value_w, out_ref):
    del at_ref
    total = lax.dot_general(query_ref[...], query_w[...], NT, preferred_element_type=jnp.float32)
    total += lax.dot_general(key_ref[...], key_w[...], NT, preferred_element_type=jnp.float32)
    total += lax.dot_general(value_ref[...], value_w[...], NT, preferred_element_type=jnp.float32)
    out_ref[...] = total.astype(out_ref.dtype)


def project_back(part, query_grad, key_grad, value_grad, query_w, key_w, value_w, dtype, block=512):
    tokens, columns = query_grad.shape
    width, _ = key_w.shape
    steps = width // 2 // block
    whole = lambda a: pl.BlockSpec(a.shape, lambda i, at: (0, 0))
    rows = lambda a: pl.BlockSpec((block, a.shape[1]), lambda i, at: (at[0] * steps + i, 0))
    return pl.pallas_call(
        project_kernel,
        out_shape=jax.ShapeDtypeStruct((tokens, width // 2), dtype),
        grid_spec=pltpu.PrefetchScalarGridSpec(
            num_scalar_prefetch=1,
            grid=(steps,),
            in_specs=[
                whole(query_grad),
                whole(key_grad),
                whole(value_grad),
                rows(query_w),
                rows(key_w),
                rows(value_w),
            ],
            out_specs=pl.BlockSpec((tokens, block), lambda i, at: (0, i)),
        ),
        cost_estimate=pl.CostEstimate(
            flops=tokens * columns * width,
            transcendentals=0,
            bytes_accessed=columns * width,
        ),
        name="project_back",
    )(part, query_grad, key_grad, value_grad, query_w, key_w, value_w)


def expert_kernel(
    rows_hbm,
    gate_hbm,
    up_hbm,
    cot_hbm,
    grad_hbm,
    hidden_ref,
    slot_ref,
    rows_v,
    gate_w,
    up_w,
    cot_ref,
    pre_gate,
    pre_up,
    grad_gate,
    grad_up,
    sem_in,
    sem_gate,
    sem_up,
    sem_cot,
    sem_out,
    *,
    chunks,
    row_block,
):
    count, sub, lanes = rows_v.shape
    width = sub * lanes
    piece, part = sub // chunks, width // chunks

    def arrive(k):
        at = pl.ds(k * piece, piece)
        return pltpu.make_async_copy(rows_hbm.at[:, at, :], rows_v.at[:, at, :], sem_in.at[k])

    def leave(k):
        at = pl.ds(k * piece, piece)
        return pltpu.make_async_copy(rows_v.at[:, at, :], grad_hbm.at[:, at, :], sem_out.at[k])

    def gate_in(k):
        at = pl.ds(k * part, part)
        return pltpu.make_async_copy(gate_hbm.at[at, :], gate_w.at[at, :], sem_gate.at[k])

    def up_in(k):
        at = pl.ds(k * part, part)
        return pltpu.make_async_copy(up_hbm.at[at, :], up_w.at[at, :], sem_up.at[k])

    cot_in = pltpu.make_async_copy(cot_hbm, cot_ref, sem_cot)
    for k in range(chunks):
        arrive(k).start()
        gate_in(k).start()
        up_in(k).start()
    cot_in.start()
    for k in range(chunks):
        arrive(k).wait()
        gate_in(k).wait()
        up_in(k).wait()
        rows = rows_v[:, k * piece : (k + 1) * piece, :].reshape(count, part)
        at = slice(k * part, (k + 1) * part)
        gate = jnp.dot(rows, gate_w[at, :], preferred_element_type=jnp.float32)
        up = jnp.dot(rows, up_w[at, :], preferred_element_type=jnp.float32)
        if k == 0:
            pre_gate[...] = gate
            pre_up[...] = up
        else:
            pre_gate[...] += gate
            pre_up[...] += up

    cot_in.wait()
    slot_count = slot_ref.shape[0]

    def between(r, carry):
        at = pl.ds(pl.multiple_of(r * row_block, 16), row_block)
        gate, up, cot = pre_gate[at, :], pre_up[at, :], cot_ref[at, :]
        sigmoid = 1.0 / (1.0 + jnp.exp(-gate))
        silu = gate * sigmoid
        hidden = (silu * up).astype(jnp.bfloat16)
        hidden_ref[at, :] = hidden
        grad_up[at, :] = (cot * silu).astype(jnp.bfloat16)
        grad_gate[at, :] = (cot * up * sigmoid * (1.0 + gate * (1.0 - sigmoid))).astype(
            jnp.bfloat16
        )
        slot = jnp.sum(hidden.astype(jnp.float32) * cot, axis=1, keepdims=True)
        row = lax.broadcasted_iota(jnp.int32, (row_block, 128), 0) + r * row_block
        block = jnp.floor((row.astype(jnp.float32) + 0.5) * (slot_count / count))
        block = block.astype(jnp.int32)
        lane = lax.broadcasted_iota(jnp.int32, (row_block, 128), 1)
        per = count // slot_count
        spread = jnp.where(row - block * per == lane, slot, 0.0)
        select = jnp.where(block == lane, 1.0, 0.0).astype(jnp.bfloat16)
        for _ in range(3):
            rounded = spread.astype(jnp.bfloat16)
            slot_ref[...] += lax.dot_general(
                select, rounded, TN, preferred_element_type=jnp.float32
            )
            spread = spread - rounded.astype(jnp.float32)
        return carry

    slot_ref[...] = jnp.zeros_like(slot_ref)

    lax.fori_loop(0, count // row_block, between, 0)
    for k in range(chunks):
        at = slice(k * part, (k + 1) * part)
        grad = lax.dot_general(grad_gate[...], gate_w[at, :], NT, preferred_element_type=jnp.float32)
        grad += lax.dot_general(grad_up[...], up_w[at, :], NT, preferred_element_type=jnp.float32)
        rows_v[:, k * piece : (k + 1) * piece, :] = grad.astype(jnp.bfloat16).reshape(
            count, piece, lanes
        )
        leave(k).start()
    for k in range(chunks):
        leave(k).wait()


def expert(rows3, gate_w, up_w, cot_hidden, slot_count, chunks=4, row_block=80):
    count = rows3.shape[0]
    inner = gate_w.shape[1]
    hbm = pl.BlockSpec(memory_space=pltpu.HBM)
    return pl.pallas_call(
        functools.partial(expert_kernel, chunks=chunks, row_block=row_block),
        out_shape=(
            jax.ShapeDtypeStruct(rows3.shape, jnp.bfloat16),
            jax.ShapeDtypeStruct((count, inner), jnp.bfloat16),
            jax.ShapeDtypeStruct((slot_count, 128), jnp.float32),
        ),
        in_specs=[hbm, hbm, hbm, hbm],
        out_specs=(hbm, VM, VM),
        scratch_shapes=[
            pltpu.VMEM(rows3.shape, jnp.bfloat16),
            pltpu.VMEM(gate_w.shape, jnp.bfloat16),
            pltpu.VMEM(up_w.shape, jnp.bfloat16),
            pltpu.VMEM((count, inner), jnp.float32),
            pltpu.VMEM((count, inner), jnp.float32),
            pltpu.VMEM((count, inner), jnp.float32),
            pltpu.VMEM((count, inner), jnp.bfloat16),
            pltpu.VMEM((count, inner), jnp.bfloat16),
            pltpu.SemaphoreType.DMA((chunks,)),
            pltpu.SemaphoreType.DMA((chunks,)),
            pltpu.SemaphoreType.DMA((chunks,)),
            pltpu.SemaphoreType.DMA,
            pltpu.SemaphoreType.DMA((chunks,)),
        ],
        compiler_params=pltpu.CompilerParams(vmem_limit_bytes=VMEM_LIMIT),
        cost_estimate=pl.CostEstimate(
            flops=8 * count * inner * gate_w.shape[0],
            transcendentals=0,
            bytes_accessed=4 * rows3.shape[0] * gate_w.shape[0],
        ),
        name="expert",
    )(rows3, gate_w, up_w, cot_hidden)


def swap_heads(values):
    return lax.ppermute(values, "head", [(0, 1), (1, 0)])


def exchange(rows3, device_count):
    count, sub, lanes = rows3.shape
    packed = rows3.reshape(device_count, (count // device_count) * sub, lanes)
    moved = lax.all_to_all(packed, ("req", "head"), split_axis=0, concat_axis=0, tiled=True)
    return moved.reshape(count, sub, lanes)


def device_step(
    layer_input,
    q_proj,
    key_proj,
    value_proj,
    query_gain,
    key_gain,
    attn_gain,
    moe_gain,
    router,
    expert_ids,
    req_lengths,
    w_gate,
    w_up,
    w_down,
    cotangent,
):
    head_count = lax.axis_size("head")
    head_index = lax.axis_index("head")
    device_count = lax.axis_size("req") * head_count
    token_count, width = layer_input.shape
    moe_tokens = token_count // head_count
    half_width = width // head_count
    capacity = 5
    first_core = head_index == 0

    query_w = lax.all_gather(q_proj, "req", axis=0, tiled=True)

    expert_range = jnp.arange(device_count, dtype=jnp.int32)
    chosen_mask = expert_ids[:, :, None] == expert_range[None, None, :]
    member = jnp.any(chosen_mask, axis=1)
    token_range = jnp.arange(moe_tokens, dtype=jnp.int32)
    before = (token_range[:, None] > token_range[None, :]).astype(jnp.bfloat16)
    rank = jnp.dot(before, member.astype(jnp.bfloat16), preferred_element_type=jnp.float32)
    rank = rank.astype(jnp.int32)
    slot_of = jnp.sum(jnp.where(chosen_mask, rank[:, None, :], 0), axis=2)
    target = (expert_ids * capacity + slot_of).reshape(-1)
    slot_range = jnp.arange(capacity, dtype=jnp.int32)
    hit = member[:, :, None] & (rank[:, :, None] == slot_range[None, None, :])
    source = jnp.sum(jnp.where(hit, token_range[:, None, None], 0), axis=0).reshape(-1)

    cot_send = pick_rows(cotangent, source)

    segment, offsets = segments_of(req_lengths[0], token_count)
    input32 = layer_input.astype(jnp.float32)
    input_scale = rms_scale(input32)
    normed = (input32 * input_scale * attn_gain[None, :]).astype(jnp.bfloat16)
    head_dim = key_proj.shape[1]
    cosine_table, sine_table = rope_tables(offsets, head_dim // 2)
    key_raw = jnp.dot(normed, key_proj, preferred_element_type=jnp.float32)
    key_normed = key_raw * rms_scale(key_raw) * key_gain
    key_rows = rotate(key_normed, cosine_table, sine_table).astype(jnp.bfloat16)
    value_rows = jnp.dot(normed, value_proj, preferred_element_type=jnp.float32)
    value_rows = value_rows.astype(jnp.bfloat16)
    places = jnp.arange(token_count, dtype=jnp.int32)
    allowed = (segment[:, None] == segment[None, :]) & (places[None, :] <= places[:, None])
    mask = allowed.astype(jnp.float32)
    cosines = jnp.concatenate([cosine_table, cosine_table], axis=1)
    sines = jnp.concatenate([-sine_table, sine_table], axis=1)
    query_gain2, key_gain2 = query_gain[None, :], key_gain[None, :]
    prep = (cot_send, query_w, normed, key_raw, key_rows, value_rows, cosines, sines, mask)
    prep = (*prep, target)
    prep = lax.optimization_barrier(prep)
    cot_send, query_w, normed, key_raw, key_rows, value_rows, cosines, sines, mask, target = prep
    cot_rows3 = exchange(cot_send, device_count)
    context, query_raw, attn_weights = attend(
        normed, query_w, key_rows, value_rows, cosines, sines, query_gain2, mask
    )
    other_rows = lax.dynamic_slice_in_dim(context, (1 - head_index) * moe_tokens, moe_tokens, 0)
    own_rows = lax.dynamic_slice_in_dim(context, head_index * moe_tokens, moe_tokens, 0)
    came = swap_heads(other_rows)
    context_tok = jnp.concatenate(
        [jnp.where(first_core, own_rows, came), jnp.where(first_core, came, own_rows)], axis=1
    )
    own_input = lax.dynamic_slice_in_dim(layer_input, head_index * moe_tokens, moe_tokens, 0)
    residual = own_input.astype(jnp.float32) + context_tok.astype(jnp.float32)
    moe_scale = rms_scale(residual)
    moe_in = (residual * moe_scale * moe_gain[None, :]).astype(jnp.bfloat16)
    moe_send = pick_rows(moe_in, source)
    rows3 = exchange(moe_send, device_count)

    logits = jnp.dot(moe_in, router, preferred_element_type=jnp.float32)
    chosen = jnp.sum(jnp.where(chosen_mask, logits[:, None, :], 0.0), axis=2)
    gates = jax.nn.softmax(chosen, axis=1)
    flat_gates = gates.reshape(-1)
    cot32 = cotangent.astype(jnp.float32)

    gate_w = w_gate[0]
    up_w = w_up[0]
    down_w = w_down[0]
    cot_rows = spread_rows(cot_rows3)
    cot_hidden = jnp.dot(cot_rows, down_w.T, preferred_element_type=jnp.float32)
    cot_hidden = lax.optimization_barrier(cot_hidden)
    grad_send, hidden, slot_grad = expert(rows3, gate_w, up_w, cot_hidden, device_count)
    slot_back = lax.all_to_all(
        slot_grad.reshape(device_count, 1, 128),
        ("req", "head"),
        split_axis=0,
        concat_axis=0,
        tiled=True,
    )
    slot_back = slot_back.reshape(device_count, 128)[:, :capacity]
    grad_back = exchange(grad_send, device_count)
    outputs = jnp.dot(hidden, down_w, preferred_element_type=jnp.float32).astype(jnp.bfloat16)
    out_send = fold_rows(outputs)
    out_back = exchange(out_send, device_count)

    hit_grad = jnp.sum(jnp.where(hit, slot_back[None, :, :], 0.0), axis=2)
    gate_grad = jnp.sum(jnp.where(chosen_mask, hit_grad[:, None, :], 0.0), axis=2)
    total_gate = jnp.sum(gates * gate_grad, axis=1, keepdims=True)
    grad_logit = gates * (gate_grad - total_gate)
    dense = jnp.sum(jnp.where(chosen_mask, grad_logit[:, :, None], 0.0), axis=1)
    router_part = jnp.dot(
        dense, router.astype(jnp.float32).T, precision=lax.Precision.HIGHEST
    )
    router_part = lax.optimization_barrier(router_part)
    grad_in = mix_rows(grad_back, target, flat_gates, moe_tokens, router_part[:8, :128])
    grad_in = grad_in.reshape(moe_tokens, width)
    grad_in = grad_in + router_part
    grad_resid = cot32 + norm_backward(residual, moe_scale, moe_gain, grad_in)
    left, right = grad_resid[:, :half_width], grad_resid[:, half_width:]
    came_grad = swap_heads(jnp.where(first_core, right, left))
    own_grad = jnp.where(first_core, left, right)
    grad_heads = jnp.concatenate(
        [jnp.where(first_core, own_grad, came_grad), jnp.where(first_core, came_grad, own_grad)],
        axis=0,
    )
    query_grad, key_grad, value_grad = attend_back(
        grad_heads.astype(jnp.bfloat16),
        attn_weights,
        query_raw,
        key_rows,
        value_rows,
        key_raw,
        cosines,
        sines,
        query_gain2,
        key_gain2,
    )
    weights3 = (query_w, key_proj, value_proj)
    grads3 = (query_grad, key_grad, value_grad)
    other_half = project_back((1 - head_index)[None], *grads3, *weights3, jnp.bfloat16)
    came_half = swap_heads(other_half)
    own_half = project_back(head_index[None], *grads3, *weights3, jnp.float32)
    input_half = lax.dynamic_slice_in_dim(layer_input, head_index * half_width, half_width, 1)
    input_half = input_half.astype(jnp.float32)
    gain_half = lax.dynamic_slice_in_dim(attn_gain, head_index * half_width, half_width, 0)
    weighted = (own_half + came_half.astype(jnp.float32)) * gain_half[None, :]
    inner_part = jnp.sum(weighted * input_half, axis=1)
    direct_part = jnp.sum(grad_heads * input_half, axis=1)
    parts = jnp.stack([inner_part, direct_part], axis=0)
    inner_sum, direct_sum = parts + swap_heads(parts)
    inner = inner_sum[:, None] / width
    grad_attn = input_scale * weighted - input_half * input_scale**3 * inner
    attribution = (grad_heads + grad_attn) * input_half
    square_sum = jnp.sum(input32 * input32, axis=1)
    scale_row = input_scale[:, 0]
    token_score = direct_sum + (
        scale_row * inner_sum - scale_row**3 * (inner_sum / width) * square_sum
    )
    moe_sum = mix_rows(out_back, target, flat_gates, moe_tokens, own_half[:8, :128]).reshape(moe_tokens, width)
    mixed = (residual + moe_sum).astype(jnp.bfloat16)
    return (mixed, attribution, token_score)


def solution(mesh):
    return jax.shard_map(
        device_step,
        mesh=mesh,
        in_specs=(
            P("req", None),
            P("req", "head"),
            P(None, "head"),
            P(None, "head"),
            P(),
            P(),
            P(),
            P(),
            P(),
            P(("req", "head"), None),
            P("req", None),
            P(("req", "head"), None, None),
            P(("req", "head"), None, None),
            P(("req", "head"), None, None),
            P(("req", "head"), None),
        ),
        out_specs=(P(("req", "head"), None), P("req", "head"), P("req")),
        check_vma=False,
    )
```

time: 557 us -> 474 us (0.85)
  matrix products: 123 us -> 24.4 us
  waiting for transfers between devices: 212 us -> 243 us
  local copies, waits for them, and re-layouts: 35.2 us -> 9.02 us
  Pallas kernels: 78.1 us -> 101 us
  blocking collectives: 0 us -> 16.1 us
  other arithmetic: 40.3 us -> 26.8 us
  starting transfers between devices: 42.8 us -> 32.6 us
    dot_general x15 -> x2, matrix products: 96.3 us -> 3.16 us  [the longest x1 2.14 us: device_step(): key_raw = jnp.dot(normed, key_proj, preferred_element_type=jnp.float32)]
    pallas_call x2 -> x7, Pallas kernels: 12 us -> 74.4 us  [the longest x1 25.8 us: expert(): pl.pallas_call(functools.partial(expert_kernel, chunks=chunks, row_block=...]
    all_to_all x4, waiting for transfers between devices: 113 us -> 152 us  [exchange(): lax.all_to_all(packed, ('req', 'head'), split_axis=0, concat_axis=0, tile...]
    pallas_call x4 -> x1, Pallas kernels: 32.6 us -> 7.66 us  [fold_rows(): pl.pallas_call(fold_kernel, out_shape=jax.ShapeDtypeStruct((count, SUB, l...]
    all_to_all x0 -> x1, blocking collectives: none -> 16.1 us  [device_step(): lax.all_to_all(slot_grad.reshape(device_count, 1, 128), ('req', 'head'),...]
    pallas_call x2 -> x1, Pallas kernels: 22.1 us -> 7.36 us  [spread_rows(): pl.pallas_call(spread_kernel, out_shape=jax.ShapeDtypeStruct((count, sub...]
    unnamed x118 -> x51, local copies, waits for them, and re-layouts: 11 us -> 2.85 us
    all_gather x1, waiting for transfers between devices: 95.8 us -> 88.5 us  [device_step(): query_w = lax.all_gather(q_proj, 'req', axis=0, tiled=True)]
  transfers between devices with their start and end apart: 10 -> 9, of which waited for: 6 -> 7; matrix products, arithmetic and copies ran while one was open for 27% -> 11% of each run, Pallas kernels for 11% -> 16%
where the time goes in v2:
time: 474 us; the launch traced here: 467 us
  waiting for transfers between devices  243 us (51%)
  Pallas kernels  101 us (21%)
  starting transfers between devices  32.6 us (7%)
  other arithmetic  26.8 us (6%)
  matrix products  24.4 us (5%)
  blocking collectives  16.1 us (3%)
  between operations  14.7 us (3%)
  local copies, waits for them, and re-layouts  9.02 us (2%)
    all_to_all x4, waiting for transfers between devices, exchange(): lax.all_to_all(packed, ('req', 'head'), split_axis=0, concat_axis=0, tile...  152 us
    all_gather x1, waiting for transfers between devices, device_step(): query_w = lax.all_gather(q_proj, 'req', axis=0, tiled=True)  88.5 us
    all_to_all x4, starting transfers between devices, exchange(): lax.all_to_all(packed, ('req', 'head'), split_axis=0, concat_axis=0, tile...  28.5 us
    pallas_call x1, Pallas kernels, expert(): pl.pallas_call(functools.partial(expert_kernel, chunks=chunks, row_block=...  25.8 us
    all_to_all x1, blocking collectives, device_step(): lax.all_to_all(slot_grad.reshape(device_count, 1, 128), ('req', 'head'),...  16.1 us
    pallas_call x2, Pallas kernels, project_back(): pl.pallas_call(project_kernel, out_shape=jax.ShapeDtypeStruct((tokens, wi...  14.5 us
    pallas_call x1, Pallas kernels, attend(): pl.pallas_call(attend_kernel, out_shape=(jax.ShapeDtypeStruct((tokens, co...  13.5 us
    pallas_call x2, Pallas kernels, pick_rows(): pl.pallas_call(pick_kernel, out_shape=jax.ShapeDtypeStruct((count, SUB, l...  12.5 us
  transfers between devices with their start and end apart: 9, of which 7 were waited for; matrix products, arithmetic and copies ran while one was open for 11% of the time, Pallas kernels for 16%

profile of v2, /device:TPU:1, one launch (start us, length us, event | category | flops | bytes accessed | tf_op | source)
XLA Modules:
  0.0 467.1 jit_solution(5316412539808407187)
XLA Ops:
  12.7 1.5 fusion.3
  15.3 1.6 fusion.5.normed_ref
  16.9 2.1 multiply_reduce_fusion.2
  19.4 6.2 %pick_rows.2 = bf16[640,32,128]{2,1,0:T(8,128)(2,1)} custom-call(s32[640]{0:T(1024)} %reshape.190.index_ref, bf16[64,4096]{1,0:T(8,128)(2,1)} %rows_ref.1), custom_call_target="tpu_custom_call" | custom-call | bytes 5242880 | tf_op jit(solution)/shard_map/pick_rows/pallas_call | solution.py:78
  29.4 88.5 %all-gather.2.cloned.1.call-done.query_w_ref.query_w = bf16[4096,2048]{1,0:T(8,128)(2,1)} async-done(((bf16[64,2048]{1,0:T(8,128)(2,1)}), bf16[4096,2048]{1,0:T(8,128)(2,1)}) %all-gather.2.cloned.1.call-update) | async-done | bytes 16777232 | tf_op jit(solution)/shard_map/all_gather | solution.py:584
  117.9 8.4 %all-to-all-start.1 = ((bf16[128,160,128]{2,1,0:T(8,128)(2,1)}), bf16[128,160,128]{2,1,0:T(8,128)(2,1)}, u32[]{:S(2)}, u32[]{:S(2)}) async-start(bf16[128,160,128]{2,1,0:T(8,128)(2,1)} %bitcast.71), calls=%async_computation.1 | async-start | bytes 10485760 | tf_op jit(solution)/shard_map/all_to_all | solution.py:554
  126.4 13.5 %attend.1 = (bf16[128,2048]{1,0:T(8,128)(2,1)}, f32[128,2048]{1,0:T(8,128)}, f32[128,2048]{1,0:T(8,128)}) custom-call(bf16[128,4096]{1,0:T(8,128)(2,1)} %copy-done.2, bf16[4096,2048]{1,0:T(8,128)(2,1)} %all-gather.2.cloned.1.call-done.query_w_ref.query_w, bf16[128,128]{1,0:T(8,128)(2,1)} %pad_maximum_fusion.4.key_ref, ...), custom_call_target="tpu_custom_call" | custom-call | flops 2147483648 | bytes 16777216 | tf_op jit(solution)/shard_map/attend/pallas_call | solution.py:237
  146.1 6.2 %pick_rows.3 = bf16[640,32,128]{2,1,0:T(8,128)(2,1)} custom-call(s32[640]{0:T(1024)} %reshape.190.index_ref, bf16[64,4096]{1,0:T(8,128)(2,1)} %multiply_convert_fusion.rows_ref), custom_call_target="tpu_custom_call" | custom-call | bytes 5242880 | tf_op jit(solution)/shard_map/pick_rows/pallas_call | solution.py:78
  152.3 38.3 %all-to-all-done.1 = bf16[128,160,128]{2,1,0:T(8,128)(2,1)} async-done(((bf16[128,160,128]{2,1,0:T(8,128)(2,1)}), bf16[128,160,128]{2,1,0:T(8,128)(2,1)}, u32[]{:S(2)}, u32[]{:S(2)}) %all-to-all-start.1) | async-done | bytes 5242912 | tf_op jit(solution)/shard_map/all_to_all | solution.py:554
  190.6 7.5 %all-to-all-start = ((bf16[128,160,128]{2,1,0:T(8,128)(2,1)}), bf16[128,160,128]{2,1,0:T(8,128)(2,1)}, u32[]{:S(2)}, u32[]{:S(2)}) async-start(bf16[128,160,128]{2,1,0:T(8,128)(2,1)} %bitcast.72), calls=%async_computation | async-start | bytes 10485760 | tf_op jit(solution)/shard_map/all_to_all | solution.py:554
  198.0 7.4 %spread_rows.1 = bf16[640,4096]{1,0:T(8,128)(2,1)} custom-call(bf16[640,32,128]{2,1,0:T(8,128)(2,1)} %bitcast.10.rows_ref), custom_call_target="tpu_custom_call" | custom-call | bytes 10485760 | tf_op jit(solution)/shard_map/spread_rows/pallas_call | solution.py:141
  205.4 9.9 %fusion.1.cot_hbm = f32[640,768]{1,0:T(8,128)} fusion(bf16[640,4096]{1,0:T(8,128)(2,1)} %spread_rows.1, bf16[1,768,4096]{2,1,0:T(8,128)(2,1)} %param.28), kind=kOutput, calls=%fused_computation.2 | convolution fusion | flops 4026531840 | bytes 13500416 | tf_op jit(solution)/shard_map/dot_general | solution.py:649
  215.3 46.8 %all-to-all-done = bf16[128,160,128]{2,1,0:T(8,128)(2,1)} async-done(((bf16[128,160,128]{2,1,0:T(8,128)(2,1)}), bf16[128,160,128]{2,1,0:T(8,128)(2,1)}, u32[]{:S(2)}, u32[]{:S(2)}) %all-to-all-start) | async-done | bytes 5242912 | tf_op jit(solution)/shard_map/all_to_all | solution.py:554
  262.2 25.8 %expert.1 = (bf16[640,32,128]{2,1,0:T(8,128)(2,1)}, bf16[640,768]{1,0:T(8,128)(2,1)}, f32[128,128]{1,0:T(8,128)}) custom-call(bf16[640,32,128]{2,1,0:T(8,128)(2,1)} %bitcast.6.rows_hbm, bf16[4096,768]{1,0:T(8,128)(2,1)} %bitcast.86, bf16[4096,768]{1,0:T(8,128)(2,1)} %bitcast.87, f32[640,768]{1,0:T(8,128)} %fusion.1.cot_hbm), custom_call_target="tpu_custom_call" | custom-call | flops 16106127360 | bytes 10485760 | tf_op jit(solution)/shard_map/expert/pallas_call | solution.py:513
  288.0 16.1 %all_to_all.25 = f32[128,1,128]{2,1,0:T(1,128)S(1)} all-to-all(f32[128,1,128]{2,1,0:T(1,128)} %bitcast.78), channel_id=1, replica_groups=mesh['req'=64,'head'=2] {'req','head'}, dimensions={0} | all-to-all | bytes 131072 | tf_op jit(solution)/shard_map/all_to_all | solution.py:652
  304.1 5.4 %all-to-all-start.3 = ((bf16[128,160,128]{2,1,0:T(8,128)(2,1)}), bf16[128,160,128]{2,1,0:T(8,128)(2,1)}, u32[]{:S(2)}, u32[]{:S(2)}) async-start(bf16[128,160,128]{2,1,0:T(8,128)(2,1)} %bitcast.75), calls=%async_computation.3 | async-start | bytes 10485760 | tf_op jit(solution)/shard_map/all_to_all | solution.py:554
  309.5 9.7 %convolution_convert_fusion.rows_ref = bf16[640,4096]{1,0:T(8,128)(2,1)} fusion(bf16[640,768]{1,0:T(8,128)(2,1)} %get-tuple-element.32, bf16[1,768,4096]{2,1,0:T(8,128)(2,1)} %param.28), kind=kOutput, calls=%fused_computation | convolution fusion | flops 4029153280 | bytes 12517376 | tf_op jit(solution)/shard_map/dot_general | solution.py:661
  319.1 7.7 %fold_rows.1 = bf16[640,32,128]{2,1,0:T(8,128)(2,1)} custom-call(bf16[640,4096]{1,0:T(8,128)(2,1)} %convolution_convert_fusion.rows_ref), custom_call_target="tpu_custom_call" | custom-call | bytes 10485760 | tf_op jit(solution)/shard_map/fold_rows/pallas_call | solution.py:161
  326.8 47.1 %all-to-all-done.3 = bf16[128,160,128]{2,1,0:T(8,128)(2,1)} async-done(((bf16[128,160,128]{2,1,0:T(8,128)(2,1)}), bf16[128,160,128]{2,1,0:T(8,128)(2,1)}, u32[]{:S(2)}, u32[]{:S(2)}) %all-to-all-start.3) | async-done | bytes 5242912 | tf_op jit(solution)/shard_map/all_to_all | solution.py:554
  373.9 7.3 %all-to-all-start.2 = ((bf16[128,160,128]{2,1,0:T(8,128)(2,1)}), bf16[128,160,128]{2,1,0:T(8,128)(2,1)}, u32[]{:S(2)}, u32[]{:S(2)}) async-start(bf16[128,160,128]{2,1,0:T(8,128)(2,1)} %bitcast.70), calls=%async_computation.2 | async-start | bytes 10485760 | tf_op jit(solution)/shard_map/all_to_all | solution.py:554
  385.2 5.6 %mix_rows.2 = f32[64,32,128]{2,1,0:T(8,128)} custom-call(s32[512]{0:T(512)} %reshape.193.index_ref, f32[512]{0:T(512)} %div.50.gate_ref, bf16[640,32,128]{2,1,0:T(8,128)(2,1)} %bitcast.16.rows_ref, f32[8,128]{1,0:T(8,128)} %slice.31.after_ref), custom_call_target="tpu_custom_call" | custom-call | flops 4194304 | bytes 5242880 | tf_op jit(solution)/shard_map/mix_rows/pallas_call | solution.py:114
  390.8 2.1 multiply_reduce_fusion
  392.9 2.5 subtract_add_fusion
  399.1 1.5 broadcast_select_fusion.1
  401.5 8.1 %attend_back.1 = (bf16[128,2048]{1,0:T(8,128)(2,1)}, bf16[128,128]{1,0:T(8,128)(2,1)}, bf16[128,128]{1,0:T(8,128)(2,1)}) custom-call(bf16[128,2048]{1,0:T(8,128)(2,1)} %fusion.13.grad_ref, f32[128,2048]{1,0:T(8,128)} %get-tuple-element.35.weight_ref, f32[128,2048]{1,0:T(8,128)} %get-tuple-element.36.raw_ref, bf16[128,128]{1,0:T(8,128)(2,1)} %pad_maximum_fusion.4.key_ref, ...), custom_call_target="tpu_custom_call" | custom-call | flops 402653184 | bytes 3145728 | tf_op jit(solution)/shard_map/attend_back/pallas_call | solution.py:339
  409.6 7.2 %project_back.3 = bf16[128,2048]{1,0:T(8,128)(2,1)} custom-call(s32[1]{0:T(128)} %bitcast.21.at_ref, bf16[128,2048]{1,0:T(8,128)(2,1)} %get-tuple-element.38.query_ref, bf16[128,128]{1,0:T(8,128)(2,1)} %get-tuple-element.39.key_ref, bf16[128,128]{1,0:T(8,128)(2,1)} %get-tuple-element.40.value_ref, ...), custom_call_target="tpu_custom_call" | custom-call | flops 1073741824 | bytes 8388608 | tf_op jit(solution)/shard_map/project_back/pallas_call | solution.py:373
  417.2 7.3 %project_back.2 = f32[128,2048]{1,0:T(8,128)} custom-call(s32[1]{0:T(128)} %bitcast.14.at_ref, bf16[128,2048]{1,0:T(8,128)(2,1)} %get-tuple-element.38.query_ref, bf16[128,128]{1,0:T(8,128)(2,1)} %get-tuple-element.39.key_ref, bf16[128,128]{1,0:T(8,128)(2,1)} %get-tuple-element.40.value_ref, ...), custom_call_target="tpu_custom_call" | custom-call | flops 1073741824 | bytes 8388608 | tf_op jit(solution)/shard_map/project_back/pallas_call | solution.py:373
  425.9 19.4 %all-to-all-done.2 = bf16[128,160,128]{2,1,0:T(8,128)(2,1)} async-done(((bf16[128,160,128]{2,1,0:T(8,128)(2,1)}), bf16[128,160,128]{2,1,0:T(8,128)(2,1)}, u32[]{:S(2)}, u32[]{:S(2)}) %all-to-all-start.2) | async-done | bytes 5242912 | tf_op jit(solution)/shard_map/all_to_all | solution.py:554
  445.3 5.7 %mix_rows.3 = f32[64,32,128]{2,1,0:T(8,128)} custom-call(s32[512]{0:T(512)} %reshape.193.index_ref, f32[512]{0:T(512)} %div.50.gate_ref, bf16[640,32,128]{2,1,0:T(8,128)(2,1)} %bitcast.13.rows_ref, f32[8,128]{1,0:T(8,128)} %slice.34.after_ref), custom_call_target="tpu_custom_call" | custom-call | flops 4194304 | bytes 5242880 | tf_op jit(solution)/shard_map/mix_rows/pallas_call | solution.py:114
  451.0 1.8 fusion.9
  454.2 2.7 fusion.11
  457.5 2.6 convert_multiply_fusion.2
  (112 shorter events, 29.1 us)
Async XLA Ops:
  7.2 374.0 %copy-start = (bf16[4096,128]{1,0:T(8,128)(2,1)S(1)}, bf16[4096,128]{1,0:T(8,128)(2,1)}, u32[]{:S(2)}) copy-start(bf16[4096,128]{1,0:T(8,128)(2,1)} %param.23) | copy-start | bytes 3145732
  7.2 12.0 %copy-start.24 = (s32[1,4]{1,0:T(1,128)S(1)}, s32[1,4]{1,0:T(1,128)}, u32[]{:S(2)}) copy-start(s32[1,4]{1,0:T(1,128)} %param.25) | copy-start | bytes 52
  7.2 110.7 %all-gather.2.cloned.1.call-start = ((), (), s32[]{:S(2)}) async-start(), calls=%async_computation.5 | async-start | bytes 17039360 | tf_op jit(solution)/shard_map/all_gather | solution.py:584
  8.9 2.9 copy-start.13
  14.3 11.6 %copy-start.20 = (f32[128]{0:T(128)S(1)}, f32[128]{0:T(128)}, u32[]{:S(2)}) copy-start(f32[128]{0:T(128)} %param.20) | copy-start | bytes 1540
  15.3 13.1 %copy-start.4 = (bf16[4096,128]{1,0:T(8,128)(2,1)S(1)}, bf16[4096,128]{1,0:T(8,128)(2,1)}, u32[]{:S(2)}) copy-start(bf16[4096,128]{1,0:T(8,128)(2,1)} %value_w.3) | copy-start | bytes 3145732
  16.9 12.5 %copy-start.2 = (bf16[128,4096]{1,0:T(8,128)(2,1)}, bf16[128,4096]{1,0:T(8,128)(2,1)S(1)}, u32[]{:S(2)}) copy-start(bf16[128,4096]{1,0:T(8,128)(2,1)S(1)} %fusion.5.normed_ref) | copy-start | bytes 3145732
  117.9 72.7 %all-to-all-start.1 = ((bf16[128,160,128]{2,1,0:T(8,128)(2,1)}), bf16[128,160,128]{2,1,0:T(8,128)(2,1)}, u32[]{:S(2)}, u32[]{:S(2)}) async-start(bf16[128,160,128]{2,1,0:T(8,128)(2,1)} %bitcast.71), calls=%async_computation.1 | async-start | bytes 10485760 | tf_op jit(solution)/shard_map/all_to_all | solution.py:554
  126.3 17.9 %copy-start.1 = (bf16[128,4096]{1,0:T(8,128)(2,1)S(1)}, bf16[128,4096]{1,0:T(8,128)(2,1)}, u32[]{:S(2)}) copy-start(bf16[128,4096]{1,0:T(8,128)(2,1)} %param.15) | copy-start | bytes 3145732
  126.4 18.7 %copy-start.12 = (f32[4096]{0:T(1024)S(1)}, f32[4096]{0:T(1024)}, u32[]{:S(2)}) copy-start(f32[4096]{0:T(1024)} %param.22) | copy-start | bytes 49156
  140.8 2.4 collective-permute-start
  144.3 46.3 %copy-start.5 = (bf16[64,2048]{1,0:T(8,128)(2,1)}, bf16[64,2048]{1,0:T(8,128)(2,1)S(1)}, u32[]{:S(2)}) copy-start(bf16[64,2048]{1,0:T(8,128)(2,1)S(1)} %get-tuple-element.50) | copy-start | bytes 786436
  145.1 45.5 %copy-start.16 = (f32[64]{0:T(128)}, f32[64]{0:T(128)S(1)}, u32[]{:S(2)}) copy-start(f32[64]{0:T(128)S(1)} %get-tuple-element.62) | copy-start | bytes 772
  190.6 71.6 %all-to-all-start = ((bf16[128,160,128]{2,1,0:T(8,128)(2,1)}), bf16[128,160,128]{2,1,0:T(8,128)(2,1)}, u32[]{:S(2)}, u32[]{:S(2)}) async-start(bf16[128,160,128]{2,1,0:T(8,128)(2,1)} %bitcast.72), calls=%async_computation | async-start | bytes 10485760 | tf_op jit(solution)/shard_map/all_to_all | solution.py:554
  304.1 69.8 %all-to-all-start.3 = ((bf16[128,160,128]{2,1,0:T(8,128)(2,1)}), bf16[128,160,128]{2,1,0:T(8,128)(2,1)}, u32[]{:S(2)}, u32[]{:S(2)}) async-start(bf16[128,160,128]{2,1,0:T(8,128)(2,1)} %bitcast.75), calls=%async_computation.3 | async-start | bytes 10485760 | tf_op jit(solution)/shard_map/all_to_all | solution.py:554
  373.9 7.3 %copy-start.11 = (bf16[64,4096]{1,0:T(8,128)(2,1)S(1)}, bf16[64,4096]{1,0:T(8,128)(2,1)}, u32[]{:S(2)}) copy-start(bf16[64,4096]{1,0:T(8,128)(2,1)} %multiply_convert_fusion.rows_ref) | copy-start | bytes 1572868
  373.9 7.7 %copy-start.14 = (pred[64,128]{1,0:T(8,128)(4,1)S(1)}, pred[64,128]{1,0:T(8,128)(4,1)}, u32[]{:S(2)}) copy-start(pred[64,128]{1,0:T(8,128)(4,1)} %copy-done.13) | copy-start | bytes 24580
  373.9 71.4 %all-to-all-start.2 = ((bf16[128,160,128]{2,1,0:T(8,128)(2,1)}), bf16[128,160,128]{2,1,0:T(8,128)(2,1)}, u32[]{:S(2)}, u32[]{:S(2)}) async-start(bf16[128,160,128]{2,1,0:T(8,128)(2,1)} %bitcast.70), calls=%async_computation.2 | async-start | bytes 10485760 | tf_op jit(solution)/shard_map/all_to_all | solution.py:554
  384.5 8.3 %copy-start.17 = (f32[64]{0:T(128)S(1)}, f32[64]{0:T(128)}, u32[]{:S(2)}) copy-start(f32[64]{0:T(128)} %copy-done.16) | copy-start | bytes 772
  384.6 8.3 %copy-start.23 = (f32[64]{0:T(128)S(1)}, f32[64]{0:T(128)}, u32[]{:S(2)}) copy-start(f32[64]{0:T(128)} %get-tuple-element.61) | copy-start | bytes 772
  395.3 1.0 copy-start.6
  396.3 2.7 collective-permute-start.1
  400.5 16.3 %copy-start.7 = (f32[64,2048]{1,0:T(8,128)}, f32[64,2048]{1,0:T(8,128)S(1)}, u32[]{:S(2)}) copy-start(f32[64,2048]{1,0:T(8,128)S(1)} %get-tuple-element.47) | copy-start | bytes 1572868
  400.5 16.3 %copy-start.9 = (f32[64,2048]{1,0:T(8,128)}, f32[64,2048]{1,0:T(8,128)S(1)}, u32[]{:S(2)}) copy-start(f32[64,2048]{1,0:T(8,128)S(1)} %get-tuple-element.48) | copy-start | bytes 1572868
  409.6 7.7 %copy-start.15 = (f32[4096]{0:T(1024)S(1)}, f32[4096]{0:T(1024)}, u32[]{:S(2)}) copy-start(f32[4096]{0:T(1024)} %param.21) | copy-start | bytes 49156
  416.8 34.2 %collective-permute-start.2 = (bf16[128,2048]{1,0:T(8,128)(2,1)}, bf16[128,2048]{1,0:T(8,128)(2,1)}, u32[]{:S(2)}, u32[]{:S(2)}) collective-permute-start(bf16[128,2048]{1,0:T(8,128)(2,1)} %project_back.3), channel_id=1, source_target_pairs={{0,1},{1,0},{2,3},{3,2},{4,5},{5,4},{6,7},{7,6},{8,9},{9,8},{10,11... | collective-permute-start | bytes 1572872 | tf_op jit(solution)/shard_map/ppermute | solution.py:548
  424.5 26.5 %copy-start.3 = (f32[128,2048]{1,0:T(8,128)S(1)}, f32[128,2048]{1,0:T(8,128)}, u32[]{:S(2)}) copy-start(f32[128,2048]{1,0:T(8,128)} %project_back.2) | copy-start | bytes 3145732
  445.3 11.6 %copy-start.19 = (f32[128]{0:T(128)S(1)}, f32[128]{0:T(128)}, u32[]{:S(2)}) copy-start(f32[128]{0:T(128)} %copy-done.18) | copy-start | bytes 1540
  445.3 12.2 %copy-start.22 = (f32[128]{0:T(128)S(1)}, f32[128]{0:T(128)}, u32[]{:S(2)}) copy-start(f32[128]{0:T(128)} %copy-done.21) | copy-start | bytes 1540
  451.0 6.4 %copy-start.8 = (f32[64,2048]{1,0:T(8,128)S(1)}, f32[64,2048]{1,0:T(8,128)}, u32[]{:S(2)}) copy-start(f32[64,2048]{1,0:T(8,128)} %copy-done.7) | copy-start | bytes 1572868
  451.0 6.4 %copy-start.10 = (f32[64,2048]{1,0:T(8,128)S(1)}, f32[64,2048]{1,0:T(8,128)}, u32[]{:S(2)}) copy-start(f32[64,2048]{1,0:T(8,128)} %copy-done.9) | copy-start | bytes 1572868
  452.9 4.0 collective-permute-start.3
  (2 other events, 1.0 us)
Sparse Core Ops, SparseCore 0:
  10.9 106.9 all-gather.1

commit v3 on v2

--- a/solution.py
+++ b/solution.py
@@ -53,6 +53,7 @@
 
 
 SUB = 32
+PART = 1024
 VMEM_LIMIT = 56 * 1024 * 1024
 
 
@@ -92,44 +93,90 @@
     )(index, rows)
 
 
-def mix_kernel(index_ref, gate_ref, rows_ref, after_ref, out_ref):
+def mix_block(id_ref, slot_ref, gate_ref, rows_ref, total):
+    tokens = total.shape[0]
+    top = id_ref.shape[0] // tokens
+
+    def one(i, carry):
+        at = i * top
+        row = gate_ref[at] * rows_ref[id_ref[at], slot_ref[at]].astype(jnp.float32)
+        for k in range(1, top):
+            own = rows_ref[id_ref[at + k], slot_ref[at + k]].astype(jnp.float32)
+            row = row + gate_ref[at + k] * own
+        total[i] = row
+        return carry
+
+    lax.fori_loop(0, tokens, one, 0, unroll=4)
+
+
+def mix_out_kernel(id_ref, slot_ref, gate_ref, rows_ref, base_ref, after_ref, out_ref, total):
     del after_ref
-    step_tokens = out_ref.shape[0]
-    top = index_ref.shape[0] // (step_tokens * pl.num_programs(0))
-    base = pl.program_id(0) * step_tokens
-
-    def one(i, carry):
-        at = (base + i) * top
-        total = gate_ref[at] * rows_ref[index_ref[at]].astype(jnp.float32)
-        for k in range(1, top):
-            total = total + gate_ref[at + k] * rows_ref[index_ref[at + k]].astype(jnp.float32)
-        out_ref[i] = total
-        return carry
-
-    lax.fori_loop(0, step_tokens, one, 0, unroll=2)
-
-
-def mix_rows(rows3, index, gates, tokens, after, step_tokens=16):
-    _, sub, lanes = rows3.shape
+    mix_block(id_ref, slot_ref, gate_ref, rows_ref, total)
+    mixed = base_ref[...] + total[...].reshape(out_ref.shape)
+    out_ref[...] = mixed.astype(out_ref.dtype)
+
+
+def mix_grad_kernel(id_ref, slot_ref, gate_ref, rows_ref, extra_ref, after_ref, out_ref, sum_ref, total):
+    del after_ref
+    mix_block(id_ref, slot_ref, gate_ref, rows_ref, total)
+    out_ref[...] = total[...].reshape(out_ref.shape)
+    tokens = total.shape[0]
+    top = id_ref.shape[0] // tokens
+
+    @pl.when(pl.program_id(0) == 0)
+    def _():
+        line = lax.broadcasted_iota(jnp.int32, extra_ref.shape[2:], 0)
+
+        def one(i, carry):
+            tile = jnp.zeros(extra_ref.shape[2:], jnp.float32)
+            for k in range(top):
+                at = i * top + k
+                own = gate_ref[at] * extra_ref[id_ref[at], 0].astype(jnp.float32)
+                tile = tile + jnp.where(line == slot_ref[at], own, 0.0)
+            sum_ref[pl.ds(i, 1), :] = jnp.sum(tile, axis=0, keepdims=True)
+            return carry
+
+        lax.fori_loop(0, tokens, one, 0, unroll=2)
+
+
+def mix_rows(back4, ids, places, gates, base, after, capacity):
+    blocks, _, sub, lanes = back4.shape
+    top_tokens = ids.shape[0]
+    tokens = after.shape[0]
+    part = sub * lanes
+    steps = SUB // sub
+    rows_spec = pl.BlockSpec((blocks, capacity, sub, lanes), lambda k, *_: (0, k, 0, 0))
+    wide = pl.BlockSpec((tokens, part), lambda k, *_: (0, k))
+    flat = pl.BlockSpec((tokens, lanes), lambda k, *_: (0, 0))
+    if base is None:
+        extra = pl.BlockSpec((blocks, 1, sub, lanes), lambda k, *_: (0, steps * capacity, 0, 0))
+        kernel, specs, operands = mix_grad_kernel, [rows_spec, extra, flat], (back4, back4, after)
+        out_shape = (
+            jax.ShapeDtypeStruct((tokens, steps * part), jnp.float32),
+            jax.ShapeDtypeStruct((tokens, lanes), jnp.float32),
+        )
+        out_specs = (wide, flat)
+    else:
+        kernel, specs, operands = mix_out_kernel, [rows_spec, wide, flat], (back4, base, after)
+        out_shape = jax.ShapeDtypeStruct((tokens, steps * part), jnp.bfloat16)
+        out_specs = wide
     return pl.pallas_call(
-        mix_kernel,
-        out_shape=jax.ShapeDtypeStruct((tokens, sub, lanes), jnp.float32),
+        kernel,
+        out_shape=out_shape,
         grid_spec=pltpu.PrefetchScalarGridSpec(
-            num_scalar_prefetch=2,
-            grid=(tokens // step_tokens,),
-            in_specs=[
-                pl.BlockSpec(rows3.shape, lambda i, ids, g: (0, 0, 0)),
-                pl.BlockSpec(after.shape, lambda i, ids, g: (0, 0)),
-            ],
-            out_specs=pl.BlockSpec((step_tokens, sub, lanes), lambda i, ids, g: (i, 0, 0)),
+            num_scalar_prefetch=3,
+            grid=(steps,),
+            in_specs=specs,
+            out_specs=out_specs,
+            scratch_shapes=[pltpu.VMEM((tokens, sub, lanes), jnp.float32)],
         ),
         cost_estimate=pl.CostEstimate(
-            flops=index.shape[0] * sub * lanes * 2,
+            flops=top_tokens * steps * part * 2,
             transcendentals=0,
-            bytes_accessed=rows3.shape[0] * sub * lanes * 2,
+            bytes_accessed=blocks * capacity * steps * part * 2,
         ),
         name="mix_rows",
-    )(index, gates, rows3, after)
+    )(ids, places, gates, *operands)
 
 
 def spread_kernel(rows_ref, out_ref):
@@ -152,18 +199,25 @@
 
 
 def fold_kernel(rows_ref, out_ref):
-    out_ref[...] = rows_ref[...].reshape(out_ref.shape)
-
-
-def fold_rows(rows, step_rows=128):
+    blocks, places, sub, lanes = out_ref.shape
+    part = sub * lanes
+    parts = rows_ref.shape[1] // part
+    per = places // parts
+    for k in range(parts):
+        rows = rows_ref[:, k * part : (k + 1) * part]
+        out_ref[:, k * per : (k + 1) * per] = rows.reshape(blocks, per, sub, lanes)
+
+
+def fold_rows(rows, capacity, step_blocks=32):
     count, width = rows.shape
-    lanes = width // SUB
+    blocks = count // capacity
+    places = capacity * width // PART
     return pl.pallas_call(
         fold_kernel,
-        out_shape=jax.ShapeDtypeStruct((count, SUB, lanes), jnp.bfloat16),
-        grid=(count // step_rows,),
-        in_specs=[pl.BlockSpec((step_rows, width), lambda i: (i, 0))],
-        out_specs=pl.BlockSpec((step_rows, SUB, lanes), lambda i: (i, 0, 0)),
+        out_shape=jax.ShapeDtypeStruct((blocks, places, 8, PART // 8), jnp.bfloat16),
+        grid=(blocks // step_blocks,),
+        in_specs=[pl.BlockSpec((step_blocks * capacity, width), lambda i: (i, 0))],
+        out_specs=pl.BlockSpec((step_blocks, places, 8, PART // 8), lambda i: (i, 0, 0, 0)),
         cost_estimate=pl.CostEstimate(
             flops=0, transcendentals=0, bytes_accessed=4 * count * width
         ),
@@ -400,10 +454,12 @@
     gate_hbm,
     up_hbm,
     cot_hbm,
+    router_ref,
     grad_hbm,
     hidden_ref,
-    slot_ref,
     rows_v,
+    made_v,
+    slot_v,
     gate_w,
     up_w,
     cot_ref,
@@ -428,9 +484,12 @@
         at = pl.ds(k * piece, piece)
         return pltpu.make_async_copy(rows_hbm.at[:, at, :], rows_v.at[:, at, :], sem_in.at[k])
 
+    blocks, places = made_v.shape[:2]
+    per = count // blocks
+
     def leave(k):
-        at = pl.ds(k * piece, piece)
-        return pltpu.make_async_copy(rows_v.at[:, at, :], grad_hbm.at[:, at, :], sem_out.at[k])
+        at = pl.ds(k * per, per if k < chunks else places - chunks * per)
+        return pltpu.make_async_copy(made_v.at[:, at], grad_hbm.at[:, at], sem_out.at[k])
 
     def gate_in(k):
         at = pl.ds(k * part, part)
@@ -462,7 +521,6 @@
             pre_up[...] += up
 
     cot_in.wait()
-    slot_count = slot_ref.shape[0]
 
     def between(r, carry):
         at = pl.ds(pl.multiple_of(r * row_block, 16), row_block)
@@ -476,51 +534,55 @@
             jnp.bfloat16
         )
         slot = jnp.sum(hidden.astype(jnp.float32) * cot, axis=1, keepdims=True)
-        row = lax.broadcasted_iota(jnp.int32, (row_block, 128), 0) + r * row_block
-        block = jnp.floor((row.astype(jnp.float32) + 0.5) * (slot_count / count))
-        block = block.astype(jnp.int32)
-        lane = lax.broadcasted_iota(jnp.int32, (row_block, 128), 1)
-        per = count // slot_count
-        spread = jnp.where(row - block * per == lane, slot, 0.0)
-        select = jnp.where(block == lane, 1.0, 0.0).astype(jnp.bfloat16)
-        for _ in range(3):
-            rounded = spread.astype(jnp.bfloat16)
-            slot_ref[...] += lax.dot_general(
-                select, rounded, TN, preferred_element_type=jnp.float32
-            )
-            spread = spread - rounded.astype(jnp.float32)
+        slot_v[at, :] = jnp.broadcast_to(slot, (row_block, slot_v.shape[1]))
         return carry
-
-    slot_ref[...] = jnp.zeros_like(slot_ref)
 
     lax.fori_loop(0, count // row_block, between, 0)
     for k in range(chunks):
         at = slice(k * part, (k + 1) * part)
         grad = lax.dot_general(grad_gate[...], gate_w[at, :], NT, preferred_element_type=jnp.float32)
         grad += lax.dot_general(grad_up[...], up_w[at, :], NT, preferred_element_type=jnp.float32)
-        rows_v[:, k * piece : (k + 1) * piece, :] = grad.astype(jnp.bfloat16).reshape(
-            count, piece, lanes
+        grad += slot_v[:, :1] * router_ref[:, at]
+        made_v[:, k * per : (k + 1) * per] = grad.astype(jnp.bfloat16).reshape(
+            blocks, per, piece, lanes
         )
         leave(k).start()
-    for k in range(chunks):
+    slot = slot_v[...]
+    upper = slot.astype(jnp.bfloat16)
+    lower = (slot - upper.astype(jnp.float32)).astype(jnp.bfloat16)
+    lane = lax.broadcasted_iota(jnp.int32, slot.shape, 1)
+    value = jnp.where(lane < lanes // 2, upper.astype(jnp.float32), lower.astype(jnp.float32))
+    value = value.astype(jnp.bfloat16)
+    group = 16
+    column = lax.broadcasted_iota(jnp.int32, (group * 8, count), 1)
+    line = lax.broadcasted_iota(jnp.int32, (group * 8, count), 0)
+    for b in range(0, blocks, group):
+        block, place = lax.shift_right_logical(line, 3) + b, line & 7
+        select = jnp.where((block * per + place == column) & (place < per), 1.0, 0.0)
+        extra = jnp.dot(select.astype(jnp.bfloat16), value, preferred_element_type=jnp.float32)
+        made_v[b : b + group, chunks * per] = extra.astype(jnp.bfloat16).reshape(group, 8, lanes)
+    leave(chunks).start()
+    for k in range(chunks + 1):
         leave(k).wait()
 
 
-def expert(rows3, gate_w, up_w, cot_hidden, slot_count, chunks=4, row_block=80):
-    count = rows3.shape[0]
+def expert(rows3, gate_w, up_w, cot_hidden, router_row, blocks, chunks=4, row_block=80):
+    count, sub, lanes = rows3.shape
+    made = (blocks, chunks * count // blocks + 1, sub // chunks, lanes)
     inner = gate_w.shape[1]
     hbm = pl.BlockSpec(memory_space=pltpu.HBM)
     return pl.pallas_call(
         functools.partial(expert_kernel, chunks=chunks, row_block=row_block),
         out_shape=(
-            jax.ShapeDtypeStruct(rows3.shape, jnp.bfloat16),
+            jax.ShapeDtypeStruct(made, jnp.bfloat16),
             jax.ShapeDtypeStruct((count, inner), jnp.bfloat16),
-            jax.ShapeDtypeStruct((slot_count, 128), jnp.float32),
-        ),
-        in_specs=[hbm, hbm, hbm, hbm],
-        out_specs=(hbm, VM, VM),
+        ),
+        in_specs=[hbm, hbm, hbm, hbm, VM],
+        out_specs=(hbm, VM),
         scratch_shapes=[
             pltpu.VMEM(rows3.shape, jnp.bfloat16),
+            pltpu.VMEM(made, jnp.bfloat16),
+            pltpu.VMEM((count, lanes), jnp.float32),
             pltpu.VMEM(gate_w.shape, jnp.bfloat16),
             pltpu.VMEM(up_w.shape, jnp.bfloat16),
             pltpu.VMEM((count, inner), jnp.float32),
@@ -532,7 +594,7 @@
             pltpu.SemaphoreType.DMA((chunks,)),
             pltpu.SemaphoreType.DMA((chunks,)),
             pltpu.SemaphoreType.DMA,
-            pltpu.SemaphoreType.DMA((chunks,)),
+            pltpu.SemaphoreType.DMA((chunks + 1,)),
         ],
         compiler_params=pltpu.CompilerParams(vmem_limit_bytes=VMEM_LIMIT),
         cost_estimate=pl.CostEstimate(
@@ -541,18 +603,17 @@
             bytes_accessed=4 * rows3.shape[0] * gate_w.shape[0],
         ),
         name="expert",
-    )(rows3, gate_w, up_w, cot_hidden)
+    )(rows3, gate_w, up_w, cot_hidden, router_row)
 
 
 def swap_heads(values):
     return lax.ppermute(values, "head", [(0, 1), (1, 0)])
 
 
-def exchange(rows3, device_count):
-    count, sub, lanes = rows3.shape
-    packed = rows3.reshape(device_count, (count // device_count) * sub, lanes)
+def exchange(rows, device_count):
+    packed = rows.reshape(device_count, -1, 128)
     moved = lax.all_to_all(packed, ("req", "head"), split_axis=0, concat_axis=0, tiled=True)
-    return moved.reshape(count, sub, lanes)
+    return moved.reshape(rows.shape)
 
 
 def device_step(
@@ -591,7 +652,9 @@
     rank = jnp.dot(before, member.astype(jnp.bfloat16), preferred_element_type=jnp.float32)
     rank = rank.astype(jnp.int32)
     slot_of = jnp.sum(jnp.where(chosen_mask, rank[:, None, :], 0), axis=2)
-    target = (expert_ids * capacity + slot_of).reshape(-1)
+    flat_ids, flat_slots = expert_ids.reshape(-1), slot_of.reshape(-1)
+    device_index = lax.axis_index("req") * head_count + head_index
+    router_row = lax.dynamic_slice_in_dim(router, device_index, 1, 1).astype(jnp.float32).T
     slot_range = jnp.arange(capacity, dtype=jnp.int32)
     hit = member[:, :, None] & (rank[:, :, None] == slot_range[None, None, :])
     source = jnp.sum(jnp.where(hit, token_range[:, None, None], 0), axis=0).reshape(-1)
@@ -616,9 +679,10 @@
     sines = jnp.concatenate([-sine_table, sine_table], axis=1)
     query_gain2, key_gain2 = query_gain[None, :], key_gain[None, :]
     prep = (cot_send, query_w, normed, key_raw, key_rows, value_rows, cosines, sines, mask)
-    prep = (*prep, target)
+    prep = (*prep, flat_ids, flat_slots, router_row)
     prep = lax.optimization_barrier(prep)
-    cot_send, query_w, normed, key_raw, key_rows, value_rows, cosines, sines, mask, target = prep
+    cot_send, query_w, normed, key_raw, key_rows, value_rows, cosines, sines, mask = prep[:9]
+    flat_ids, flat_slots, router_row = prep[9:]
     cot_rows3 = exchange(cot_send, device_count)
     context, query_raw, attn_weights = attend(
         normed, query_w, key_rows, value_rows, cosines, sines, query_gain2, mask
@@ -640,6 +704,11 @@
     chosen = jnp.sum(jnp.where(chosen_mask, logits[:, None, :], 0.0), axis=2)
     gates = jax.nn.softmax(chosen, axis=1)
     flat_gates = gates.reshape(-1)
+    dense = jnp.sum(jnp.where(chosen_mask, gates[:, :, None], 0.0), axis=1)
+    router_part = jnp.dot(
+        dense, router.astype(jnp.float32).T, precision=lax.Precision.HIGHEST
+    )
+    router_part = lax.optimization_barrier(router_part)
     cot32 = cotangent.astype(jnp.float32)
 
     gate_w = w_gate[0]
@@ -648,32 +717,17 @@
     cot_rows = spread_rows(cot_rows3)
     cot_hidden = jnp.dot(cot_rows, down_w.T, preferred_element_type=jnp.float32)
     cot_hidden = lax.optimization_barrier(cot_hidden)
-    grad_send, hidden, slot_grad = expert(rows3, gate_w, up_w, cot_hidden, device_count)
-    slot_back = lax.all_to_all(
-        slot_grad.reshape(device_count, 1, 128),
-        ("req", "head"),
-        split_axis=0,
-        concat_axis=0,
-        tiled=True,
-    )
-    slot_back = slot_back.reshape(device_count, 128)[:, :capacity]
+    grad_send, hidden = expert(rows3, gate_w, up_w, cot_hidden, router_row, device_count)
     grad_back = exchange(grad_send, device_count)
     outputs = jnp.dot(hidden, down_w, preferred_element_type=jnp.float32).astype(jnp.bfloat16)
-    out_send = fold_rows(outputs)
+    out_send = fold_rows(outputs, capacity)
     out_back = exchange(out_send, device_count)
 
-    hit_grad = jnp.sum(jnp.where(hit, slot_back[None, :, :], 0.0), axis=2)
-    gate_grad = jnp.sum(jnp.where(chosen_mask, hit_grad[:, None, :], 0.0), axis=2)
-    total_gate = jnp.sum(gates * gate_grad, axis=1, keepdims=True)
-    grad_logit = gates * (gate_grad - total_gate)
-    dense = jnp.sum(jnp.where(chosen_mask, grad_logit[:, :, None], 0.0), axis=1)
-    router_part = jnp.dot(
-        dense, router.astype(jnp.float32).T, precision=lax.Precision.HIGHEST
-    )
-    router_part = lax.optimization_barrier(router_part)
-    grad_in = mix_rows(grad_back, target, flat_gates, moe_tokens, router_part[:8, :128])
-    grad_in = grad_in.reshape(moe_tokens, width)
-    grad_in = grad_in + router_part
+    grad_sum, slot_sum = mix_rows(
+        grad_back, flat_ids, flat_slots, flat_gates, None, router_part[:, :128], capacity
+    )
+    total_gate = slot_sum[:, :1] + slot_sum[:, 64:65]
+    grad_in = grad_sum - total_gate * router_part
     grad_resid = cot32 + norm_backward(residual, moe_scale, moe_gain, grad_in)
     left, right = grad_resid[:, :half_width], grad_resid[:, half_width:]
     came_grad = swap_heads(jnp.where(first_core, right, left))
@@ -715,8 +769,9 @@
     token_score = direct_sum + (
         scale_row * inner_sum - scale_row**3 * (inner_sum / width) * square_sum
     )
-    moe_sum = mix_rows(out_back, target, flat_gates, moe_tokens, own_half[:8, :128]).reshape(moe_tokens, width)
-    mixed = (residual + moe_sum).astype(jnp.bfloat16)
+    mixed = mix_rows(
+        out_back, flat_ids, flat_slots, flat_gates, residual, own_half[:moe_tokens, :128], capacity
+    )
     return (mixed, attribution, token_score)
 
 

time: 474 us -> 462 us (0.975)
  blocking collectives: 16.1 us -> 0 us
  Pallas kernels: 101 us -> 110 us
  waiting for transfers between devices: 243 us -> 237 us
    all_to_all x1 -> x0, blocking collectives: 16.1 us -> none  [device_step(): lax.all_to_all(slot_grad.reshape(device_count, 1, 128), ('req', 'head'),...]
    pallas_call x3, Pallas kernels: 19 us -> 25.4 us  [the longest x2 17.5 us: mix_rows(): pl.pallas_call(kernel, out_shape=out_shape, grid_spec=pltpu.PrefetchScala...]
  transfers between devices with their start and end apart: 9 -> 9, of which waited for: 7 -> 7; matrix products, arithmetic and copies ran while one was open for 11% -> 12% of each run, Pallas kernels for 16% -> 18%
where the time goes in v3:
time: 462 us; the launch traced here: 455 us
  waiting for transfers between devices  237 us (51%)
  Pallas kernels  110 us (24%)
  starting transfers between devices  33.5 us (7%)
  matrix products  26.7 us (6%)
  other arithmetic  24.3 us (5%)
  between operations  14.6 us (3%)
  local copies, waits for them, and re-layouts  8.48 us (2%)
    all_to_all x4, waiting for transfers between devices, exchange(): lax.all_to_all(packed, ('req', 'head'), split_axis=0, concat_axis=0, tile...  147 us
    all_gather x1, waiting for transfers between devices, device_step(): query_w = lax.all_gather(q_proj, 'req', axis=0, tiled=True)  87.6 us
    all_to_all x4, starting transfers between devices, exchange(): lax.all_to_all(packed, ('req', 'head'), split_axis=0, concat_axis=0, tile...  30.4 us
    pallas_call x1, Pallas kernels, expert(): pl.pallas_call(functools.partial(expert_kernel, chunks=chunks, row_block=...  28.3 us
    pallas_call x2, Pallas kernels, mix_rows(): pl.pallas_call(kernel, out_shape=out_shape, grid_spec=pltpu.PrefetchScala...  17.5 us
    pallas_call x2, Pallas kernels, project_back(): pl.pallas_call(project_kernel, out_shape=jax.ShapeDtypeStruct((tokens, wi...  14.5 us
    pallas_call x1, Pallas kernels, attend(): pl.pallas_call(attend_kernel, out_shape=(jax.ShapeDtypeStruct((tokens, co...  13.5 us
    pallas_call x2, Pallas kernels, pick_rows(): pl.pallas_call(pick_kernel, out_shape=jax.ShapeDtypeStruct((count, SUB, l...  12.5 us
  transfers between devices with their start and end apart: 9, of which 7 were waited for; matrix products, arithmetic and copies ran while one was open for 12% of the time, Pallas kernels for 18%

profile of v3, /device:TPU:1, one launch (start us, length us, event | category | flops | bytes accessed | tf_op | source)
XLA Modules:
  0.0 454.6 jit_solution(6027329811118028600)
XLA Ops:
  13.4 1.5 fusion.3
  14.9 1.6 fusion.5.normed_ref
  16.6 2.2 multiply_reduce_fusion.2
  18.9 6.2 %pick_rows.2 = bf16[640,32,128]{2,1,0:T(8,128)(2,1)} custom-call(s32[640]{0:T(1024)} %reshape.160.index_ref, bf16[64,4096]{1,0:T(8,128)(2,1)} %rows_ref.1), custom_call_target="tpu_custom_call" | custom-call | bytes 5242880 | tf_op jit(solution)/shard_map/pick_rows/pallas_call | solution.py:79
  30.2 87.6 %all-gather.2.cloned.1.call-done.query_w_ref.query_w = bf16[4096,2048]{1,0:T(8,128)(2,1)} async-done(((bf16[64,2048]{1,0:T(8,128)(2,1)}), bf16[4096,2048]{1,0:T(8,128)(2,1)}) %all-gather.2.cloned.1.call-update) | async-done | bytes 16777232 | tf_op jit(solution)/shard_map/all_gather | solution.py:645
  117.9 8.4 %all-to-all-start.1 = ((bf16[128,160,128]{2,1,0:T(8,128)(2,1)}), bf16[128,160,128]{2,1,0:T(8,128)(2,1)}, u32[]{:S(2)}, u32[]{:S(2)}) async-start(bf16[128,160,128]{2,1,0:T(8,128)(2,1)} %bitcast.53), calls=%async_computation.1 | async-start | bytes 10485760 | tf_op jit(solution)/shard_map/all_to_all | solution.py:615
  126.3 13.5 %attend.1 = (bf16[128,2048]{1,0:T(8,128)(2,1)}, f32[128,2048]{1,0:T(8,128)}, f32[128,2048]{1,0:T(8,128)}) custom-call(bf16[128,4096]{1,0:T(8,128)(2,1)} %copy-done.1, bf16[4096,2048]{1,0:T(8,128)(2,1)} %all-gather.2.cloned.1.call-done.query_w_ref.query_w, bf16[128,128]{1,0:T(8,128)(2,1)} %pad_maximum_fusion.3.key_ref, ...), custom_call_target="tpu_custom_call" | custom-call | flops 2147483648 | bytes 16777216 | tf_op jit(solution)/shard_map/attend/pallas_call | solution.py:291
  145.7 6.3 %pick_rows.3 = bf16[640,32,128]{2,1,0:T(8,128)(2,1)} custom-call(s32[640]{0:T(1024)} %reshape.160.index_ref, bf16[64,4096]{1,0:T(8,128)(2,1)} %multiply_convert_fusion.rows_ref), custom_call_target="tpu_custom_call" | custom-call | bytes 5242880 | tf_op jit(solution)/shard_map/pick_rows/pallas_call | solution.py:79
  151.9 38.6 %all-to-all-done.1 = bf16[128,160,128]{2,1,0:T(8,128)(2,1)} async-done(((bf16[128,160,128]{2,1,0:T(8,128)(2,1)}), bf16[128,160,128]{2,1,0:T(8,128)(2,1)}, u32[]{:S(2)}, u32[]{:S(2)}) %all-to-all-start.1) | async-done | bytes 5242912 | tf_op jit(solution)/shard_map/all_to_all | solution.py:615
  190.5 7.5 %all-to-all-start = ((bf16[128,160,128]{2,1,0:T(8,128)(2,1)}), bf16[128,160,128]{2,1,0:T(8,128)(2,1)}, u32[]{:S(2)}, u32[]{:S(2)}) async-start(bf16[128,160,128]{2,1,0:T(8,128)(2,1)} %bitcast.54), calls=%async_computation | async-start | bytes 10485760 | tf_op jit(solution)/shard_map/all_to_all | solution.py:615
  198.0 7.3 %spread_rows.1 = bf16[640,4096]{1,0:T(8,128)(2,1)} custom-call(bf16[640,32,128]{2,1,0:T(8,128)(2,1)} %bitcast.10.rows_ref), custom_call_target="tpu_custom_call" | custom-call | bytes 10485760 | tf_op jit(solution)/shard_map/spread_rows/pallas_call | solution.py:188
  205.3 10.0 %fusion.1.cot_hbm = f32[640,768]{1,0:T(8,128)} fusion(bf16[640,4096]{1,0:T(8,128)(2,1)} %spread_rows.1, bf16[1,768,4096]{2,1,0:T(8,128)(2,1)} %param.28), kind=kOutput, calls=%fused_computation.2 | convolution fusion | flops 4026531840 | bytes 13500416 | tf_op jit(solution)/shard_map/dot_general | solution.py:718
  215.3 46.9 %all-to-all-done = bf16[128,160,128]{2,1,0:T(8,128)(2,1)} async-done(((bf16[128,160,128]{2,1,0:T(8,128)(2,1)}), bf16[128,160,128]{2,1,0:T(8,128)(2,1)}, u32[]{:S(2)}, u32[]{:S(2)}) %all-to-all-start) | async-done | bytes 5242912 | tf_op jit(solution)/shard_map/all_to_all | solution.py:615
  262.1 28.3 %expert.1 = (bf16[128,21,8,128]{3,2,1,0:T(8,128)(2,1)}, bf16[640,768]{1,0:T(8,128)(2,1)}) custom-call(bf16[640,32,128]{2,1,0:T(8,128)(2,1)} %bitcast.6.rows_hbm, bf16[4096,768]{1,0:T(8,128)(2,1)} %bitcast.64, bf16[4096,768]{1,0:T(8,128)(2,1)} %bitcast.65, f32[640,768]{1,0:T(8,128)} %fusion.1.cot_hbm, f32[1,4096]{1,0:T(1,128)} %bitcast.56), custom_call_target="tpu_custom_call" | custom-call | flops 16106127360 | bytes 10485760 | tf_op jit(solution)/shard_map/expert/pallas_call | solution.py:574
  290.5 7.4 %all-to-all-start.3 = ((bf16[128,168,128]{2,1,0:T(8,128)(2,1)}), bf16[128,168,128]{2,1,0:T(8,128)(2,1)}, u32[]{:S(2)}, u32[]{:S(2)}) async-start(bf16[128,168,128]{2,1,0:T(8,128)(2,1)} %bitcast.55), calls=%async_computation.3 | async-start | bytes 11010048 | tf_op jit(solution)/shard_map/all_to_all | solution.py:615
  297.8 1.4 fusion.28
  299.2 9.7 %convolution_convert_fusion.rows_ref = bf16[640,4096]{1,0:T(8,128)(2,1)} fusion(bf16[640,768]{1,0:T(8,128)(2,1)} %get-tuple-element.37, bf16[1,768,4096]{2,1,0:T(8,128)(2,1)} %param.28), kind=kOutput, calls=%fused_computation | convolution fusion | flops 4029153280 | bytes 12517376 | tf_op jit(solution)/shard_map/dot_general | solution.py:722
  308.8 8.0 %fold_rows.1 = bf16[128,20,8,128]{3,2,1,0:T(8,128)(2,1)} custom-call(bf16[640,4096]{1,0:T(8,128)(2,1)} %convolution_convert_fusion.rows_ref), custom_call_target="tpu_custom_call" | custom-call | bytes 10485760 | tf_op jit(solution)/shard_map/fold_rows/pallas_call | solution.py:215
  316.8 48.0 %all-to-all-done.3 = bf16[128,168,128]{2,1,0:T(8,128)(2,1)} async-done(((bf16[128,168,128]{2,1,0:T(8,128)(2,1)}), bf16[128,168,128]{2,1,0:T(8,128)(2,1)}, u32[]{:S(2)}, u32[]{:S(2)}) %all-to-all-start.3) | async-done | bytes 5505056 | tf_op jit(solution)/shard_map/all_to_all | solution.py:615
  364.8 7.2 %all-to-all-start.2 = ((bf16[128,160,128]{2,1,0:T(8,128)(2,1)}), bf16[128,160,128]{2,1,0:T(8,128)(2,1)}, u32[]{:S(2)}, u32[]{:S(2)}) async-start(bf16[128,160,128]{2,1,0:T(8,128)(2,1)} %bitcast.52), calls=%async_computation.2 | async-start | bytes 10485760 | tf_op jit(solution)/shard_map/all_to_all | solution.py:615
  373.5 2.4 fusion.29
  376.6 9.4 %mix_rows.2 = (f32[64,4096]{1,0:T(8,128)}, f32[64,128]{1,0:T(8,128)}) custom-call(s32[512]{0:T(512)} %reshape.163.id_ref, s32[512]{0:T(512)} %reshape.164.slot_ref, f32[512]{0:T(512)} %div.50.gate_ref, bf16[128,21,8,128]{3,2,1,0:T(8,128)(2,1)} %bitcast.16.rows_ref.extra_ref, bf16[128,21,8,128]{3,2,1,0:T(8,128)(2,1)} %bitcast.16.rows_ref.extra_ref, ...), custom_call_target="tpu_custom_call" | custom-call | flops 4194304 | bytes 5242880 | tf_op jit(solution)/shard_map/mix_rows/pallas_call | solution.py:163
  386.9 1.6 multiply_reduce_fusion
  388.5 1.8 subtract_add_fusion
  396.3 8.1 %attend_back.1 = (bf16[128,2048]{1,0:T(8,128)(2,1)}, bf16[128,128]{1,0:T(8,128)(2,1)}, bf16[128,128]{1,0:T(8,128)(2,1)}) custom-call(bf16[128,2048]{1,0:T(8,128)(2,1)} %fusion.11.grad_ref, f32[128,2048]{1,0:T(8,128)} %get-tuple-element.41.weight_ref, f32[128,2048]{1,0:T(8,128)} %get-tuple-element.42.raw_ref, bf16[128,128]{1,0:T(8,128)(2,1)} %pad_maximum_fusion.3.key_ref, ...), custom_call_target="tpu_custom_call" | custom-call | flops 402653184 | bytes 3145728 | tf_op jit(solution)/shard_map/attend_back/pallas_call | solution.py:393
  404.4 7.2 %project_back.3 = bf16[128,2048]{1,0:T(8,128)(2,1)} custom-call(s32[1]{0:T(128)} %bitcast.18.at_ref, bf16[128,2048]{1,0:T(8,128)(2,1)} %get-tuple-element.44.query_ref, bf16[128,128]{1,0:T(8,128)(2,1)} %get-tuple-element.45.key_ref, bf16[128,128]{1,0:T(8,128)(2,1)} %get-tuple-element.46.value_ref, ...), custom_call_target="tpu_custom_call" | custom-call | flops 1073741824 | bytes 8388608 | tf_op jit(solution)/shard_map/project_back/pallas_call | solution.py:427
  412.0 7.3 %project_back.2 = f32[128,2048]{1,0:T(8,128)} custom-call(s32[1]{0:T(128)} %bitcast.14.at_ref, bf16[128,2048]{1,0:T(8,128)(2,1)} %get-tuple-element.44.query_ref, bf16[128,128]{1,0:T(8,128)(2,1)} %get-tuple-element.45.key_ref, bf16[128,128]{1,0:T(8,128)(2,1)} %get-tuple-element.46.value_ref, ...), custom_call_target="tpu_custom_call" | custom-call | flops 1073741824 | bytes 8388608 | tf_op jit(solution)/shard_map/project_back/pallas_call | solution.py:427
  419.3 1.8 fusion.9
  421.3 1.4 slice.37.after_ref
  422.7 13.6 %all-to-all-done.2 = bf16[128,160,128]{2,1,0:T(8,128)(2,1)} async-done(((bf16[128,160,128]{2,1,0:T(8,128)(2,1)}), bf16[128,160,128]{2,1,0:T(8,128)(2,1)}, u32[]{:S(2)}, u32[]{:S(2)}) %all-to-all-start.2) | async-done | bytes 5242912 | tf_op jit(solution)/shard_map/all_to_all | solution.py:615
  436.2 8.1 %mix_rows.3 = bf16[64,4096]{1,0:T(8,128)(2,1)} custom-call(s32[512]{0:T(512)} %reshape.163.id_ref, s32[512]{0:T(512)} %reshape.164.slot_ref, f32[512]{0:T(512)} %div.50.gate_ref, bf16[128,20,8,128]{3,2,1,0:T(8,128)(2,1)} %bitcast.13.rows_ref, f32[64,4096]{1,0:T(8,128)} %copy-done, f32[64,128]{1,0:T(8,128)} %slice.37.after_ref), custom_call_target="tpu_custom_call" | custom-call | flops 4194304 | bytes 5242880 | tf_op jit(solution)/shard_map/mix_rows/pallas_call | solution.py:163
  444.9 2.6 convert_multiply_fusion.2
  (79 shorter events, 27.4 us)
Async XLA Ops:
  7.2 110.7 %all-gather.2.cloned.1.call-start = ((), (), s32[]{:S(2)}) async-start(), calls=%async_computation.4 | async-start | bytes 17039360 | tf_op jit(solution)/shard_map/all_gather | solution.py:645
  14.9 10.2 %copy-start.5 = (bf16[4096,128]{1,0:T(8,128)(2,1)S(1)}, bf16[4096,128]{1,0:T(8,128)(2,1)}, u32[]{:S(2)}) copy-start(bf16[4096,128]{1,0:T(8,128)(2,1)} %param.23) | copy-start | bytes 3145732
  14.9 11.6 %copy-start.10 = (s32[1,4]{1,0:T(1,128)S(1)}, s32[1,4]{1,0:T(1,128)}, u32[]{:S(2)}) copy-start(s32[1,4]{1,0:T(1,128)} %param.25) | copy-start | bytes 52
  14.9 11.7 %copy-start.9 = (f32[128]{0:T(128)S(1)}, f32[128]{0:T(128)}, u32[]{:S(2)}) copy-start(f32[128]{0:T(128)} %param.20) | copy-start | bytes 1540
  16.6 13.7 %copy-start.1 = (bf16[128,4096]{1,0:T(8,128)(2,1)}, bf16[128,4096]{1,0:T(8,128)(2,1)S(1)}, u32[]{:S(2)}) copy-start(bf16[128,4096]{1,0:T(8,128)(2,1)S(1)} %fusion.5.normed_ref) | copy-start | bytes 3145732
  16.6 12.6 %copy-start.4 = (bf16[4096,128]{1,0:T(8,128)(2,1)S(1)}, bf16[4096,128]{1,0:T(8,128)(2,1)}, u32[]{:S(2)}) copy-start(bf16[4096,128]{1,0:T(8,128)(2,1)} %value_w.3) | copy-start | bytes 3145732
  117.9 72.7 %all-to-all-start.1 = ((bf16[128,160,128]{2,1,0:T(8,128)(2,1)}), bf16[128,160,128]{2,1,0:T(8,128)(2,1)}, u32[]{:S(2)}, u32[]{:S(2)}) async-start(bf16[128,160,128]{2,1,0:T(8,128)(2,1)} %bitcast.53), calls=%async_computation.1 | async-start | bytes 10485760 | tf_op jit(solution)/shard_map/all_to_all | solution.py:615
  126.3 17.9 %copy-start.2 = (bf16[128,4096]{1,0:T(8,128)(2,1)S(1)}, bf16[128,4096]{1,0:T(8,128)(2,1)}, u32[]{:S(2)}) copy-start(bf16[128,4096]{1,0:T(8,128)(2,1)} %param.15) | copy-start | bytes 3145732
  126.3 18.2 %copy-start.7 = (f32[4096]{0:T(1024)S(1)}, f32[4096]{0:T(1024)}, u32[]{:S(2)}) copy-start(f32[4096]{0:T(1024)} %param.22) | copy-start | bytes 49156
  140.8 2.4 collective-permute-start
  144.5 244.0 %copy-start = (f32[64,4096]{1,0:T(8,128)}, f32[64,4096]{1,0:T(8,128)S(1)}, u32[]{:S(2)}) copy-start(f32[64,4096]{1,0:T(8,128)S(1)} %get-tuple-element.50.base_ref) | copy-start | bytes 3145732
  190.5 71.6 %all-to-all-start = ((bf16[128,160,128]{2,1,0:T(8,128)(2,1)}), bf16[128,160,128]{2,1,0:T(8,128)(2,1)}, u32[]{:S(2)}, u32[]{:S(2)}) async-start(bf16[128,160,128]{2,1,0:T(8,128)(2,1)} %bitcast.54), calls=%async_computation | async-start | bytes 10485760 | tf_op jit(solution)/shard_map/all_to_all | solution.py:615
  290.5 74.3 %all-to-all-start.3 = ((bf16[128,168,128]{2,1,0:T(8,128)(2,1)}), bf16[128,168,128]{2,1,0:T(8,128)(2,1)}, u32[]{:S(2)}, u32[]{:S(2)}) async-start(bf16[128,168,128]{2,1,0:T(8,128)(2,1)} %bitcast.55), calls=%async_computation.3 | async-start | bytes 11010048 | tf_op jit(solution)/shard_map/all_to_all | solution.py:615
  364.8 71.4 %all-to-all-start.2 = ((bf16[128,160,128]{2,1,0:T(8,128)(2,1)}), bf16[128,160,128]{2,1,0:T(8,128)(2,1)}, u32[]{:S(2)}, u32[]{:S(2)}) async-start(bf16[128,160,128]{2,1,0:T(8,128)(2,1)} %bitcast.52), calls=%async_computation.2 | async-start | bytes 10485760 | tf_op jit(solution)/shard_map/all_to_all | solution.py:615
  390.3 1.0 copy-start.6
  391.4 2.8 collective-permute-start.1
  404.4 7.6 %copy-start.8 = (f32[4096]{0:T(1024)S(1)}, f32[4096]{0:T(1024)}, u32[]{:S(2)}) copy-start(f32[4096]{0:T(1024)} %param.21) | copy-start | bytes 49156
  411.6 7.7 %collective-permute-start.2 = (bf16[128,2048]{1,0:T(8,128)(2,1)}, bf16[128,2048]{1,0:T(8,128)(2,1)}, u32[]{:S(2)}, u32[]{:S(2)}) collective-permute-start(bf16[128,2048]{1,0:T(8,128)(2,1)} %project_back.3), channel_id=1, source_target_pairs={{0,1},{1,0},{2,3},{3,2},{4,5},{5,4},{6,7},{7,6},{8,9},{9,8},{10,11... | collective-permute-start | bytes 1572872 | tf_op jit(solution)/shard_map/ppermute | solution.py:610
  419.3 25.6 %copy-start.3 = (f32[128,2048]{1,0:T(8,128)S(1)}, f32[128,2048]{1,0:T(8,128)}, u32[]{:S(2)}) copy-start(f32[128,2048]{1,0:T(8,128)} %project_back.2) | copy-start | bytes 3145732
  421.1 23.2 %collective-permute-start.3 = (f32[2,128]{1,0:T(2,128)S(1)}, f32[2,128]{1,0:T(2,128)S(1)}, u32[]{:S(2)}, u32[]{:S(2)}) collective-permute-start(f32[2,128]{1,0:T(2,128)S(1)} %pad_maximum_fusion.4), channel_id=1, source_target_pairs={{0,1},{1,0},{2,3},{3,2},{4,5},{5,4},{6,7},{7,6},{8,9},{9,8},{10,11... | collective-permute-start | bytes 3080 | tf_op jit(solution)/shard_map/ppermute | solution.py:610
Sparse Core Ops, SparseCore 0:
  10.9 106.9 all-gather.1

commit v4 on v3

--- a/solution.py
+++ b/solution.py
@@ -94,33 +94,42 @@
 
 
 def mix_block(id_ref, slot_ref, gate_ref, rows_ref, total):
-    tokens = total.shape[0]
+    parts, tokens = total.shape[:2]
     top = id_ref.shape[0] // tokens
+    per = rows_ref.shape[1] // parts
 
     def one(i, carry):
-        at = i * top
-        row = gate_ref[at] * rows_ref[id_ref[at], slot_ref[at]].astype(jnp.float32)
-        for k in range(1, top):
-            own = rows_ref[id_ref[at + k], slot_ref[at + k]].astype(jnp.float32)
-            row = row + gate_ref[at + k] * own
-        total[i] = row
+        sums = [None] * parts
+        for k in range(top):
+            at = i * top + k
+            block, place, gate = id_ref[at], slot_ref[at], gate_ref[at]
+            for p in range(parts):
+                own = gate * rows_ref[block, place + p * per].astype(jnp.float32)
+                sums[p] = own if k == 0 else sums[p] + own
+        for p in range(parts):
+            total[p, i] = sums[p]
         return carry
 
-    lax.fori_loop(0, tokens, one, 0, unroll=4)
+    lax.fori_loop(0, tokens, one, 0, unroll=2)
 
 
 def mix_out_kernel(id_ref, slot_ref, gate_ref, rows_ref, base_ref, after_ref, out_ref, total):
     del after_ref
     mix_block(id_ref, slot_ref, gate_ref, rows_ref, total)
-    mixed = base_ref[...] + total[...].reshape(out_ref.shape)
-    out_ref[...] = mixed.astype(out_ref.dtype)
+    parts, tokens, sub, lanes = total.shape
+    for p in range(parts):
+        at = slice(p * sub * lanes, (p + 1) * sub * lanes)
+        mixed = base_ref[:, at] + total[p].reshape(tokens, sub * lanes)
+        out_ref[:, at] = mixed.astype(out_ref.dtype)
 
 
 def mix_grad_kernel(id_ref, slot_ref, gate_ref, rows_ref, extra_ref, after_ref, out_ref, sum_ref, total):
     del after_ref
     mix_block(id_ref, slot_ref, gate_ref, rows_ref, total)
-    out_ref[...] = total[...].reshape(out_ref.shape)
-    tokens = total.shape[0]
+    parts, tokens, sub, lanes = total.shape
+    for p in range(parts):
+        at = slice(p * sub * lanes, (p + 1) * sub * lanes)
+        out_ref[:, at] = total[p].reshape(tokens, sub * lanes)
     top = id_ref.shape[0] // tokens
 
     @pl.when(pl.program_id(0) == 0)
@@ -143,13 +152,14 @@
     blocks, _, sub, lanes = back4.shape
     top_tokens = ids.shape[0]
     tokens = after.shape[0]
-    part = sub * lanes
-    steps = SUB // sub
-    rows_spec = pl.BlockSpec((blocks, capacity, sub, lanes), lambda k, *_: (0, k, 0, 0))
+    steps = 2
+    parts = SUB // sub // steps
+    part = parts * sub * lanes
+    rows_spec = pl.BlockSpec((blocks, parts * capacity, sub, lanes), lambda k, *_: (0, k, 0, 0))
     wide = pl.BlockSpec((tokens, part), lambda k, *_: (0, k))
     flat = pl.BlockSpec((tokens, lanes), lambda k, *_: (0, 0))
     if base is None:
-        extra = pl.BlockSpec((blocks, 1, sub, lanes), lambda k, *_: (0, steps * capacity, 0, 0))
+        extra = pl.BlockSpec((blocks, 1, sub, lanes), lambda k, *_: (0, steps * parts * capacity, 0, 0))
         kernel, specs, operands = mix_grad_kernel, [rows_spec, extra, flat], (back4, back4, after)
         out_shape = (
             jax.ShapeDtypeStruct((tokens, steps * part), jnp.float32),
@@ -168,7 +178,7 @@
             grid=(steps,),
             in_specs=specs,
             out_specs=out_specs,
-            scratch_shapes=[pltpu.VMEM((tokens, sub, lanes), jnp.float32)],
+            scratch_shapes=[pltpu.VMEM((parts, tokens, sub, lanes), jnp.float32)],
         ),
         cost_estimate=pl.CostEstimate(
             flops=top_tokens * steps * part * 2,
@@ -459,6 +469,7 @@
     hidden_ref,
     rows_v,
     made_v,
+    extra_v,
     slot_v,
     gate_w,
     up_w,
@@ -472,54 +483,54 @@
     sem_up,
     sem_cot,
     sem_out,
+    sem_extra,
     *,
     chunks,
     row_block,
 ):
-    count, sub, lanes = rows_v.shape
-    width = sub * lanes
-    piece, part = sub // chunks, width // chunks
-
-    def arrive(k):
-        at = pl.ds(k * piece, piece)
-        return pltpu.make_async_copy(rows_hbm.at[:, at, :], rows_v.at[:, at, :], sem_in.at[k])
-
-    blocks, places = made_v.shape[:2]
-    per = count // blocks
+    count, piece, lanes = rows_v.shape[1:]
+    part = piece * lanes
+
+    def arrive(k, place):
+        at = pl.ds(place * piece, piece)
+        return pltpu.make_async_copy(rows_hbm.at[:, at, :], rows_v.at[k], sem_in.at[k])
+
+    blocks, per = made_v.shape[1:3]
 
     def leave(k):
-        at = pl.ds(k * per, per if k < chunks else places - chunks * per)
-        return pltpu.make_async_copy(made_v.at[:, at], grad_hbm.at[:, at], sem_out.at[k])
+        at = pl.ds(k * per, per)
+        return pltpu.make_async_copy(made_v.at[k], grad_hbm.at[:, at], sem_out.at[k])
+
+    leave_extra = pltpu.make_async_copy(extra_v, grad_hbm.at[:, chunks * per], sem_extra)
 
     def gate_in(k):
-        at = pl.ds(k * part, part)
+        at = pl.ds(pl.multiple_of(k * part, part), part)
         return pltpu.make_async_copy(gate_hbm.at[at, :], gate_w.at[at, :], sem_gate.at[k])
 
     def up_in(k):
-        at = pl.ds(k * part, part)
+        at = pl.ds(pl.multiple_of(k * part, part), part)
         return pltpu.make_async_copy(up_hbm.at[at, :], up_w.at[at, :], sem_up.at[k])
 
     cot_in = pltpu.make_async_copy(cot_hbm, cot_ref, sem_cot)
     for k in range(chunks):
-        arrive(k).start()
+        arrive(k, k).start()
         gate_in(k).start()
         up_in(k).start()
     cot_in.start()
-    for k in range(chunks):
-        arrive(k).wait()
+    pre_gate[...] = jnp.zeros_like(pre_gate)
+    pre_up[...] = jnp.zeros_like(pre_up)
+
+    def ahead(k, carry):
+        arrive(k, 0).wait()
         gate_in(k).wait()
         up_in(k).wait()
-        rows = rows_v[:, k * piece : (k + 1) * piece, :].reshape(count, part)
-        at = slice(k * part, (k + 1) * part)
-        gate = jnp.dot(rows, gate_w[at, :], preferred_element_type=jnp.float32)
-        up = jnp.dot(rows, up_w[at, :], preferred_element_type=jnp.float32)
-        if k == 0:
-            pre_gate[...] = gate
-            pre_up[...] = up
-        else:
-            pre_gate[...] += gate
-            pre_up[...] += up
-
+        rows = rows_v[k].reshape(count, part)
+        at = pl.ds(pl.multiple_of(k * part, part), part)
+        pre_gate[...] += jnp.dot(rows, gate_w[at, :], preferred_element_type=jnp.float32)
+        pre_up[...] += jnp.dot(rows, up_w[at, :], preferred_element_type=jnp.float32)
+        return carry
+
+    lax.fori_loop(0, chunks, ahead, 0)
     cot_in.wait()
 
     def between(r, carry):
@@ -538,15 +549,19 @@
         return carry
 
     lax.fori_loop(0, count // row_block, between, 0)
-    for k in range(chunks):
-        at = slice(k * part, (k + 1) * part)
+
+    def behind(k, carry):
+        at = pl.ds(pl.multiple_of(k * part, part), part)
         grad = lax.dot_general(grad_gate[...], gate_w[at, :], NT, preferred_element_type=jnp.float32)
         grad += lax.dot_general(grad_up[...], up_w[at, :], NT, preferred_element_type=jnp.float32)
         grad += slot_v[:, :1] * router_ref[:, at]
-        made_v[:, k * per : (k + 1) * per] = grad.astype(jnp.bfloat16).reshape(
+        made_v[k] = grad.astype(jnp.bfloat16).reshape(
             blocks, per, piece, lanes
         )
         leave(k).start()
+        return carry
+
+    lax.fori_loop(0, chunks, behind, 0)
     slot = slot_v[...]
     upper = slot.astype(jnp.bfloat16)
     lower = (slot - upper.astype(jnp.float32)).astype(jnp.bfloat16)
@@ -560,10 +575,11 @@
         block, place = lax.shift_right_logical(line, 3) + b, line & 7
         select = jnp.where((block * per + place == column) & (place < per), 1.0, 0.0)
         extra = jnp.dot(select.astype(jnp.bfloat16), value, preferred_element_type=jnp.float32)
-        made_v[b : b + group, chunks * per] = extra.astype(jnp.bfloat16).reshape(group, 8, lanes)
-    leave(chunks).start()
-    for k in range(chunks + 1):
+        extra_v[b : b + group] = extra.astype(jnp.bfloat16).reshape(group, 8, lanes)
+    leave_extra.start()
+    for k in range(chunks):
         leave(k).wait()
+    leave_extra.wait()
 
 
 def expert(rows3, gate_w, up_w, cot_hidden, router_row, blocks, chunks=4, row_block=80):
@@ -580,8 +596,9 @@
         in_specs=[hbm, hbm, hbm, hbm, VM],
         out_specs=(hbm, VM),
         scratch_shapes=[
-            pltpu.VMEM(rows3.shape, jnp.bfloat16),
-            pltpu.VMEM(made, jnp.bfloat16),
+            pltpu.VMEM((chunks, count, sub // chunks, lanes), jnp.bfloat16),
+            pltpu.VMEM((chunks, blocks, count // blocks, *made[2:]), jnp.bfloat16),
+            pltpu.VMEM((blocks, *made[2:]), jnp.bfloat16),
             pltpu.VMEM((count, lanes), jnp.float32),
             pltpu.VMEM(gate_w.shape, jnp.bfloat16),
             pltpu.VMEM(up_w.shape, jnp.bfloat16),
@@ -594,7 +611,8 @@
             pltpu.SemaphoreType.DMA((chunks,)),
             pltpu.SemaphoreType.DMA((chunks,)),
             pltpu.SemaphoreType.DMA,
-            pltpu.SemaphoreType.DMA((chunks + 1,)),
+            pltpu.SemaphoreType.DMA((chunks,)),
+            pltpu.SemaphoreType.DMA,
         ],
         compiler_params=pltpu.CompilerParams(vmem_limit_bytes=VMEM_LIMIT),
         cost_estimate=pl.CostEstimate(

time: 462 us -> 454 us (0.983); the launches traced: 455 us -> 453 us
  transfers between devices with their start and end apart: 9 -> 9, of which waited for: 7 -> 7; matrix products, arithmetic and copies ran while one was open for 12% -> 12% of each run, Pallas kernels for 18% -> 17%
where the time goes in v4:
time: 454 us; the launch traced here: 453 us
  waiting for transfers between devices  240 us (53%)
  Pallas kernels  106 us (23%)
  starting transfers between devices  32.9 us (7%)
  matrix products  26.7 us (6%)
  other arithmetic  24.3 us (5%)
  between operations  14.4 us (3%)
  local copies, waits for them, and re-layouts  8.48 us (2%)
    all_to_all x4, waiting for transfers between devices, exchange(): lax.all_to_all(packed, ('req', 'head'), split_axis=0, concat_axis=0, tile...  149 us
    all_gather x1, waiting for transfers between devices, device_step(): query_w = lax.all_gather(q_proj, 'req', axis=0, tiled=True)  87.6 us
    all_to_all x4, starting transfers between devices, exchange(): lax.all_to_all(packed, ('req', 'head'), split_axis=0, concat_axis=0, tile...  29.8 us
    pallas_call x1, Pallas kernels, expert(): pl.pallas_call(functools.partial(expert_kernel, chunks=chunks, row_block=...  28.8 us
    pallas_call x2, Pallas kernels, project_back(): pl.pallas_call(project_kernel, out_shape=jax.ShapeDtypeStruct((tokens, wi...  14.5 us
    pallas_call x2, Pallas kernels, mix_rows(): pl.pallas_call(kernel, out_shape=out_shape, grid_spec=pltpu.PrefetchScala...  13.6 us
    pallas_call x1, Pallas kernels, attend(): pl.pallas_call(attend_kernel, out_shape=(jax.ShapeDtypeStruct((tokens, co...  13.5 us
    pallas_call x2, Pallas kernels, pick_rows(): pl.pallas_call(pick_kernel, out_shape=jax.ShapeDtypeStruct((count, SUB, l...  12.5 us
  transfers between devices with their start and end apart: 9, of which 7 were waited for; matrix products, arithmetic and copies ran while one was open for 12% of the time, Pallas kernels for 17%

profile of v4, /device:TPU:1, one launch (start us, length us, event | category | flops | bytes accessed | tf_op | source)
XLA Modules:
  0.0 452.5 jit_solution(5651094540845068599)
XLA Ops:
  13.4 1.5 fusion.3
  14.9 1.6 fusion.5.normed_ref
  16.6 2.2 multiply_reduce_fusion.2
  18.9 6.2 %pick_rows.2 = bf16[640,32,128]{2,1,0:T(8,128)(2,1)} custom-call(s32[640]{0:T(1024)} %reshape.160.index_ref, bf16[64,4096]{1,0:T(8,128)(2,1)} %rows_ref.1), custom_call_target="tpu_custom_call" | custom-call | bytes 5242880 | tf_op jit(solution)/shard_map/pick_rows/pallas_call | solution.py:79
  30.2 87.6 %all-gather.2.cloned.1.call-done.query_w_ref.query_w = bf16[4096,2048]{1,0:T(8,128)(2,1)} async-done(((bf16[64,2048]{1,0:T(8,128)(2,1)}), bf16[4096,2048]{1,0:T(8,128)(2,1)}) %all-gather.2.cloned.1.call-update) | async-done | bytes 16777232 | tf_op jit(solution)/shard_map/all_gather | solution.py:663
  117.9 8.4 %all-to-all-start.1 = ((bf16[128,160,128]{2,1,0:T(8,128)(2,1)}), bf16[128,160,128]{2,1,0:T(8,128)(2,1)}, u32[]{:S(2)}, u32[]{:S(2)}) async-start(bf16[128,160,128]{2,1,0:T(8,128)(2,1)} %bitcast.53), calls=%async_computation.1 | async-start | bytes 10485760 | tf_op jit(solution)/shard_map/all_to_all | solution.py:633
  126.3 13.5 %attend.1 = (bf16[128,2048]{1,0:T(8,128)(2,1)}, f32[128,2048]{1,0:T(8,128)}, f32[128,2048]{1,0:T(8,128)}) custom-call(bf16[128,4096]{1,0:T(8,128)(2,1)} %copy-done.1, bf16[4096,2048]{1,0:T(8,128)(2,1)} %all-gather.2.cloned.1.call-done.query_w_ref.query_w, bf16[128,128]{1,0:T(8,128)(2,1)} %pad_maximum_fusion.3.key_ref, ...), custom_call_target="tpu_custom_call" | custom-call | flops 2147483648 | bytes 16777216 | tf_op jit(solution)/shard_map/attend/pallas_call | solution.py:301
  145.7 6.3 %pick_rows.3 = bf16[640,32,128]{2,1,0:T(8,128)(2,1)} custom-call(s32[640]{0:T(1024)} %reshape.160.index_ref, bf16[64,4096]{1,0:T(8,128)(2,1)} %multiply_convert_fusion.rows_ref), custom_call_target="tpu_custom_call" | custom-call | bytes 5242880 | tf_op jit(solution)/shard_map/pick_rows/pallas_call | solution.py:79
  151.9 38.6 %all-to-all-done.1 = bf16[128,160,128]{2,1,0:T(8,128)(2,1)} async-done(((bf16[128,160,128]{2,1,0:T(8,128)(2,1)}), bf16[128,160,128]{2,1,0:T(8,128)(2,1)}, u32[]{:S(2)}, u32[]{:S(2)}) %all-to-all-start.1) | async-done | bytes 5242912 | tf_op jit(solution)/shard_map/all_to_all | solution.py:633
  190.5 6.8 %all-to-all-start = ((bf16[128,160,128]{2,1,0:T(8,128)(2,1)}), bf16[128,160,128]{2,1,0:T(8,128)(2,1)}, u32[]{:S(2)}, u32[]{:S(2)}) async-start(bf16[128,160,128]{2,1,0:T(8,128)(2,1)} %bitcast.54), calls=%async_computation | async-start | bytes 10485760 | tf_op jit(solution)/shard_map/all_to_all | solution.py:633
  197.4 7.3 %spread_rows.1 = bf16[640,4096]{1,0:T(8,128)(2,1)} custom-call(bf16[640,32,128]{2,1,0:T(8,128)(2,1)} %bitcast.10.rows_ref), custom_call_target="tpu_custom_call" | custom-call | bytes 10485760 | tf_op jit(solution)/shard_map/spread_rows/pallas_call | solution.py:198
  204.7 10.0 %fusion.1.cot_hbm = f32[640,768]{1,0:T(8,128)} fusion(bf16[640,4096]{1,0:T(8,128)(2,1)} %spread_rows.1, bf16[1,768,4096]{2,1,0:T(8,128)(2,1)} %param.28), kind=kOutput, calls=%fused_computation.2 | convolution fusion | flops 4026531840 | bytes 13500416 | tf_op jit(solution)/shard_map/dot_general | solution.py:736
  214.6 47.0 %all-to-all-done = bf16[128,160,128]{2,1,0:T(8,128)(2,1)} async-done(((bf16[128,160,128]{2,1,0:T(8,128)(2,1)}), bf16[128,160,128]{2,1,0:T(8,128)(2,1)}, u32[]{:S(2)}, u32[]{:S(2)}) %all-to-all-start) | async-done | bytes 5242912 | tf_op jit(solution)/shard_map/all_to_all | solution.py:633
  261.6 28.8 %expert.1 = (bf16[128,21,8,128]{3,2,1,0:T(8,128)(2,1)}, bf16[640,768]{1,0:T(8,128)(2,1)}) custom-call(bf16[640,32,128]{2,1,0:T(8,128)(2,1)} %bitcast.6.rows_hbm, bf16[4096,768]{1,0:T(8,128)(2,1)} %bitcast.64, bf16[4096,768]{1,0:T(8,128)(2,1)} %bitcast.65, f32[640,768]{1,0:T(8,128)} %fusion.1.cot_hbm, f32[1,4096]{1,0:T(1,128)} %bitcast.56), custom_call_target="tpu_custom_call" | custom-call | flops 16106127360 | bytes 10485760 | tf_op jit(solution)/shard_map/expert/pallas_call | solution.py:590
  290.4 6.8 %all-to-all-start.3 = ((bf16[128,168,128]{2,1,0:T(8,128)(2,1)}), bf16[128,168,128]{2,1,0:T(8,128)(2,1)}, u32[]{:S(2)}, u32[]{:S(2)}) async-start(bf16[128,168,128]{2,1,0:T(8,128)(2,1)} %bitcast.55), calls=%async_computation.3 | async-start | bytes 11010048 | tf_op jit(solution)/shard_map/all_to_all | solution.py:633
  297.3 1.4 fusion.28
  298.6 9.7 %convolution_convert_fusion.rows_ref = bf16[640,4096]{1,0:T(8,128)(2,1)} fusion(bf16[640,768]{1,0:T(8,128)(2,1)} %get-tuple-element.37, bf16[1,768,4096]{2,1,0:T(8,128)(2,1)} %param.28), kind=kOutput, calls=%fused_computation | convolution fusion | flops 4029153280 | bytes 12517376 | tf_op jit(solution)/shard_map/dot_general | solution.py:740
  308.3 8.0 %fold_rows.1 = bf16[128,20,8,128]{3,2,1,0:T(8,128)(2,1)} custom-call(bf16[640,4096]{1,0:T(8,128)(2,1)} %convolution_convert_fusion.rows_ref), custom_call_target="tpu_custom_call" | custom-call | bytes 10485760 | tf_op jit(solution)/shard_map/fold_rows/pallas_call | solution.py:225
  316.3 48.1 %all-to-all-done.3 = bf16[128,168,128]{2,1,0:T(8,128)(2,1)} async-done(((bf16[128,168,128]{2,1,0:T(8,128)(2,1)}), bf16[128,168,128]{2,1,0:T(8,128)(2,1)}, u32[]{:S(2)}, u32[]{:S(2)}) %all-to-all-start.3) | async-done | bytes 5505056 | tf_op jit(solution)/shard_map/all_to_all | solution.py:633
  364.3 7.8 %all-to-all-start.2 = ((bf16[128,160,128]{2,1,0:T(8,128)(2,1)}), bf16[128,160,128]{2,1,0:T(8,128)(2,1)}, u32[]{:S(2)}, u32[]{:S(2)}) async-start(bf16[128,160,128]{2,1,0:T(8,128)(2,1)} %bitcast.52), calls=%async_computation.2 | async-start | bytes 10485760 | tf_op jit(solution)/shard_map/all_to_all | solution.py:633
  373.6 2.4 fusion.29
  376.7 7.4 %mix_rows.2 = (f32[64,4096]{1,0:T(8,128)}, f32[64,128]{1,0:T(8,128)}) custom-call(s32[512]{0:T(512)} %reshape.163.id_ref, s32[512]{0:T(512)} %reshape.164.slot_ref, f32[512]{0:T(512)} %div.50.gate_ref, bf16[128,21,8,128]{3,2,1,0:T(8,128)(2,1)} %bitcast.16.rows_ref.extra_ref, bf16[128,21,8,128]{3,2,1,0:T(8,128)(2,1)} %bitcast.16.rows_ref.extra_ref, ...), custom_call_target="tpu_custom_call" | custom-call | flops 4194304 | bytes 5242880 | tf_op jit(solution)/shard_map/mix_rows/pallas_call | solution.py:173
  385.0 1.6 multiply_reduce_fusion
  386.6 1.8 subtract_add_fusion
  394.4 8.1 %attend_back.1 = (bf16[128,2048]{1,0:T(8,128)(2,1)}, bf16[128,128]{1,0:T(8,128)(2,1)}, bf16[128,128]{1,0:T(8,128)(2,1)}) custom-call(bf16[128,2048]{1,0:T(8,128)(2,1)} %fusion.11.grad_ref, f32[128,2048]{1,0:T(8,128)} %get-tuple-element.41.weight_ref, f32[128,2048]{1,0:T(8,128)} %get-tuple-element.42.raw_ref, bf16[128,128]{1,0:T(8,128)(2,1)} %pad_maximum_fusion.3.key_ref, ...), custom_call_target="tpu_custom_call" | custom-call | flops 402653184 | bytes 3145728 | tf_op jit(solution)/shard_map/attend_back/pallas_call | solution.py:403
  402.5 7.2 %project_back.3 = bf16[128,2048]{1,0:T(8,128)(2,1)} custom-call(s32[1]{0:T(128)} %bitcast.18.at_ref, bf16[128,2048]{1,0:T(8,128)(2,1)} %get-tuple-element.44.query_ref, bf16[128,128]{1,0:T(8,128)(2,1)} %get-tuple-element.45.key_ref, bf16[128,128]{1,0:T(8,128)(2,1)} %get-tuple-element.46.value_ref, ...), custom_call_target="tpu_custom_call" | custom-call | flops 1073741824 | bytes 8388608 | tf_op jit(solution)/shard_map/project_back/pallas_call | solution.py:437
  410.1 7.3 %project_back.2 = f32[128,2048]{1,0:T(8,128)} custom-call(s32[1]{0:T(128)} %bitcast.14.at_ref, bf16[128,2048]{1,0:T(8,128)(2,1)} %get-tuple-element.44.query_ref, bf16[128,128]{1,0:T(8,128)(2,1)} %get-tuple-element.45.key_ref, bf16[128,128]{1,0:T(8,128)(2,1)} %get-tuple-element.46.value_ref, ...), custom_call_target="tpu_custom_call" | custom-call | flops 1073741824 | bytes 8388608 | tf_op jit(solution)/shard_map/project_back/pallas_call | solution.py:437
  417.4 1.8 fusion.9
  419.4 1.4 slice.37.after_ref
  420.8 15.6 %all-to-all-done.2 = bf16[128,160,128]{2,1,0:T(8,128)(2,1)} async-done(((bf16[128,160,128]{2,1,0:T(8,128)(2,1)}), bf16[128,160,128]{2,1,0:T(8,128)(2,1)}, u32[]{:S(2)}, u32[]{:S(2)}) %all-to-all-start.2) | async-done | bytes 5242912 | tf_op jit(solution)/shard_map/all_to_all | solution.py:633
  436.3 6.2 %mix_rows.3 = bf16[64,4096]{1,0:T(8,128)(2,1)} custom-call(s32[512]{0:T(512)} %reshape.163.id_ref, s32[512]{0:T(512)} %reshape.164.slot_ref, f32[512]{0:T(512)} %div.50.gate_ref, bf16[128,20,8,128]{3,2,1,0:T(8,128)(2,1)} %bitcast.13.rows_ref, f32[64,4096]{1,0:T(8,128)} %copy-done, f32[64,128]{1,0:T(8,128)} %slice.37.after_ref), custom_call_target="tpu_custom_call" | custom-call | flops 4194304 | bytes 5242880 | tf_op jit(solution)/shard_map/mix_rows/pallas_call | solution.py:173
  443.1 2.6 convert_multiply_fusion.2
  (79 shorter events, 27.4 us)
Async XLA Ops:
  7.2 110.7 %all-gather.2.cloned.1.call-start = ((), (), s32[]{:S(2)}) async-start(), calls=%async_computation.4 | async-start | bytes 17039360 | tf_op jit(solution)/shard_map/all_gather | solution.py:663
  14.9 10.2 %copy-start.5 = (bf16[4096,128]{1,0:T(8,128)(2,1)S(1)}, bf16[4096,128]{1,0:T(8,128)(2,1)}, u32[]{:S(2)}) copy-start(bf16[4096,128]{1,0:T(8,128)(2,1)} %param.23) | copy-start | bytes 3145732
  14.9 11.6 %copy-start.10 = (s32[1,4]{1,0:T(1,128)S(1)}, s32[1,4]{1,0:T(1,128)}, u32[]{:S(2)}) copy-start(s32[1,4]{1,0:T(1,128)} %param.25) | copy-start | bytes 52
  14.9 11.7 %copy-start.9 = (f32[128]{0:T(128)S(1)}, f32[128]{0:T(128)}, u32[]{:S(2)}) copy-start(f32[128]{0:T(128)} %param.20) | copy-start | bytes 1540
  16.6 13.7 %copy-start.1 = (bf16[128,4096]{1,0:T(8,128)(2,1)}, bf16[128,4096]{1,0:T(8,128)(2,1)S(1)}, u32[]{:S(2)}) copy-start(bf16[128,4096]{1,0:T(8,128)(2,1)S(1)} %fusion.5.normed_ref) | copy-start | bytes 3145732
  16.6 12.6 %copy-start.4 = (bf16[4096,128]{1,0:T(8,128)(2,1)S(1)}, bf16[4096,128]{1,0:T(8,128)(2,1)}, u32[]{:S(2)}) copy-start(bf16[4096,128]{1,0:T(8,128)(2,1)} %value_w.3) | copy-start | bytes 3145732
  117.9 72.7 %all-to-all-start.1 = ((bf16[128,160,128]{2,1,0:T(8,128)(2,1)}), bf16[128,160,128]{2,1,0:T(8,128)(2,1)}, u32[]{:S(2)}, u32[]{:S(2)}) async-start(bf16[128,160,128]{2,1,0:T(8,128)(2,1)} %bitcast.53), calls=%async_computation.1 | async-start | bytes 10485760 | tf_op jit(solution)/shard_map/all_to_all | solution.py:633
  126.3 17.9 %copy-start.2 = (bf16[128,4096]{1,0:T(8,128)(2,1)S(1)}, bf16[128,4096]{1,0:T(8,128)(2,1)}, u32[]{:S(2)}) copy-start(bf16[128,4096]{1,0:T(8,128)(2,1)} %param.15) | copy-start | bytes 3145732
  126.3 18.2 %copy-start.7 = (f32[4096]{0:T(1024)S(1)}, f32[4096]{0:T(1024)}, u32[]{:S(2)}) copy-start(f32[4096]{0:T(1024)} %param.22) | copy-start | bytes 49156
  140.8 2.4 collective-permute-start
  144.5 242.1 %copy-start = (f32[64,4096]{1,0:T(8,128)}, f32[64,4096]{1,0:T(8,128)S(1)}, u32[]{:S(2)}) copy-start(f32[64,4096]{1,0:T(8,128)S(1)} %get-tuple-element.50.base_ref) | copy-start | bytes 3145732
  190.5 71.1 %all-to-all-start = ((bf16[128,160,128]{2,1,0:T(8,128)(2,1)}), bf16[128,160,128]{2,1,0:T(8,128)(2,1)}, u32[]{:S(2)}, u32[]{:S(2)}) async-start(bf16[128,160,128]{2,1,0:T(8,128)(2,1)} %bitcast.54), calls=%async_computation | async-start | bytes 10485760 | tf_op jit(solution)/shard_map/all_to_all | solution.py:633
  290.4 73.9 %all-to-all-start.3 = ((bf16[128,168,128]{2,1,0:T(8,128)(2,1)}), bf16[128,168,128]{2,1,0:T(8,128)(2,1)}, u32[]{:S(2)}, u32[]{:S(2)}) async-start(bf16[128,168,128]{2,1,0:T(8,128)(2,1)} %bitcast.55), calls=%async_computation.3 | async-start | bytes 11010048 | tf_op jit(solution)/shard_map/all_to_all | solution.py:633
  364.3 72.0 %all-to-all-start.2 = ((bf16[128,160,128]{2,1,0:T(8,128)(2,1)}), bf16[128,160,128]{2,1,0:T(8,128)(2,1)}, u32[]{:S(2)}, u32[]{:S(2)}) async-start(bf16[128,160,128]{2,1,0:T(8,128)(2,1)} %bitcast.52), calls=%async_computation.2 | async-start | bytes 10485760 | tf_op jit(solution)/shard_map/all_to_all | solution.py:633
  388.4 1.0 copy-start.6
  389.5 2.8 collective-permute-start.1
  402.5 7.6 %copy-start.8 = (f32[4096]{0:T(1024)S(1)}, f32[4096]{0:T(1024)}, u32[]{:S(2)}) copy-start(f32[4096]{0:T(1024)} %param.21) | copy-start | bytes 49156
  409.7 7.7 %collective-permute-start.2 = (bf16[128,2048]{1,0:T(8,128)(2,1)}, bf16[128,2048]{1,0:T(8,128)(2,1)}, u32[]{:S(2)}, u32[]{:S(2)}) collective-permute-start(bf16[128,2048]{1,0:T(8,128)(2,1)} %project_back.3), channel_id=1, source_target_pairs={{0,1},{1,0},{2,3},{3,2},{4,5},{5,4},{6,7},{7,6},{8,9},{9,8},{10,11... | collective-permute-start | bytes 1572872 | tf_op jit(solution)/shard_map/ppermute | solution.py:628
  417.4 25.7 %copy-start.3 = (f32[128,2048]{1,0:T(8,128)S(1)}, f32[128,2048]{1,0:T(8,128)}, u32[]{:S(2)}) copy-start(f32[128,2048]{1,0:T(8,128)} %project_back.2) | copy-start | bytes 3145732
  419.2 23.3 %collective-permute-start.3 = (f32[2,128]{1,0:T(2,128)S(1)}, f32[2,128]{1,0:T(2,128)S(1)}, u32[]{:S(2)}, u32[]{:S(2)}) collective-permute-start(f32[2,128]{1,0:T(2,128)S(1)} %pad_maximum_fusion.4), channel_id=1, source_target_pairs={{0,1},{1,0},{2,3},{3,2},{4,5},{5,4},{6,7},{7,6},{8,9},{9,8},{10,11... | collective-permute-start | bytes 3080 | tf_op jit(solution)/shard_map/ppermute | solution.py:628
Sparse Core Ops, SparseCore 0:
  10.9 106.9 all-gather.1
